TPU v7x, 32 devices: a whole 2x2x4 slice. The times are simulated.
32 devices in a mesh: dp: 2 (over y), row: 4 (over z), col: 4 (over x, core).
Axes of the slice: x: 2, y: 2, z: 4, core: 2. Of those that a mesh axis runs over, the one named last changes fastest.
Arguments:
- tokens: bfloat16 [128, 12288], P(('dp', 'row')), may hold values from -6 to 6
- cotangent: bfloat16 [128, 49152], P('dp', ('row', 'col')), may hold values from -6 to 6
- weight_blocks: bfloat16 [16, 96, 128, 128], P(('row', 'col')), may hold values from -0.125 to 0.125
- block_rows: int32 [16, 96], P(('row', 'col')), may hold values from 0 to 95, as said below
- block_cols: int32 [16, 96], P(('row', 'col')), may hold values from 0 to 23
- block_count: int32 [16], P(('row', 'col')), may hold values from 24 to 96, as said below
Outputs:
- hidden: bfloat16 [128, 49152], P('dp', ('row', 'col'))
- weight_grad: bfloat16 [16, 96, 128, 128], P(('row', 'col'), 'dp')
Inputs may be any that keep to these rules, and one draw needn't show every extreme that they name: Within each shard, the pairs (block_rows, block_cols) of the live slots are distinct. `block_count`: some shard has all 96 slots live in every draw.
All inputs are finite; a program needn't handle non-finite values.
Results may differ from a plain program's by a relative error of at most 0.009.
Values may be sent and summed in bfloat16 or wider, within the bound.
No kernel may reach another device: no remote copies, remote signals or barrier semaphores. Data moves between devices by JAX's collectives and lax.ppermute only.
A program may use at most 64 MiB of HBM per device.

v0:
```python
import math

import jax
import jax.numpy as jnp
from jax import lax
from jax.sharding import PartitionSpec as P


def broadcast(value, axis, root):
    mine = lax.axis_index(axis) == root
    return lax.psum(jnp.where(mine, value, jnp.zeros_like(value)), axis)


def on_device(tokens, cotangent, weight_blocks, block_rows, block_cols, block_count):
    steps = lax.axis_size("row")
    tok_dev, width = tokens.shape
    group, ff_dev = cotangent.shape
    capacity = weight_blocks.shape[1]
    side = weight_blocks.shape[2]
    col_blocks = ff_dev // side
    scale = 1.0 / (group * lax.axis_size("dp")) ** 0.5
    rows = block_rows[0]
    cols = block_cols[0]
    weights = weight_blocks[0]
    live = (jnp.arange(capacity) < block_count[0]).astype(jnp.float32)
    select = (cols[:, None] == jnp.arange(col_blocks)[None, :]).astype(jnp.float32) * live[:, None]

    def piece_terms(piece, start):
        count = piece.shape[0]
        blocks = piece.reshape(count, width // side, side)[:, rows, :]
        product = jnp.einsum("nkb,kbc->nkc", blocks, weights, preferred_element_type=jnp.float32)
        output = jnp.einsum("nkc,kj->njc", product, select).reshape(count, ff_dev)
        grads = lax.dynamic_slice_in_dim(cotangent, start, count, 0)
        grads = grads.reshape(count, col_blocks, side)[:, cols, :]
        wgrad = jnp.einsum("nkb,nkc->kbc", blocks, grads, preferred_element_type=jnp.float32)
        return (output, wgrad)

    def fold_piece(carry, piece, start):
        count = piece.shape[0]
        sub_rows = math.gcd(count, tok_dev)
        pieces = piece.reshape(count // sub_rows, sub_rows, width)
        offsets = start + sub_rows * jnp.arange(count // sub_rows, dtype=jnp.int32)

        def one_sub(state, item):
            output_all, wsum = state
            sub_piece, offset = item
            output, wgrad = piece_terms(sub_piece, offset)
            output_all = lax.dynamic_update_slice_in_dim(output_all, output, offset, 0)
            return ((output_all, wsum + wgrad), None)

        result, unused = lax.scan(one_sub, carry, (pieces, offsets))
        return result

    initial = (
        jnp.zeros((group, ff_dev), jnp.float32),
        jnp.zeros((capacity, side, side), jnp.float32),
    )

    def one_step(owner, carry):
        panel = broadcast(tokens, "row", owner)
        return fold_piece(carry, panel, owner * tok_dev)

    output_all, wsum = lax.fori_loop(0, steps, one_step, initial)
    hidden = output_all.astype(jnp.bfloat16)
    term = wsum * live[:, None, None] * scale
    summed = lax.psum_scatter(
        term[None].astype(jnp.bfloat16), "dp", scatter_dimension=1, tiled=True
    )
    return (hidden, summed)


def solution(mesh):
    in_specs = (
        P(("dp", "row"), None),
        P("dp", ("row", "col")),
        P(("row", "col"), None, None, None),
        P(("row", "col"), None),
        P(("row", "col"), None),
        P(("row", "col")),
    )
    out_specs = (P("dp", ("row", "col")), P(("row", "col"), "dp", None, None))
    return jax.shard_map(
        on_device, mesh=mesh, in_specs=in_specs, out_specs=out_specs, check_vma=False
    )
```

profile of v0, /device:TPU:29, one launch (start us, length us, event | category | flops | bytes accessed | tf_op | source)
XLA Modules:
  0.0 268.5 jit_solution(6580645578113476083)
XLA Ops:
  8.7 202.1 %while.29 = (s32[]{:T(128)}, bf16[64,3072]{1,0:T(8,128)(2,1)S(1)}, f32[96,128,128]{2,1,0:T(8,128)}, bf16[16,12288]{1,0:T(8,128)(2,1)}, s32[96]{0:T(128)}, /*inde...) while((s32[]{:T(128)}, bf16[64,3072]{1,0:T(8,128)(2,1)S(1)}, ...), condition=%wide.region_2.3_spmd.clone.clone.clone, body=%wide.region_0.2_spmd.clone.clone.clone.sunk | while | flops 113646664 | bytes 22918524 | solution.py:63
  10.3 0.9 copy_bitcast_fusion.5
  11.9 35.5 %all-reduce.2.cloned.1.call-done = bf16[16,96,128]{2,0,1:T(8,128)(2,1)} async-done(((bf16[16,96,128]{2,0,1:T(8,128)(2,1)}), bf16[16,96,128]{2,0,1:T(8,128)(2,1)}) %all-reduce.2.cloned.1.call-update) | async-done | bytes 393232 | tf_op jit(solution)/shard_map/while/body/eval_jaxpr/psum | solution.py:11
  47.4 1.7 gather_fusion
  49.0 2.8 %convolution_bitcast_fusion.2 = bf16[16,96,128]{2,0,1:T(8,128)(2,1)S(1)} fusion(bf16[96,128,128]{2,1,0:T(8,128)(2,1)} %get-tuple-element.408, bf16[96,16,128]{2,1,0:T(8,128)(2,1)S(1)} %gather_fusion), kind=kOutput, calls=%fused_computation.4.clone.1 | convolution fusion | flops 50331648 | bytes 3932160 | tf_op jit(solution)/shard_map/while/body/eval_jaxpr/while/body/eval_jaxpr/nkb,kbc->nkc/dot_general | solution.py:31
  52.1 3.7 %select_add_fusion.2 = f32[96,128,128]{2,1,0:T(8,128)} fusion(f32[96,128,128]{2,1,0:T(8,128)} %get-tuple-element.390, pred[]{:T(512)S(6)} %compare.5, bf16[96,16,128]{2,1,0:T(8,128)(2,1)S(1)} %gather_fusion.1, bf16[96,16,128]{2,1,0:T(8,128)(2,1)S(1)} %gather_fusion), kind=kOutput, calls=%fused_computation.3.clone.1 | convolution fusion | flops 53477376 | bytes 13369345 | tf_op jit(solution)/shard_map/while/body/eval_jaxpr/while/body/eval_jaxpr/nkb,nkc->kbc/dot_general | solution.py:35
  57.3 0.9 copy_bitcast_fusion.5
  58.9 37.4 %all-reduce.2.cloned.1.call-done = bf16[16,96,128]{2,0,1:T(8,128)(2,1)} async-done(((bf16[16,96,128]{2,0,1:T(8,128)(2,1)}), bf16[16,96,128]{2,0,1:T(8,128)(2,1)}) %all-reduce.2.cloned.1.call-update) | async-done | bytes 393232 | tf_op jit(solution)/shard_map/while/body/eval_jaxpr/psum | solution.py:11
  96.4 1.7 gather_fusion
  98.0 2.8 %convolution_bitcast_fusion.2 = bf16[16,96,128]{2,0,1:T(8,128)(2,1)S(1)} fusion(bf16[96,128,128]{2,1,0:T(8,128)(2,1)} %get-tuple-element.408, bf16[96,16,128]{2,1,0:T(8,128)(2,1)S(1)} %gather_fusion), kind=kOutput, calls=%fused_computation.4.clone.1 | convolution fusion | flops 50331648 | bytes 3932160 | tf_op jit(solution)/shard_map/while/body/eval_jaxpr/while/body/eval_jaxpr/nkb,kbc->nkc/dot_general | solution.py:31
  101.1 6.5 %select_add_fusion.2 = f32[96,128,128]{2,1,0:T(8,128)} fusion(f32[96,128,128]{2,1,0:T(8,128)} %get-tuple-element.390, pred[]{:T(512)S(6)} %compare.5, bf16[96,16,128]{2,1,0:T(8,128)(2,1)S(1)} %gather_fusion.1, bf16[96,16,128]{2,1,0:T(8,128)(2,1)S(1)} %gather_fusion), kind=kOutput, calls=%fused_computation.3.clone.1 | convolution fusion | flops 53477376 | bytes 13369345 | tf_op jit(solution)/shard_map/while/body/eval_jaxpr/while/body/eval_jaxpr/nkb,nkc->kbc/dot_general | solution.py:35
  109.1 0.9 copy_bitcast_fusion.5
  110.7 37.4 %all-reduce.2.cloned.1.call-done = bf16[16,96,128]{2,0,1:T(8,128)(2,1)} async-done(((bf16[16,96,128]{2,0,1:T(8,128)(2,1)}), bf16[16,96,128]{2,0,1:T(8,128)(2,1)}) %all-reduce.2.cloned.1.call-update) | async-done | bytes 393232 | tf_op jit(solution)/shard_map/while/body/eval_jaxpr/psum | solution.py:11
  148.2 1.7 gather_fusion
  149.8 2.8 %convolution_bitcast_fusion.2 = bf16[16,96,128]{2,0,1:T(8,128)(2,1)S(1)} fusion(bf16[96,128,128]{2,1,0:T(8,128)(2,1)} %get-tuple-element.408, bf16[96,16,128]{2,1,0:T(8,128)(2,1)S(1)} %gather_fusion), kind=kOutput, calls=%fused_computation.4.clone.1 | convolution fusion | flops 50331648 | bytes 3932160 | tf_op jit(solution)/shard_map/while/body/eval_jaxpr/while/body/eval_jaxpr/nkb,kbc->nkc/dot_general | solution.py:31
  152.9 6.5 %select_add_fusion.2 = f32[96,128,128]{2,1,0:T(8,128)} fusion(f32[96,128,128]{2,1,0:T(8,128)} %get-tuple-element.390, pred[]{:T(512)S(6)} %compare.5, bf16[96,16,128]{2,1,0:T(8,128)(2,1)S(1)} %gather_fusion.1, bf16[96,16,128]{2,1,0:T(8,128)(2,1)S(1)} %gather_fusion), kind=kOutput, calls=%fused_computation.3.clone.1 | convolution fusion | flops 53477376 | bytes 13369345 | tf_op jit(solution)/shard_map/while/body/eval_jaxpr/while/body/eval_jaxpr/nkb,nkc->kbc/dot_general | solution.py:35
  159.4 1.8 copy_bitcast_fusion.4
  161.9 0.9 copy_bitcast_fusion.5
  163.5 36.1 %all-reduce.2.cloned.1.call-done = bf16[16,96,128]{2,0,1:T(8,128)(2,1)} async-done(((bf16[16,96,128]{2,0,1:T(8,128)(2,1)}), bf16[16,96,128]{2,0,1:T(8,128)(2,1)}) %all-reduce.2.cloned.1.call-update) | async-done | bytes 393232 | tf_op jit(solution)/shard_map/while/body/eval_jaxpr/psum | solution.py:11
  199.6 1.7 gather_fusion
  201.3 2.8 %convolution_bitcast_fusion.2 = bf16[16,96,128]{2,0,1:T(8,128)(2,1)S(1)} fusion(bf16[96,128,128]{2,1,0:T(8,128)(2,1)} %get-tuple-element.408, bf16[96,16,128]{2,1,0:T(8,128)(2,1)S(1)} %gather_fusion), kind=kOutput, calls=%fused_computation.4.clone.1 | convolution fusion | flops 50331648 | bytes 3932160 | tf_op jit(solution)/shard_map/while/body/eval_jaxpr/while/body/eval_jaxpr/nkb,kbc->nkc/dot_general | solution.py:31
  204.3 6.5 %select_add_fusion.2 = f32[96,128,128]{2,1,0:T(8,128)} fusion(f32[96,128,128]{2,1,0:T(8,128)} %get-tuple-element.390, pred[]{:T(512)S(6)} %compare.5, bf16[96,16,128]{2,1,0:T(8,128)(2,1)S(1)} %gather_fusion.1, bf16[96,16,128]{2,1,0:T(8,128)(2,1)S(1)} %gather_fusion), kind=kOutput, calls=%fused_computation.3.clone.1 | convolution fusion | flops 53477376 | bytes 13369345 | tf_op jit(solution)/shard_map/while/body/eval_jaxpr/while/body/eval_jaxpr/nkb,nkc->kbc/dot_general | solution.py:35
  210.8 5.4 %fusion.15 = bf16[1,96,128,128]{3,2,1,0:T(8,128)(2,1)} fusion(f32[96,128,128]{2,1,0:T(8,128)} %get-tuple-element.208, f32[96]{0:T(128)S(1)} %get-tuple-element.311), kind=kLoop, calls=%fused_computation.29 | loop fusion | flops 4718592 | bytes 9437568 | tf_op jit(solution)/shard_map/convert_element_type | solution.py:67
  216.2 45.2 %reduce-scatter.2.cloned.1.call-done = bf16[1,48,128,128]{3,2,1,0:T(8,128)(2,1)} async-done(((bf16[1,96,128,128]{3,2,1,0:T(8,128)(2,1)}), bf16[1,48,128,128]{3,2,1,0:T(8,128)(2,1)}) %reduce-scatter.2.cloned.1.call-update) | async-done | bytes 1572880 | tf_op jit(solution)/shard_map/reduce_scatter | solution.py:66
  (50 shorter events, 9.0 us)
Async XLA Ops:
  8.7 43.1 %copy-start.1 = (s32[96]{0:T(128)S(1)}, s32[96]{0:T(128)}, u32[]{:S(2)}) copy-start(s32[96]{0:T(128)} %get-tuple-element.410) | copy-start | bytes 1156 | tf_op jit(solution)/shard_map/while
  8.7 38.7 %all-reduce.2.cloned.1.call-start = ((), (), s32[]{:S(2)}) async-start(), calls=%async_computation.2 | async-start | bytes 786432 | tf_op jit(solution)/shard_map/while/body/eval_jaxpr/psum | solution.py:11
  55.8 45.1 %copy-start.1 = (s32[96]{0:T(128)S(1)}, s32[96]{0:T(128)}, u32[]{:S(2)}) copy-start(s32[96]{0:T(128)} %get-tuple-element.410) | copy-start | bytes 1156 | tf_op jit(solution)/shard_map/while
  55.8 40.6 %all-reduce.2.cloned.1.call-start = ((), (), s32[]{:S(2)}) async-start(), calls=%async_computation.2 | async-start | bytes 786432 | tf_op jit(solution)/shard_map/while/body/eval_jaxpr/psum | solution.py:11
  107.6 45.1 %copy-start.1 = (s32[96]{0:T(128)S(1)}, s32[96]{0:T(128)}, u32[]{:S(2)}) copy-start(s32[96]{0:T(128)} %get-tuple-element.410) | copy-start | bytes 1156 | tf_op jit(solution)/shard_map/while
  107.6 40.6 %all-reduce.2.cloned.1.call-start = ((), (), s32[]{:S(2)}) async-start(), calls=%async_computation.2 | async-start | bytes 786432 | tf_op jit(solution)/shard_map/while/body/eval_jaxpr/psum | solution.py:11
  159.3 44.7 %copy-start.1 = (s32[96]{0:T(128)S(1)}, s32[96]{0:T(128)}, u32[]{:S(2)}) copy-start(s32[96]{0:T(128)} %get-tuple-element.410) | copy-start | bytes 1156 | tf_op jit(solution)/shard_map/while
  159.3 40.3 %all-reduce.2.cloned.1.call-start = ((), (), s32[]{:S(2)}) async-start(), calls=%async_computation.2 | async-start | bytes 786432 | tf_op jit(solution)/shard_map/while/body/eval_jaxpr/psum | solution.py:11
  210.8 5.4 %copy-start = (bf16[64,3072]{1,0:T(8,128)(2,1)}, bf16[64,3072]{1,0:T(8,128)(2,1)S(1)}, u32[]{:S(2)}) copy-start(bf16[64,3072]{1,0:T(8,128)(2,1)S(1)} %get-tuple-element.207) | copy-start | bytes 1179652
  210.8 50.6 %reduce-scatter.2.cloned.1.call-start = ((), (), s32[]{:S(2)}) async-start(), calls=%async_computation.1 | async-start | bytes 4718592 | tf_op jit(solution)/shard_map/reduce_scatter | solution.py:66
Sparse Core Ops, SparseCore 0:
  12.6 34.7 all-reduce.1
  59.7 36.6 all-reduce.1
  111.4 36.6 all-reduce.1
  162.9 36.6 all-reduce.1
Sparse Core Ops, SparseCore 1:
  216.3 45.1 reduce-scatter.1
where the time goes:
time: 272 us; the launch traced here: 269 us
  waiting for transfers between devices  192 us (71%)
  matrix products  35.2 us (13%)
  between operations  15.8 us (6%)
  local copies, waits for them, and re-layouts  13.1 us (5%)
  other arithmetic  12.5 us (5%)
    psum x4, waiting for transfers between devices, broadcast(): return lax.psum(jnp.where(mine, value, jnp.zeros_like(value)), axis)  146 us
    reduce_scatter x1, waiting for transfers between devices, on_device(): lax.psum_scatter(term[None].astype(jnp.bfloat16), 'dp', scatter_dimension...  45.2 us
    dot_general x4, matrix products, piece_terms(): jnp.einsum('nkb,nkc->kbc', blocks, grads, preferred_element_type=jnp.floa...  23.2 us
    dot_general x4, matrix products, piece_terms(): jnp.einsum('nkb,kbc->nkc', blocks, weights, preferred_element_type=jnp.fl...  11.2 us
    gather x4, local copies, waits for them, and re-layouts, piece_terms(): blocks = piece.reshape(count, width // side, side)[:, rows, :]  6.65 us
  transfers between devices with their start and end apart: 5, of which 5 were waited for; matrix products, arithmetic and copies ran while one was open for 3% of the time, Pallas kernels for 0%

commit v1 on v0

v1 whole, which is shorter than its diff:
```python
import functools

import jax
import jax.numpy as jnp
from jax import lax
from jax.experimental import pallas as pl
from jax.experimental.pallas import tpu as pltpu
from jax.sharding import PartitionSpec as P

ROWS_AT, COLS_AT, UNROLL = 0, 1, 8


def block_kernel(plan, slots, scale, *refs):
    n_tok, n_cot = plan["tokens"], plan["cotangents"]
    table, place = refs[0], refs[1]
    pieces = refs[2 : 2 + n_tok]
    cots = refs[2 + n_tok : 2 + n_tok + n_cot]
    w_hbm = refs[2 + n_tok + n_cot]
    hid_hbm, grad_hbm = refs[3 + n_tok + n_cot : 5 + n_tok + n_cot]
    tok, cot, w, acc, hid, grad, sem_tok, sem_cot, sem_w, sem_out = refs[5 + n_tok + n_cot :]
    capacity, side = w.shape[0], w.shape[1]
    col_blocks, group = acc.shape[0], acc.shape[1]
    parts = sem_w.shape[0]
    per_part = capacity // parts

    w_copies = [
        pltpu.make_async_copy(w_hbm.at[pl.ds(i * per_part, per_part)], w.at[pl.ds(i * per_part, per_part)], sem_w.at[i])
        for i in range(parts)
    ]
    tok_copies = []
    for i, (operand, first, rows, at) in enumerate(plan["pieces"]):
        src = pieces[operand]
        width = src.shape[1]
        row0 = pl.multiple_of(place[2 * at], 16)
        col0 = pl.multiple_of(place[2 * at + 1], side)
        tok_copies.append(
            pltpu.make_async_copy(
                src.at[pl.ds(first, rows)], tok.at[pl.ds(row0, rows), pl.ds(col0, width)], sem_tok.at[i]
            )
        )
    cot_copies = [
        pltpu.make_async_copy(c, cot.at[pl.ds(i * group, group)], sem_cot.at[i]) for i, c in enumerate(cots)
    ]
    for copy in tok_copies + w_copies + cot_copies:
        copy.start()
    acc[...] = jnp.zeros_like(acc)
    count = place[2 * plan["places"]]
    slot0 = place[2 * plan["places"] + 1]
    for copy in tok_copies:
        copy.wait()

    def hidden_step(step, carry):
        base = step * UNROLL
        products = []
        for u in range(UNROLL):
            k = base + u
            lane = pl.multiple_of(table[ROWS_AT, k] * side, side)
            product = jnp.dot(tok[pl.ds(0, group), pl.ds(lane, side)], w[k], preferred_element_type=jnp.float32)
            products.append(jnp.where(k < count, product, 0.0))
        for u in range(UNROLL):
            col = table[COLS_AT, base + u]
            acc[col] = acc[col] + products[u]
        return carry

    for i in range(parts):
        w_copies[i].wait()
        lax.fori_loop(i * per_part // UNROLL, (i + 1) * per_part // UNROLL, hidden_step, 0)
    for j in range(col_blocks):
        hid[:, j * side : (j + 1) * side] = acc[j].astype(hid.dtype)
    out_hid = pltpu.make_async_copy(hid, hid_hbm, sem_out.at[0])
    out_hid.start()
    for copy in cot_copies:
        copy.wait()

    def grad_step(step, carry):
        base = step * UNROLL
        for u in range(UNROLL):
            k = slot0 + base + u
            lane = pl.multiple_of(table[ROWS_AT, k] * side, side)
            col = pl.multiple_of(table[COLS_AT, k] * side, side)
            product = lax.dot_general(
                tok[:, pl.ds(lane, side)],
                cot[:, pl.ds(col, side)],
                (((0,), (0,)), ((), ())),
                preferred_element_type=jnp.float32,
            )
            grad[base + u] = jnp.where(k < count, product * scale, 0.0).astype(grad.dtype)
        return carry

    lax.fori_loop(0, slots // UNROLL, grad_step, 0)
    out_grad = pltpu.make_async_copy(grad, grad_hbm, sem_out.at[1])
    out_grad.start()
    out_hid.wait()
    out_grad.wait()


def run_blocks(table, placements, pieces, plan, cots, weights, count, slot0, slots, scale):
    capacity, side, _ = weights.shape
    group, ff_dev = cots[0].shape
    width = plan["width"]
    flat = [jnp.asarray(v, jnp.int32).reshape(()) for pair in placements for v in pair]
    place = jnp.stack(flat + [count, jnp.asarray(slot0, jnp.int32).reshape(())])
    plan = dict(plan, tokens=len(pieces), cotangents=len(cots), places=len(placements))
    n_any = len(pieces) + len(cots) + 1
    flops = 2 * side * side * group * (capacity + slots * len(cots))
    moved = 2 * (weights.size + slots * side * side + group * len(cots) * (ff_dev + width) + group * ff_dev)
    return pl.pallas_call(
        functools.partial(block_kernel, plan, slots, scale),
        out_shape=(
            jax.ShapeDtypeStruct((group, ff_dev), jnp.bfloat16),
            jax.ShapeDtypeStruct((slots, side, side), jnp.bfloat16),
        ),
        in_specs=[pl.BlockSpec(memory_space=pltpu.SMEM)] * 2 + [pl.BlockSpec(memory_space=pl.ANY)] * n_any,
        out_specs=(pl.BlockSpec(memory_space=pl.ANY),) * 2,
        scratch_shapes=[
            pltpu.VMEM((group * len(cots), width), jnp.bfloat16),
            pltpu.VMEM((group * len(cots), ff_dev), jnp.bfloat16),
            pltpu.VMEM((capacity, side, side), jnp.bfloat16),
            pltpu.VMEM((ff_dev // side, group, side), jnp.float32),
            pltpu.VMEM((group, ff_dev), jnp.bfloat16),
            pltpu.VMEM((slots, side, side), jnp.bfloat16),
            pltpu.SemaphoreType.DMA((len(plan["pieces"]),)),
            pltpu.SemaphoreType.DMA((len(cots),)),
            pltpu.SemaphoreType.DMA((4,)),
            pltpu.SemaphoreType.DMA((2,)),
        ],
        compiler_params=pltpu.CompilerParams(vmem_limit_bytes=40 << 20),
        cost_estimate=pl.CostEstimate(flops=flops, bytes_accessed=moved, transcendentals=0),
        name="blocks",
    )(table, place, *pieces, *cots, weights)


def gather_inputs(tokens, cotangent):
    tok_dev, width = tokens.shape
    quarter = width // 4
    row, col, group = lax.axis_index("row"), lax.axis_index("col"), cotangent.shape[0]
    x, core = col // 2, col % 2
    over_y = functools.partial(lax.ppermute, axis_name="dp", perm=[(0, 1), (1, 0)])
    over_x = functools.partial(lax.ppermute, axis_name="col", perm=[(0, 2), (2, 0), (1, 3), (3, 1)])
    over_core = functools.partial(lax.ppermute, axis_name="col", perm=[(0, 1), (1, 0), (2, 3), (3, 2)])

    def over_z(value, by):
        return lax.ppermute(value, "row", [(i, (i + by) % 4) for i in range(4)])

    mine = lax.dynamic_slice_in_dim(tokens, col * quarter, quarter, 1)
    other = over_y(mine)
    both = jnp.concatenate([mine, other], 0)
    hops = (1, 3, 2)
    arrived = [over_z(both, by) for by in hops]
    other_x = over_x(other)
    arrived_x = [over_x(v) for v in arrived]
    cot_other = over_y(cotangent)

    pieces, placements, listed = [], [], []

    def add(value, first, own, at_row, quarter_x, quarter_core):
        if not pieces or pieces[-1] is not value:
            pieces.append(value)
        row0 = (0 if own else group) + at_row * tok_dev
        listed.append((len(pieces) - 1, first, tok_dev, len(placements)))
        placements.append((row0, (quarter_x * 2 + quarter_core) * quarter))

    pieces.append(tokens)
    listed.append((0, 0, tok_dev, 0))
    placements.append((row * tok_dev, 0))
    for value, quarter_x in ((other, x), (other_x, 1 - x)):
        add(value, 0, False, row, quarter_x, core)
        add(over_core(value), 0, False, row, quarter_x, 1 - core)
    for values, quarter_x in ((arrived, x), (arrived_x, 1 - x)):
        for by, value in zip(hops, values):
            at_row = (row + 4 - by) % 4
            for sent, quarter_core in ((value, core), (over_core(value), 1 - core)):
                add(sent, 0, True, at_row, quarter_x, quarter_core)
                add(sent, tok_dev, False, at_row, quarter_x, quarter_core)
    return pieces, placements, listed, [cotangent, cot_other]


def on_device(tokens, cotangent, weight_blocks, block_rows, block_cols, block_count):
    groups, steps = lax.axis_size("dp"), lax.axis_size("row")
    tok_dev, width = tokens.shape
    group = cotangent.shape[0]
    weights = weight_blocks[0]
    capacity = weights.shape[0]
    scale = 1.0 / (group * groups) ** 0.5
    table = jnp.concatenate([block_rows, block_cols], 0)
    count = block_count[0]
    if (groups, steps, lax.axis_size("col")) == (2, 4, 4):
        slots = capacity // groups
        pieces, placements, listed, cots = gather_inputs(tokens, cotangent)
        plan = {"pieces": listed, "width": width}
        slot0 = lax.axis_index("dp") * slots
        hidden, grad = run_blocks(table, placements, pieces, plan, cots, weights, count, slot0, slots, scale)
        return hidden, grad[None]
    gathered = lax.all_gather(tokens, "row", axis=0, tiled=True)
    plan = {"pieces": [(0, 0, group, 0)], "width": width}
    hidden, partial = run_blocks(table, [(0, 0)], [gathered], plan, [cotangent], weights, count, 0, capacity, scale)
    return hidden, lax.psum_scatter(partial[None], "dp", scatter_dimension=1, tiled=True)


def solution(mesh):
    in_specs = (
        P(("dp", "row"), None),
        P("dp", ("row", "col")),
        P(("row", "col"), None, None, None),
        P(("row", "col"), None),
        P(("row", "col"), None),
        P(("row", "col")),
    )
    out_specs = (P("dp", ("row", "col")), P(("row", "col"), "dp", None, None))
    return jax.shard_map(
        on_device, mesh=mesh, in_specs=in_specs, out_specs=out_specs, check_vma=False
    )
```

time: 272 us -> 53.9 us (0.20); the launches traced: 269 us -> 53.6 us
  waiting for transfers between devices: 192 us -> 8.86 us
  matrix products: 35.2 us -> 0 us
  starting transfers between devices: 0.05 us -> 28.2 us
  between operations: 15.8 us -> 1.35 us
  other arithmetic: 12.5 us -> 0.7 us
  Pallas kernels: 0 us -> 9.61 us
  local copies, waits for them, and re-layouts: 13.1 us -> 4.92 us
    psum x4 -> x0, waiting for transfers between devices: 146 us -> none  [broadcast(): return lax.psum(jnp.where(mine, value, jnp.zeros_like(value)), axis)]
    reduce_scatter x1 -> x0, waiting for transfers between devices: 45.2 us -> none  [on_device(): lax.psum_scatter(term[None].astype(jnp.bfloat16), 'dp', scatter_dimension...]
    dot_general x12 -> x0, matrix products: 35.2 us -> none  [the longest x4 23.2 us: piece_terms(): jnp.einsum('nkb,nkc->kbc', blocks, grads, preferred_element_type=jnp.floa...]
    ppermute x0 -> x17, starting transfers between devices: none -> 28.2 us  [the longest x6 16.4 us: gather_inputs(): over_core(value)]
    pallas_call x0 -> x1, Pallas kernels: none -> 9.61 us  [run_blocks(): pl.pallas_call(functools.partial(block_kernel, plan, slots, scale), out_s...]
    gather x8 -> x0, local copies, waits for them, and re-layouts: 9.32 us -> none  [the longest x4 6.65 us: piece_terms(): blocks = piece.reshape(count, width // side, side)[:, rows, :]]
    ppermute x0 -> x17, waiting for transfers between devices: none -> 8.86 us  [the longest x3 6.83 us: over_z(): return lax.ppermute(value, 'row', [(i, (i + by) % 4) for i in range(4)])]
    convert_element_type x1 -> x0, other arithmetic: 5.37 us -> none  [on_device(): term[None].astype(jnp.bfloat16)]
  transfers between devices with their start and end apart: 5 -> 17, of which waited for: 5 -> 2; matrix products, arithmetic and copies ran while one was open for 3% -> 2% of each run, Pallas kernels for 0% -> 0%
where the time goes in v1:
time: 53.9 us; the launch traced here: 53.6 us
  starting transfers between devices  28.2 us (52%)
  Pallas kernels  9.61 us (18%)
  waiting for transfers between devices  8.86 us (16%)
  local copies, waits for them, and re-layouts  4.92 us (9%)
  between operations  1.35 us (3%)
  other arithmetic  0.7 us (1%)
    ppermute x6, starting transfers between devices, gather_inputs(): over_core(value)  16.4 us
    pallas_call x1, Pallas kernels, run_blocks(): pl.pallas_call(functools.partial(block_kernel, plan, slots, scale), out_s...  9.61 us
    ppermute x3, waiting for transfers between devices, over_z(): return lax.ppermute(value, 'row', [(i, (i + by) % 4) for i in range(4)])  6.83 us
    ppermute x2, starting transfers between devices, gather_inputs(): add(over_core(value), 0, False, row, quarter_x, 1 - core)  4.01 us
    unnamed x6, local copies, waits for them, and re-layouts  3.88 us
    ppermute x3, starting transfers between devices, over_z(): return lax.ppermute(value, 'row', [(i, (i + by) % 4) for i in range(4)])  3.39 us
    ppermute x1, waiting for transfers between devices, gather_inputs(): other = over_y(mine)  2 us
    ppermute x3, starting transfers between devices, gather_inputs(): arrived_x = [over_x(v) for v in arrived]  1.72 us
  transfers between devices with their start and end apart: 17, of which 2 were waited for; matrix products, arithmetic and copies ran while one was open for 2% of the time, Pallas kernels for 0%

profile of v1, /device:TPU:29, one launch (start us, length us, event | category | flops | bytes accessed | tf_op | source)
XLA Modules:
  0.0 53.6 jit_solution(16477823172975646374)
XLA Ops:
  0.6 0.9 %constant_dynamic-slice_fusion = bf16[16,3072]{1,0:T(8,128)(2,1)S(1)} fusion(bf16[16,12288]{1,0:T(8,128)(2,1)} %refs_2_.1, s32[]{:T(128)S(6)} %select_n.37), kind=kLoop, calls=%fused_computation.2 | loop fusion | bytes 196612 | tf_op jit(solution)/shard_map/dynamic_slice | solution.py:145
  1.5 0.2 collective-permute-start
  1.8 1.2 %collective-permute-start.16 = (bf16[64,3072]{1,0:T(8,128)(2,1)}, bf16[64,3072]{1,0:T(8,128)(2,1)S(1)}, u32[]{:S(2)}, u32[]{:S(2)}) collective-permute-start(bf16[64,3072]{1,0:T(8,128)(2,1)} %refs_19_.1), channel_id=1, source_target_pairs={{0,16},{16,0},{1,17},{17,1},{2,18},{18,2},{3,19},{19,3},{4,20},{20... | collective-permute-start | bytes 1179656 | tf_op jit(solution)/shard_map/ppermute | solution.py:152
  3.0 2.0 %collective-permute-done.refs_3_ = bf16[16,3072]{1,0:T(8,128)(2,1)S(1)} collective-permute-done((bf16[16,3072]{1,0:T(8,128)(2,1)S(1)}, bf16[16,3072]{1,0:T(8,128)(2,1)S(1)}, u32[]{:S(2)}, u32[]{:S(2)}) %collective-permute-start) | collective-permute-done | bytes 98336 | tf_op jit(solution)/shard_map/ppermute | solution.py:146
  5.0 1.2 %collective-permute-start.2 = (bf16[16,3072]{1,0:T(8,128)(2,1)S(1)}, bf16[16,3072]{1,0:T(8,128)(2,1)S(1)}, u32[]{:S(2)}, u32[]{:S(2)}) collective-permute-start(bf16[16,3072]{1,0:T(8,128)(2,1)S(1)} %collective-permute-done.refs_3_), channel_id=1, source_target_pairs={{0,2},{2,0},{1,3},{3,1},{4,6},{6,4},{5,7},{7,5},{8,10},{10,8},{9,1... | collective-permute-start | bytes 294920 | tf_op jit(solution)/shard_map/ppermute | solution.py:150
  6.4 3.4 %collective-permute-start.1 = (bf16[16,3072]{1,0:T(8,128)(2,1)S(1)}, bf16[16,3072]{1,0:T(8,128)(2,1)S(1)}, u32[]{:S(2)}, u32[]{:S(2)}) collective-permute-start(bf16[16,3072]{1,0:T(8,128)(2,1)S(1)} %collective-permute-done.refs_3_), channel_id=1, source_target_pairs={{0,1},{1,0},{2,3},{3,2},{4,5},{5,4},{6,7},{7,6},{8,9},{9,8},{10,11... | collective-permute-start | bytes 294920 | tf_op jit(solution)/shard_map/ppermute | solution.py:168
  9.8 0.2 collective-permute-start.6
  10.0 3.1 %collective-permute-start.4 = (bf16[32,3072]{1,0:T(8,128)(2,1)S(1)}, bf16[32,3072]{1,0:T(8,128)(2,1)S(1)}, u32[]{:S(2)}, u32[]{:S(2)}) collective-permute-start(bf16[32,3072]{1,0:T(8,128)(2,1)S(1)} %pad_maximum_fusion), channel_id=1, source_target_pairs={{0,4},{4,8},{8,12},{12,0},{1,5},{5,9},{9,13},{13,1},{2,6},{6,10},{... | collective-permute-start | bytes 589832 | tf_op jit(solution)/shard_map/ppermute | solution.py:143
  13.1 0.6 %collective-permute-start.3 = (bf16[16,3072]{1,0:T(8,128)(2,1)S(1)}, bf16[16,3072]{1,0:T(8,128)(2,1)S(1)}, u32[]{:S(2)}, u32[]{:S(2)}) collective-permute-start(bf16[16,3072]{1,0:T(8,128)(2,1)S(1)} %collective-permute-done.2.refs_5_), channel_id=1, source_target_pairs={{0,1},{1,0},{2,3},{3,2},{4,5},{5,4},{6,7},{7,6},{8,9},{9,8},{10,11... | collective-permute-start | bytes 294920 | tf_op jit(solution)/shard_map/ppermute | solution.py:168
  13.6 6.8 %collective-permute-done.8.refs_11_ = bf16[32,3072]{1,0:T(8,128)(2,1)S(1)} collective-permute-done((bf16[32,3072]{1,0:T(8,128)(2,1)S(1)}, bf16[32,3072]{1,0:T(8,128)(2,1)S(1)}, u32[]{:S(2)}, u32[]{:S(2)}) %collective-permute-start.8) | collective-permute-done | bytes 196640 | tf_op jit(solution)/shard_map/ppermute | solution.py:143
  20.5 0.3 collective-permute-start.14
  20.7 4.3 %collective-permute-start.9 = (bf16[32,3072]{1,0:T(8,128)(2,1)S(1)}, bf16[32,3072]{1,0:T(8,128)(2,1)S(1)}, u32[]{:S(2)}, u32[]{:S(2)}) collective-permute-start(bf16[32,3072]{1,0:T(8,128)(2,1)S(1)} %collective-permute-done.8.refs_11_), channel_id=1, source_target_pairs={{0,1},{1,0},{2,3},{3,2},{4,5},{5,4},{6,7},{7,6},{8,9},{9,8},{10,11... | collective-permute-start | bytes 589832 | tf_op jit(solution)/shard_map/ppermute | solution.py:172
  25.1 1.2 %collective-permute-start.12 = (bf16[32,3072]{1,0:T(8,128)(2,1)S(1)}, bf16[32,3072]{1,0:T(8,128)(2,1)S(1)}, u32[]{:S(2)}, u32[]{:S(2)}) collective-permute-start(bf16[32,3072]{1,0:T(8,128)(2,1)S(1)} %collective-permute-done.6.refs_9_), channel_id=1, source_target_pairs={{0,2},{2,0},{1,3},{3,1},{4,6},{6,4},{5,7},{7,5},{8,10},{10,8},{9,1... | collective-permute-start | bytes 589832 | tf_op jit(solution)/shard_map/ppermute | solution.py:151
  26.3 0.3 collective-permute-start.10
  26.5 0.6 %collective-permute-start.7 = (bf16[32,3072]{1,0:T(8,128)(2,1)S(1)}, bf16[32,3072]{1,0:T(8,128)(2,1)S(1)}, u32[]{:S(2)}, u32[]{:S(2)}) collective-permute-start(bf16[32,3072]{1,0:T(8,128)(2,1)S(1)} %collective-permute-done.6.refs_9_), channel_id=1, source_target_pairs={{0,1},{1,0},{2,3},{3,2},{4,5},{5,4},{6,7},{7,6},{8,9},{9,8},{10,11... | collective-permute-start | bytes 589832 | tf_op jit(solution)/shard_map/ppermute | solution.py:172
  27.2 5.0 %collective-permute-start.5 = (bf16[32,3072]{1,0:T(8,128)(2,1)S(1)}, bf16[32,3072]{1,0:T(8,128)(2,1)S(1)}, u32[]{:S(2)}, u32[]{:S(2)}) collective-permute-start(bf16[32,3072]{1,0:T(8,128)(2,1)S(1)} %collective-permute-done.4.refs_7_), channel_id=1, source_target_pairs={{0,1},{1,0},{2,3},{3,2},{4,5},{5,4},{6,7},{7,6},{8,9},{9,8},{10,11... | collective-permute-start | bytes 589832 | tf_op jit(solution)/shard_map/ppermute | solution.py:172
  32.2 4.2 %collective-permute-start.13 = (bf16[32,3072]{1,0:T(8,128)(2,1)S(1)}, bf16[32,3072]{1,0:T(8,128)(2,1)S(1)}, u32[]{:S(2)}, u32[]{:S(2)}) collective-permute-start(bf16[32,3072]{1,0:T(8,128)(2,1)S(1)} %collective-permute-done.12.refs_15_), channel_id=1, source_target_pairs={{0,1},{1,0},{2,3},{3,2},{4,5},{5,4},{6,7},{7,6},{8,9},{9,8},{10,11... | collective-permute-start | bytes 589832 | tf_op jit(solution)/shard_map/ppermute | solution.py:172
  36.4 2.2 %collective-permute-start.11 = (bf16[32,3072]{1,0:T(8,128)(2,1)S(1)}, bf16[32,3072]{1,0:T(8,128)(2,1)S(1)}, u32[]{:S(2)}, u32[]{:S(2)}) collective-permute-start(bf16[32,3072]{1,0:T(8,128)(2,1)S(1)} %collective-permute-done.10.refs_13_), channel_id=1, source_target_pairs={{0,1},{1,0},{2,3},{3,2},{4,5},{5,4},{6,7},{7,6},{8,9},{9,8},{10,11... | collective-permute-start | bytes 589832 | tf_op jit(solution)/shard_map/ppermute | solution.py:172
  39.3 0.1 stack.3.refs_1_
  39.4 0.7 %pad_add_fusion.refs_0_ = s32[2,96]{1,0:T(2,128)S(1)} fusion(s32[1,96]{1,0:T(1,128)} %param.10, s32[1,96]{1,0:T(1,128)} %param.9), kind=kLoop, calls=%fused_computation.1 | loop fusion | flops 192 | bytes 1536 | tf_op jit(solution)/shard_map/concatenate | solution.py:185
  40.2 1.9 %copy-done = bf16[1,96,128,128]{3,2,1,0:T(8,128)(2,1)S(1)} copy-done((bf16[1,96,128,128]{3,2,1,0:T(8,128)(2,1)S(1)}, bf16[1,96,128,128]{3,2,1,0:T(8,128)(2,1)}, u32[]{:S(2)}) %copy-start) | copy-done | bytes 3145752
  42.0 1.0 %copy-done.1 = bf16[16,12288]{1,0:T(8,128)(2,1)S(1)} copy-done((bf16[16,12288]{1,0:T(8,128)(2,1)S(1)}, bf16[16,12288]{1,0:T(8,128)(2,1)}, u32[]{:S(2)}) %copy-start.1) | copy-done | bytes 393240
  43.0 1.0 %copy-done.2 = bf16[64,3072]{1,0:T(8,128)(2,1)S(1)} copy-done((bf16[64,3072]{1,0:T(8,128)(2,1)S(1)}, bf16[64,3072]{1,0:T(8,128)(2,1)}, u32[]{:S(2)}) %copy-start.2) | copy-done | bytes 393240
  44.0 9.6 %blocks.1 = (bf16[64,3072]{1,0:T(8,128)(2,1)}, bf16[48,128,128]{2,1,0:T(8,128)(2,1)}) custom-call(s32[2,96]{1,0:T(2,128)S(1)} %pad_add_fusion.refs_0_, s32[60]{0:T(128)S(1)} %stack.3.refs_1_, bf16[16,12288]{1,0:T(8,128)(2,1)S(1)} %copy-done.1, bf16[16,3072]{1,0:T(8,128)(2,1)S(1)} %collective-permute-done.refs_3_, ...), custom_call_target="tpu_custom_call" | custom-call | flops 402653184 | bytes 9043968 | tf_op jit(solution)/shard_map/blocks/pallas_call | solution.py:107
  (21 shorter events, 0.2 us)
Async XLA Ops:
  1.5 3.5 %collective-permute-start = (bf16[16,3072]{1,0:T(8,128)(2,1)S(1)}, bf16[16,3072]{1,0:T(8,128)(2,1)S(1)}, u32[]{:S(2)}, u32[]{:S(2)}) collective-permute-start(bf16[16,3072]{1,0:T(8,128)(2,1)S(1)} %constant_dynamic-slice_fusion), channel_id=1, source_target_pairs={{0,16},{16,0},{1,17},{17,1},{2,18},{18,2},{3,19},{19,3},{4,20},{20... | collective-permute-start | bytes 294920 | tf_op jit(solution)/shard_map/ppermute | solution.py:146
  1.8 24.8 %collective-permute-start.16 = (bf16[64,3072]{1,0:T(8,128)(2,1)}, bf16[64,3072]{1,0:T(8,128)(2,1)S(1)}, u32[]{:S(2)}, u32[]{:S(2)}) collective-permute-start(bf16[64,3072]{1,0:T(8,128)(2,1)} %refs_19_.1), channel_id=1, source_target_pairs={{0,16},{16,0},{1,17},{17,1},{2,18},{18,2},{3,19},{19,3},{4,20},{20... | collective-permute-start | bytes 1179656 | tf_op jit(solution)/shard_map/ppermute | solution.py:152
  5.0 5.0 %collective-permute-start.2 = (bf16[16,3072]{1,0:T(8,128)(2,1)S(1)}, bf16[16,3072]{1,0:T(8,128)(2,1)S(1)}, u32[]{:S(2)}, u32[]{:S(2)}) collective-permute-start(bf16[16,3072]{1,0:T(8,128)(2,1)S(1)} %collective-permute-done.refs_3_), channel_id=1, source_target_pairs={{0,2},{2,0},{1,3},{3,1},{4,6},{6,4},{5,7},{7,5},{8,10},{10,8},{9,1... | collective-permute-start | bytes 294920 | tf_op jit(solution)/shard_map/ppermute | solution.py:150
  6.2 14.2 %collective-permute-start.8 = (bf16[32,3072]{1,0:T(8,128)(2,1)S(1)}, bf16[32,3072]{1,0:T(8,128)(2,1)S(1)}, u32[]{:S(2)}, u32[]{:S(2)}) collective-permute-start(bf16[32,3072]{1,0:T(8,128)(2,1)S(1)} %pad_maximum_fusion), channel_id=1, source_target_pairs={{0,8},{4,12},{8,0},{12,4},{1,9},{5,13},{9,1},{13,5},{2,10},{6,14},... | collective-permute-start | bytes 589832 | tf_op jit(solution)/shard_map/ppermute | solution.py:143
  6.4 6.7 %collective-permute-start.1 = (bf16[16,3072]{1,0:T(8,128)(2,1)S(1)}, bf16[16,3072]{1,0:T(8,128)(2,1)S(1)}, u32[]{:S(2)}, u32[]{:S(2)}) collective-permute-start(bf16[16,3072]{1,0:T(8,128)(2,1)S(1)} %collective-permute-done.refs_3_), channel_id=1, source_target_pairs={{0,1},{1,0},{2,3},{3,2},{4,5},{5,4},{6,7},{7,6},{8,9},{9,8},{10,11... | collective-permute-start | bytes 294920 | tf_op jit(solution)/shard_map/ppermute | solution.py:168
  9.8 15.3 %collective-permute-start.6 = (bf16[32,3072]{1,0:T(8,128)(2,1)S(1)}, bf16[32,3072]{1,0:T(8,128)(2,1)S(1)}, u32[]{:S(2)}, u32[]{:S(2)}) collective-permute-start(bf16[32,3072]{1,0:T(8,128)(2,1)S(1)} %pad_maximum_fusion), channel_id=1, source_target_pairs={{0,12},{4,0},{8,4},{12,8},{1,13},{5,1},{9,5},{13,9},{2,14},{6,2},{... | collective-permute-start | bytes 589832 | tf_op jit(solution)/shard_map/ppermute | solution.py:143
  10.0 16.3 %collective-permute-start.4 = (bf16[32,3072]{1,0:T(8,128)(2,1)S(1)}, bf16[32,3072]{1,0:T(8,128)(2,1)S(1)}, u32[]{:S(2)}, u32[]{:S(2)}) collective-permute-start(bf16[32,3072]{1,0:T(8,128)(2,1)S(1)} %pad_maximum_fusion), channel_id=1, source_target_pairs={{0,4},{4,8},{8,12},{12,0},{1,5},{5,9},{9,13},{13,1},{2,6},{6,10},{... | collective-permute-start | bytes 589832 | tf_op jit(solution)/shard_map/ppermute | solution.py:143
  13.1 7.6 %collective-permute-start.3 = (bf16[16,3072]{1,0:T(8,128)(2,1)S(1)}, bf16[16,3072]{1,0:T(8,128)(2,1)S(1)}, u32[]{:S(2)}, u32[]{:S(2)}) collective-permute-start(bf16[16,3072]{1,0:T(8,128)(2,1)S(1)} %collective-permute-done.2.refs_5_), channel_id=1, source_target_pairs={{0,1},{1,0},{2,3},{3,2},{4,5},{5,4},{6,7},{7,6},{8,9},{9,8},{10,11... | collective-permute-start | bytes 294920 | tf_op jit(solution)/shard_map/ppermute | solution.py:168
  20.5 6.7 %collective-permute-start.14 = (bf16[32,3072]{1,0:T(8,128)(2,1)S(1)}, bf16[32,3072]{1,0:T(8,128)(2,1)S(1)}, u32[]{:S(2)}, u32[]{:S(2)}) collective-permute-start(bf16[32,3072]{1,0:T(8,128)(2,1)S(1)} %collective-permute-done.8.refs_11_), channel_id=1, source_target_pairs={{0,2},{2,0},{1,3},{3,1},{4,6},{6,4},{5,7},{7,5},{8,10},{10,8},{9,1... | collective-permute-start | bytes 589832 | tf_op jit(solution)/shard_map/ppermute | solution.py:151
  20.7 11.5 %collective-permute-start.9 = (bf16[32,3072]{1,0:T(8,128)(2,1)S(1)}, bf16[32,3072]{1,0:T(8,128)(2,1)S(1)}, u32[]{:S(2)}, u32[]{:S(2)}) collective-permute-start(bf16[32,3072]{1,0:T(8,128)(2,1)S(1)} %collective-permute-done.8.refs_11_), channel_id=1, source_target_pairs={{0,1},{1,0},{2,3},{3,2},{4,5},{5,4},{6,7},{7,6},{8,9},{9,8},{10,11... | collective-permute-start | bytes 589832 | tf_op jit(solution)/shard_map/ppermute | solution.py:172
  25.1 7.2 %collective-permute-start.12 = (bf16[32,3072]{1,0:T(8,128)(2,1)S(1)}, bf16[32,3072]{1,0:T(8,128)(2,1)S(1)}, u32[]{:S(2)}, u32[]{:S(2)}) collective-permute-start(bf16[32,3072]{1,0:T(8,128)(2,1)S(1)} %collective-permute-done.6.refs_9_), channel_id=1, source_target_pairs={{0,2},{2,0},{1,3},{3,1},{4,6},{6,4},{5,7},{7,5},{8,10},{10,8},{9,1... | collective-permute-start | bytes 589832 | tf_op jit(solution)/shard_map/ppermute | solution.py:151
  26.3 10.1 %collective-permute-start.10 = (bf16[32,3072]{1,0:T(8,128)(2,1)S(1)}, bf16[32,3072]{1,0:T(8,128)(2,1)S(1)}, u32[]{:S(2)}, u32[]{:S(2)}) collective-permute-start(bf16[32,3072]{1,0:T(8,128)(2,1)S(1)} %collective-permute-done.4.refs_7_), channel_id=1, source_target_pairs={{0,2},{2,0},{1,3},{3,1},{4,6},{6,4},{5,7},{7,5},{8,10},{10,8},{9,1... | collective-permute-start | bytes 589832 | tf_op jit(solution)/shard_map/ppermute | solution.py:151
  26.5 13.6 %collective-permute-start.7 = (bf16[32,3072]{1,0:T(8,128)(2,1)S(1)}, bf16[32,3072]{1,0:T(8,128)(2,1)S(1)}, u32[]{:S(2)}, u32[]{:S(2)}) collective-permute-start(bf16[32,3072]{1,0:T(8,128)(2,1)S(1)} %collective-permute-done.6.refs_9_), channel_id=1, source_target_pairs={{0,1},{1,0},{2,3},{3,2},{4,5},{5,4},{6,7},{7,6},{8,9},{9,8},{10,11... | collective-permute-start | bytes 589832 | tf_op jit(solution)/shard_map/ppermute | solution.py:172
  27.2 12.9 %collective-permute-start.5 = (bf16[32,3072]{1,0:T(8,128)(2,1)S(1)}, bf16[32,3072]{1,0:T(8,128)(2,1)S(1)}, u32[]{:S(2)}, u32[]{:S(2)}) collective-permute-start(bf16[32,3072]{1,0:T(8,128)(2,1)S(1)} %collective-permute-done.4.refs_7_), channel_id=1, source_target_pairs={{0,1},{1,0},{2,3},{3,2},{4,5},{5,4},{6,7},{7,6},{8,9},{9,8},{10,11... | collective-permute-start | bytes 589832 | tf_op jit(solution)/shard_map/ppermute | solution.py:172
  32.2 7.9 %collective-permute-start.15 = (bf16[32,3072]{1,0:T(8,128)(2,1)S(1)}, bf16[32,3072]{1,0:T(8,128)(2,1)S(1)}, u32[]{:S(2)}, u32[]{:S(2)}) collective-permute-start(bf16[32,3072]{1,0:T(8,128)(2,1)S(1)} %collective-permute-done.14.refs_17_), channel_id=1, source_target_pairs={{0,1},{1,0},{2,3},{3,2},{4,5},{5,4},{6,7},{7,6},{8,9},{9,8},{10,11... | collective-permute-start | bytes 589832 | tf_op jit(solution)/shard_map/ppermute | solution.py:172
  32.2 7.9 %collective-permute-start.13 = (bf16[32,3072]{1,0:T(8,128)(2,1)S(1)}, bf16[32,3072]{1,0:T(8,128)(2,1)S(1)}, u32[]{:S(2)}, u32[]{:S(2)}) collective-permute-start(bf16[32,3072]{1,0:T(8,128)(2,1)S(1)} %collective-permute-done.12.refs_15_), channel_id=1, source_target_pairs={{0,1},{1,0},{2,3},{3,2},{4,5},{5,4},{6,7},{7,6},{8,9},{9,8},{10,11... | collective-permute-start | bytes 589832 | tf_op jit(solution)/shard_map/ppermute | solution.py:172
  36.4 3.7 %collective-permute-start.11 = (bf16[32,3072]{1,0:T(8,128)(2,1)S(1)}, bf16[32,3072]{1,0:T(8,128)(2,1)S(1)}, u32[]{:S(2)}, u32[]{:S(2)}) collective-permute-start(bf16[32,3072]{1,0:T(8,128)(2,1)S(1)} %collective-permute-done.10.refs_13_), channel_id=1, source_target_pairs={{0,1},{1,0},{2,3},{3,2},{4,5},{5,4},{6,7},{7,6},{8,9},{9,8},{10,11... | collective-permute-start | bytes 589832 | tf_op jit(solution)/shard_map/ppermute | solution.py:172
  40.1 1.9 %copy-start = (bf16[1,96,128,128]{3,2,1,0:T(8,128)(2,1)S(1)}, bf16[1,96,128,128]{3,2,1,0:T(8,128)(2,1)}, u32[]{:S(2)}) copy-start(bf16[1,96,128,128]{3,2,1,0:T(8,128)(2,1)} %param.8) | copy-start | bytes 9437188
  42.0 1.0 %copy-start.1 = (bf16[16,12288]{1,0:T(8,128)(2,1)S(1)}, bf16[16,12288]{1,0:T(8,128)(2,1)}, u32[]{:S(2)}) copy-start(bf16[16,12288]{1,0:T(8,128)(2,1)} %refs_2_.1) | copy-start | bytes 1179652
  43.0 1.0 %copy-start.2 = (bf16[64,3072]{1,0:T(8,128)(2,1)S(1)}, bf16[64,3072]{1,0:T(8,128)(2,1)}, u32[]{:S(2)}) copy-start(bf16[64,3072]{1,0:T(8,128)(2,1)} %refs_19_.1) | copy-start | bytes 1179652

commit v2 on v0

v2 whole, which is shorter than its diff:
```python
import functools

import jax
import jax.numpy as jnp
from jax import lax
from jax.experimental import pallas as pl
from jax.experimental.pallas import tpu as pltpu
from jax.sharding import PartitionSpec as P

UNROLL = 24
OUT_PARTS = 2
VMEM_LIMIT = 40 << 20


def assemble(place, pieces, plan, tok):
    for operand, first, rows, row0, at in plan:
        src = pieces[operand]
        if at is None:
            tok[row0 : row0 + rows, :] = src[first : first + rows, :]
        else:
            lane = pl.multiple_of(place[at], 128)
            tok[row0 : row0 + rows, pl.ds(lane, src.shape[1])] = src[first : first + rows, :]


def hidden_kernel(plan, n, shard, table, place, *refs):
    pieces, w, hid_hbm = refs[:n], refs[n], refs[n + 1]
    tok, acc, hid, sem_out = refs[n + 2 :]
    capacity, side = w.shape[0], w.shape[1]
    col_blocks, group = acc.shape[0], acc.shape[1]
    acc[...] = jnp.zeros_like(acc)
    assemble(place, pieces, plan, tok)
    live = place[place.shape[0] - 2]

    def step_of(step, carry):
        base = step * UNROLL
        products = []
        for u in range(UNROLL):
            k = base + u
            lane = pl.multiple_of(table[0, k] * side, side)
            product = jnp.dot(tok[:, pl.ds(lane, side)], w[k], preferred_element_type=jnp.float32)
            products.append(jnp.where(k < live, product, 0.0))
        for u in range(UNROLL):
            col = table[1, base + u]
            acc[col] = acc[col] + products[u]
        return carry

    lax.fori_loop(0, capacity // UNROLL, step_of, 0)
    for j in range(col_blocks):
        for i in range(group // shard):
            row0 = pl.multiple_of(place[i], 16)
            hid[pl.ds(row0, shard), j * side : (j + 1) * side] = acc[j, i * shard : (i + 1) * shard, :].astype(hid.dtype)
    out = pltpu.make_async_copy(hid, hid_hbm, sem_out.at[0])
    out.start()
    out.wait()


def grad_kernel(plan, n, shard, scale, table, place, *refs):
    pieces = refs[:n]
    n_cot = (len(refs) - n - 5)
    cots, grad_hbm = refs[n : n + n_cot], refs[n + n_cot]
    tok, cot, grad, sem_out = refs[n + n_cot + 1 :]
    slots, side = grad.shape[0], grad.shape[1]
    group = cots[0].shape[0]
    assemble(place, pieces, plan, tok)
    for g, src in enumerate(cots):
        for i in range(group // shard):
            row0 = pl.multiple_of(place[i], 16)
            at = g * group + i * shard
            cot[at : at + shard, :] = src[pl.ds(row0, shard), :]
    live = place[place.shape[0] - 2]
    slot0 = place[place.shape[0] - 1]

    def step_of(step, carry):
        base = step * UNROLL
        for u in range(UNROLL):
            k = slot0 + base + u
            lane = pl.multiple_of(table[0, k] * side, side)
            col = pl.multiple_of(table[1, k] * side, side)
            product = lax.dot_general(
                tok[:, pl.ds(lane, side)],
                cot[:, pl.ds(col, side)],
                (((0,), (0,)), ((), ())),
                preferred_element_type=jnp.float32,
            )
            grad[base + u] = jnp.where(k < live, product * scale, 0.0).astype(grad.dtype)
        return carry

    per_part = slots // OUT_PARTS
    copies = []
    for i in range(OUT_PARTS):
        lax.fori_loop(i * per_part // UNROLL, (i + 1) * per_part // UNROLL, step_of, 0)
        part = pl.ds(i * per_part, per_part)
        copies.append(pltpu.make_async_copy(grad.at[part], grad_hbm.at[part], sem_out.at[i]))
        copies[-1].start()
    for copy in copies:
        copy.wait()


def call_hidden(table, place, pieces, plan, weights, group, ff_dev, width, shard):
    capacity, side, _ = weights.shape
    cost = pl.CostEstimate(
        flops=2 * side * side * group * capacity,
        bytes_accessed=2 * (weights.size + group * (width + ff_dev)),
        transcendentals=0,
    )
    return pl.pallas_call(
        functools.partial(hidden_kernel, plan, len(pieces), shard),
        out_shape=jax.ShapeDtypeStruct((group, ff_dev), jnp.bfloat16),
        in_specs=[pl.BlockSpec(memory_space=pltpu.SMEM)] * 2
        + [pl.BlockSpec(memory_space=pltpu.VMEM)] * len(pieces)
        + [pl.BlockSpec(memory_space=pltpu.VMEM)],
        out_specs=pl.BlockSpec(memory_space=pltpu.HBM),
        scratch_shapes=[
            pltpu.VMEM((group, width), jnp.bfloat16),
            pltpu.VMEM((ff_dev // side, group, side), jnp.float32),
            pltpu.VMEM((group, ff_dev), jnp.bfloat16),
            pltpu.SemaphoreType.DMA((1,)),
        ],
        compiler_params=pltpu.CompilerParams(vmem_limit_bytes=VMEM_LIMIT),
        cost_estimate=cost,
        name="hidden",
    )(table, place, *pieces, weights)


def call_grad(table, place, pieces, plan, cots, slots, side, width, shard, scale):
    group, ff_dev = cots[0].shape
    total = group * len(cots)
    cost = pl.CostEstimate(
        flops=2 * side * side * total * slots,
        bytes_accessed=2 * (slots * side * side + total * (width + ff_dev)),
        transcendentals=0,
    )
    return pl.pallas_call(
        functools.partial(grad_kernel, plan, len(pieces), shard, scale),
        out_shape=jax.ShapeDtypeStruct((slots, side, side), jnp.bfloat16),
        in_specs=[pl.BlockSpec(memory_space=pltpu.SMEM)] * 2
        + [pl.BlockSpec(memory_space=pltpu.VMEM)] * (len(pieces) + len(cots)),
        out_specs=pl.BlockSpec(memory_space=pltpu.HBM),
        scratch_shapes=[
            pltpu.VMEM((total, width), jnp.bfloat16),
            pltpu.VMEM((total, ff_dev), jnp.bfloat16),
            pltpu.VMEM((slots, side, side), jnp.bfloat16),
            pltpu.SemaphoreType.DMA((OUT_PARTS,)),
        ],
        compiler_params=pltpu.CompilerParams(vmem_limit_bytes=VMEM_LIMIT),
        cost_estimate=cost,
        name="grad",
    )(table, place, *pieces, *cots)


def two_group_plan(table, count, tokens, cotangent, weights, scale):
    tok_dev, width = tokens.shape
    quarter = width // 4
    group, ff_dev = cotangent.shape
    capacity, side, _ = weights.shape
    slots = capacity // 2
    row, col = lax.axis_index("row"), lax.axis_index("col")
    x, core = col // 2, col % 2
    swap_y = functools.partial(lax.ppermute, axis_name="dp", perm=[(0, 1), (1, 0)])

    def over_y(bundle):
        value, parts = bundle
        return swap_y(value), [(not own, shard, at) for own, shard, at in parts]

    def over_x(bundle):
        value, parts = bundle
        moved = lax.ppermute(value, "col", [(0, 2), (2, 0), (1, 3), (3, 1)])
        return moved, [(own, shard, at ^ 1) for own, shard, at in parts]

    def over_core(bundle):
        value, parts = bundle
        moved = lax.ppermute(value, "col", [(0, 1), (1, 0), (2, 3), (3, 2)])
        return moved, [(own, shard, at ^ 2) for own, shard, at in parts]

    def over_z(bundle, shard):
        value, parts = bundle
        by = (0, 1, 3, 2)[shard]
        moved = lax.ppermute(value, "row", [(i, (i + by) % 4) for i in range(4)])
        return moved, [(own, shard, at) for own, _, at in parts]

    def join(*bundles):
        return jnp.concatenate([v for v, _ in bundles], 0), [p for _, parts in bundles for p in parts]

    def cut(bundle, i, j):
        return bundle[0][i * tok_dev : j * tok_dev], bundle[1][i:j]

    def after(bundle, *earlier):
        return lax.optimization_barrier((bundle[0], [e[0] for e in earlier]))[0], bundle[1]

    place = [((row + 4 - by) % 4) * tok_dev for by in (0, 1, 3, 2)]
    place += [(xx * 2 + cc) * quarter for xx, cc in ((x, core), (1 - x, core), (x, 1 - core), (1 - x, 1 - core))]
    place = jnp.stack(place + [count, lax.axis_index("dp") * slots]).astype(jnp.int32)
    mine = lax.dynamic_slice_in_dim(tokens, col * quarter, quarter, 1)

    def planned(bundles, pick):
        pieces, plan = [tokens], [(0, 0, tok_dev, 0, None)]
        for value, parts in bundles:
            if any(map(pick, parts)):
                for i, (own, shard, at) in enumerate(parts):
                    if pick((own, shard, at)):
                        plan.append((len(pieces), i * tok_dev, tok_dev, (0 if own else group) + shard * tok_dev, 4 + at))
                pieces.append(value)
        return pieces, plan

    def run_hidden(*bundles):
        pieces, plan = planned(bundles, lambda part: part[0])
        assert len(plan) == 13
        return call_hidden(table, place, pieces, plan, weights, group, ff_dev, width, tok_dev)

    mine = (mine, [(True, 0, 0)])
    other0 = over_y(mine)
    own3 = over_z(mine, 3)
    both = join(mine, other0)
    both1 = over_z(both, 1)
    both2 = over_z(both, 2)
    other3 = over_y(own3)
    cot_other = swap_y(after((cotangent, None), other3)[0])
    own2, other2 = cut(both2, 0, 1), cut(both2, 1, 2)
    first = join(own3, other0)
    first_x = over_x(first)
    both1_x = over_x(both1)
    own2_x = over_x(own2)
    last = join(other3, other2)
    last_x = over_x(last)
    settled, (table, place) = lax.optimization_barrier((join(first, both1)[0], (table, place)))
    core_a = over_core((settled, join(first, both1)[1]))
    core_b = over_core(join(first_x, both1_x, own2, own2_x))
    hidden = run_hidden(first, both1, own2, first_x, both1_x, own2_x, core_a, core_b)
    core_c = over_core(join(last, last_x))
    got = [first, both1, own2, first_x, both1_x, own2_x, core_a, core_b, last, last_x, core_c]
    pieces, plan = planned(got, lambda part: True)
    assert len(plan) == 29
    grad = call_grad(table, place, pieces, plan, [cotangent, cot_other], slots, side, width, tok_dev, scale)
    return hidden, grad


def on_device(tokens, cotangent, weight_blocks, block_rows, block_cols, block_count):
    groups, steps = lax.axis_size("dp"), lax.axis_size("row")
    tok_dev, width = tokens.shape
    group, ff_dev = cotangent.shape
    weights = weight_blocks[0]
    capacity, side, _ = weights.shape
    scale = 1.0 / (group * groups) ** 0.5
    table, count = jnp.concatenate([block_rows, block_cols], 0), block_count[0]
    if (groups, steps, lax.axis_size("col")) == (2, 4, 4):
        hidden, grad = two_group_plan(table, count, tokens, cotangent, weights, scale)
        return hidden, grad[None]
    gathered = lax.all_gather(tokens, "row", axis=0, tiled=True)
    zero = jnp.zeros((), jnp.int32)
    place = jnp.stack([zero, count, zero])
    plan = [(0, 0, group, 0, None)]
    hidden = call_hidden(table, place, [gathered], plan, weights, group, ff_dev, width, group)
    partial = call_grad(table, place, [gathered], plan, [cotangent], capacity, side, width, group, scale)
    return hidden, lax.psum_scatter(partial[None], "dp", scatter_dimension=1, tiled=True)


def solution(mesh):
    in_specs = (
        P(("dp", "row"), None),
        P("dp", ("row", "col")),
        P(("row", "col"), None, None, None),
        P(("row", "col"), None),
        P(("row", "col"), None),
        P(("row", "col")),
    )
    out_specs = (P("dp", ("row", "col")), P(("row", "col"), "dp", None, None))
    return jax.shard_map(
        on_device, mesh=mesh, in_specs=in_specs, out_specs=out_specs, check_vma=False
    )
```

time: 272 us -> 39.2 us (0.14); the launches traced: 269 us -> 39 us
  waiting for transfers between devices: 192 us -> 9.88 us
  matrix products: 35.2 us -> 0 us
  starting transfers between devices: 0.05 us -> 20 us
  between operations: 15.8 us -> 1.37 us
  local copies, waits for them, and re-layouts: 13.1 us -> 1.08 us
  other arithmetic: 12.5 us -> 0.81 us
  Pallas kernels: 0 us -> 5.79 us
    psum x4 -> x0, waiting for transfers between devices: 146 us -> none  [broadcast(): return lax.psum(jnp.where(mine, value, jnp.zeros_like(value)), axis)]
    reduce_scatter x1 -> x0, waiting for transfers between devices: 45.2 us -> none  [on_device(): lax.psum_scatter(term[None].astype(jnp.bfloat16), 'dp', scatter_dimension...]
    dot_general x12 -> x0, matrix products: 35.2 us -> none  [the longest x4 23.2 us: piece_terms(): jnp.einsum('nkb,nkc->kbc', blocks, grads, preferred_element_type=jnp.floa...]
    ppermute x0 -> x13, starting transfers between devices: none -> 20 us  [the longest x3 7.23 us: over_core(): moved = lax.ppermute(value, 'col', [(0, 1), (1, 0), (2, 3), (3, 2)])]
    ppermute x0 -> x13, waiting for transfers between devices: none -> 9.88 us  [the longest x4 4.89 us: over_x(): moved = lax.ppermute(value, 'col', [(0, 2), (2, 0), (1, 3), (3, 1)])]
    gather x8 -> x0, local copies, waits for them, and re-layouts: 9.32 us -> none  [the longest x4 6.65 us: piece_terms(): blocks = piece.reshape(count, width // side, side)[:, rows, :]]
    pallas_call x0 -> x2, Pallas kernels: none -> 5.79 us  [the longest x1 2.93 us: call_hidden(): pl.pallas_call(functools.partial(hidden_kernel, plan, len(pieces), shard)...]
    convert_element_type x1 -> x0, other arithmetic: 5.37 us -> none  [on_device(): term[None].astype(jnp.bfloat16)]
  transfers between devices with their start and end apart: 5 -> 13, of which waited for: 5 -> 5; matrix products, arithmetic and copies ran while one was open for 3% -> 2% of each run, Pallas kernels for 0% -> 8%
where the time goes in v2:
time: 39.2 us; the launch traced here: 39 us
  starting transfers between devices  20 us (51%)
  waiting for transfers between devices  9.88 us (25%)
  Pallas kernels  5.79 us (15%)
  between operations  1.37 us (3%)
  local copies, waits for them, and re-layouts  1.08 us (3%)
  other arithmetic  0.81 us (2%)
    ppermute x3, starting transfers between devices, over_core(): moved = lax.ppermute(value, 'col', [(0, 1), (1, 0), (2, 3), (3, 2)])  7.23 us
    ppermute x4, waiting for transfers between devices, over_x(): moved = lax.ppermute(value, 'col', [(0, 2), (2, 0), (1, 3), (3, 1)])  4.89 us
    ppermute x4, starting transfers between devices, over_x(): moved = lax.ppermute(value, 'col', [(0, 2), (2, 0), (1, 3), (3, 1)])  4.08 us
    ppermute x2, starting transfers between devices, over_y(): return (swap_y(value), [(not own, shard, at) for own, shard, at in parts])  3.9 us
    ppermute x3, starting transfers between devices, over_z(): moved = lax.ppermute(value, 'row', [(i, (i + by) % 4) for i in range(4)])  3.37 us
    pallas_call x1, Pallas kernels, call_hidden(): pl.pallas_call(functools.partial(hidden_kernel, plan, len(pieces), shard)...  2.93 us
    pallas_call x1, Pallas kernels, call_grad(): pl.pallas_call(functools.partial(grad_kernel, plan, len(pieces), shard, s...  2.86 us
    ppermute x2, waiting for transfers between devices, over_y(): return (swap_y(value), [(not own, shard, at) for own, shard, at in parts])  2.76 us
  transfers between devices with their start and end apart: 13, of which 5 were waited for; matrix products, arithmetic and copies ran while one was open for 2% of the time, Pallas kernels for 8%

profile of v2, /device:TPU:29, one launch (start us, length us, event | category | flops | bytes accessed | tf_op | source)
XLA Modules:
  0.0 39.0 jit_solution(7813250666703550560)
XLA Ops:
  0.6 1.0 %constant_dynamic-slice_fusion = bf16[16,3072]{1,0:T(8,128)(2,1)S(1)} fusion(bf16[16,12288]{1,0:T(8,128)(2,1)} %refs_0_.3, s32[]{:T(128)S(6)} %select_n.30), kind=kLoop, calls=%fused_computation.8 | loop fusion | bytes 196612 | tf_op jit(solution)/shard_map/dynamic_slice | solution.py:193
  1.6 0.2 collective-permute-start.1
  1.8 0.1 collective-permute-start
  2.5 0.1 stack.39.place
  2.6 0.7 %pad_add_fusion.table = s32[2,96]{1,0:T(2,128)S(1)} fusion(s32[1,96]{1,0:T(1,128)} %param.10, s32[1,96]{1,0:T(1,128)} %param.9), kind=kLoop, calls=%fused_computation.7 | loop fusion | flops 192 | bytes 1536 | tf_op jit(solution)/shard_map/concatenate | solution.py:244
  3.3 1.8 %collective-permute-done.1 = bf16[16,3072]{1,0:T(8,128)(2,1)S(1)} collective-permute-done((bf16[16,3072]{1,0:T(8,128)(2,1)S(1)}, bf16[16,3072]{1,0:T(8,128)(2,1)S(1)}, u32[]{:S(2)}, u32[]{:S(2)}) %collective-permute-start.1) | collective-permute-done | bytes 98336 | tf_op jit(solution)/shard_map/ppermute | solution.py:163
  5.1 0.2 collective-permute-start.3
  5.3 3.1 %collective-permute-start.2 = (bf16[32,3072]{1,0:T(8,128)(2,1)S(1)}, bf16[32,3072]{1,0:T(8,128)(2,1)S(1)}, u32[]{:S(2)}, u32[]{:S(2)}) collective-permute-start(bf16[32,3072]{1,0:T(8,128)(2,1)S(1)} %pad_maximum_fusion.3), channel_id=1, source_target_pairs={{0,4},{4,8},{8,12},{12,0},{1,5},{5,9},{9,13},{13,1},{2,6},{6,10},{... | collective-permute-start | bytes 589832 | tf_op jit(solution)/shard_map/ppermute | solution.py:178
  8.4 0.7 %collective-permute-done = bf16[16,3072]{1,0:T(8,128)(2,1)S(1)} collective-permute-done((bf16[16,3072]{1,0:T(8,128)(2,1)S(1)}, bf16[16,3072]{1,0:T(8,128)(2,1)S(1)}, u32[]{:S(2)}, u32[]{:S(2)}) %collective-permute-start) | collective-permute-done | bytes 98336 | tf_op jit(solution)/shard_map/ppermute | solution.py:178
  9.1 3.7 %collective-permute-start.9 = (bf16[16,3072]{1,0:T(8,128)(2,1)S(1)}, bf16[16,3072]{1,0:T(8,128)(2,1)S(1)}, u32[]{:S(2)}, u32[]{:S(2)}) collective-permute-start(bf16[16,3072]{1,0:T(8,128)(2,1)S(1)} %collective-permute-done), channel_id=1, source_target_pairs={{0,16},{16,0},{1,17},{17,1},{2,18},{18,2},{3,19},{19,3},{4,20},{20... | collective-permute-start | bytes 294920 | tf_op jit(solution)/shard_map/ppermute | solution.py:163
  12.8 1.3 %collective-permute-start.4 = (bf16[32,3072]{1,0:T(8,128)(2,1)S(1)}, bf16[32,3072]{1,0:T(8,128)(2,1)S(1)}, u32[]{:S(2)}, u32[]{:S(2)}) collective-permute-start(bf16[32,3072]{1,0:T(8,128)(2,1)S(1)} %constant_dynamic-update-slice_fusion.refs_1_), channel_id=1, source_target_pairs={{0,2},{2,0},{1,3},{3,1},{4,6},{6,4},{5,7},{7,5},{8,10},{10,8},{9,1... | collective-permute-start | bytes 589832 | tf_op jit(solution)/shard_map/ppermute | solution.py:167
  14.1 1.0 %collective-permute-done.9 = bf16[16,3072]{1,0:T(8,128)(2,1)S(1)} collective-permute-done((bf16[16,3072]{1,0:T(8,128)(2,1)S(1)}, bf16[16,3072]{1,0:T(8,128)(2,1)S(1)}, u32[]{:S(2)}, u32[]{:S(2)}) %collective-permute-start.9) | collective-permute-done | bytes 98336 | tf_op jit(solution)/shard_map/ppermute | solution.py:163
  15.1 1.5 %collective-permute-start.12 = (bf16[64,3072]{1,0:T(8,128)(2,1)S(1)}, bf16[64,3072]{1,0:T(8,128)(2,1)S(1)}, u32[]{:S(2)}, u32[]{:S(2)}) collective-permute-start(bf16[64,3072]{1,0:T(8,128)(2,1)S(1)} %copy-done.2), channel_id=1, source_target_pairs={{0,16},{16,0},{1,17},{17,1},{2,18},{18,2},{3,19},{19,3},{4,20},{20... | collective-permute-start | bytes 1179656 | tf_op jit(solution)/shard_map/ppermute | solution.py:217
  16.6 0.0 collective-permute-done.3
  16.6 1.3 %collective-permute-start.6 = (bf16[16,3072]{1,0:T(8,128)(2,1)S(1)}, bf16[16,3072]{1,0:T(8,128)(2,1)S(1)}, u32[]{:S(2)}, u32[]{:S(2)}) collective-permute-start(bf16[16,3072]{1,0:T(8,128)(2,1)S(1)} %get-tuple-element.11.refs_3_), channel_id=1, source_target_pairs={{0,2},{2,0},{1,3},{3,1},{4,6},{6,4},{5,7},{7,5},{8,10},{10,8},{9,1... | collective-permute-start | bytes 294920 | tf_op jit(solution)/shard_map/ppermute | solution.py:167
  17.9 0.3 collective-permute-start.10
  18.2 1.2 %collective-permute-start.5 = (bf16[32,3072]{1,0:T(8,128)(2,1)S(1)}, bf16[32,3072]{1,0:T(8,128)(2,1)S(1)}, u32[]{:S(2)}, u32[]{:S(2)}) collective-permute-start(bf16[32,3072]{1,0:T(8,128)(2,1)S(1)} %collective-permute-done.2.refs_2_), channel_id=1, source_target_pairs={{0,2},{2,0},{1,3},{3,1},{4,6},{6,4},{5,7},{7,5},{8,10},{10,8},{9,1... | collective-permute-start | bytes 589832 | tf_op jit(solution)/shard_map/ppermute | solution.py:167
  19.5 4.1 %collective-permute-start.7 = (bf16[64,3072]{1,0:T(8,128)(2,1)S(1)}, bf16[64,3072]{1,0:T(8,128)(2,1)S(1)}, u32[]{:S(2)}, u32[]{:S(2)}) collective-permute-start(bf16[64,3072]{1,0:T(8,128)(2,1)S(1)} %pad_maximum_fusion.1), channel_id=1, source_target_pairs={{0,1},{1,0},{2,3},{3,2},{4,5},{5,4},{6,7},{7,6},{8,9},{9,8},{10,11... | collective-permute-start | bytes 1179656 | tf_op jit(solution)/shard_map/ppermute | solution.py:172
  23.6 4.9 %collective-permute-done.5.refs_5_ = bf16[32,3072]{1,0:T(8,128)(2,1)S(1)} collective-permute-done((bf16[32,3072]{1,0:T(8,128)(2,1)S(1)}, bf16[32,3072]{1,0:T(8,128)(2,1)S(1)}, u32[]{:S(2)}, u32[]{:S(2)}) %collective-permute-start.5) | collective-permute-done | bytes 196640 | tf_op jit(solution)/shard_map/ppermute | solution.py:167
  28.5 3.0 %collective-permute-start.8 = (bf16[96,3072]{1,0:T(8,128)(2,1)S(1)}, bf16[96,3072]{1,0:T(8,128)(2,1)S(1)}, u32[]{:S(2)}, u32[]{:S(2)}) collective-permute-start(bf16[96,3072]{1,0:T(8,128)(2,1)S(1)} %pad_maximum_fusion), channel_id=1, source_target_pairs={{0,1},{1,0},{2,3},{3,2},{4,5},{5,4},{6,7},{7,6},{8,9},{9,8},{10,11... | collective-permute-start | bytes 1769480 | tf_op jit(solution)/shard_map/ppermute | solution.py:172
  31.6 0.1 collective-permute-start.11
  31.7 1.5 %collective-permute-done.8.refs_8_ = bf16[96,3072]{1,0:T(8,128)(2,1)S(1)} collective-permute-done((bf16[96,3072]{1,0:T(8,128)(2,1)S(1)}, bf16[96,3072]{1,0:T(8,128)(2,1)S(1)}, u32[]{:S(2)}, u32[]{:S(2)}) %collective-permute-start.8) | collective-permute-done | bytes 589856 | tf_op jit(solution)/shard_map/ppermute | solution.py:172
  33.2 2.9 %hidden.1 = bf16[64,3072]{1,0:T(8,128)(2,1)} custom-call(s32[2,96]{1,0:T(2,128)S(1)} %pad_add_fusion.table, s32[10]{0:T(128)S(1)} %stack.39.place, bf16[16,12288]{1,0:T(8,128)(2,1)S(1)} %copy-done.1, bf16[32,3072]{1,0:T(8,128)(2,1)S(1)} %constant_dynamic-update-slice_fusion.refs_1_, bf16[32,3072]{1,0:T(8,128)(2,1)S(1)} %collective-permute-done.2.refs_2_, ...), custom_call_target="tpu_custom_call" | custom-call | flops 201326592 | bytes 5111808 | tf_op jit(solution)/shard_map/hidden/pallas_call | solution.py:106
  36.1 2.9 %grad.1 = bf16[48,128,128]{2,1,0:T(8,128)(2,1)} custom-call(s32[2,96]{1,0:T(2,128)S(1)} %pad_add_fusion.table, s32[10]{0:T(128)S(1)} %stack.39.place, bf16[16,12288]{1,0:T(8,128)(2,1)S(1)} %copy-done.1, bf16[32,3072]{1,0:T(8,128)(2,1)S(1)} %constant_dynamic-update-slice_fusion.refs_1_, bf16[32,3072]{1,0:T(8,128)(2,1)S(1)} %collective-permute-done.2.refs_2_, ...), custom_call_target="tpu_custom_call" | custom-call | flops 201326592 | bytes 5505024 | tf_op jit(solution)/shard_map/grad/pallas_call | solution.py:133
  (21 shorter events, 0.2 us)
Async XLA Ops:
  0.6 14.5 %copy-start.2 = (bf16[64,3072]{1,0:T(8,128)(2,1)S(1)}, bf16[64,3072]{1,0:T(8,128)(2,1)}, u32[]{:S(2)}) copy-start(bf16[64,3072]{1,0:T(8,128)(2,1)} %refs_12_.1) | copy-start | bytes 1179652
  1.6 3.5 %collective-permute-start.1 = (bf16[16,3072]{1,0:T(8,128)(2,1)S(1)}, bf16[16,3072]{1,0:T(8,128)(2,1)S(1)}, u32[]{:S(2)}, u32[]{:S(2)}) collective-permute-start(bf16[16,3072]{1,0:T(8,128)(2,1)S(1)} %constant_dynamic-slice_fusion), channel_id=1, source_target_pairs={{0,16},{16,0},{1,17},{17,1},{2,18},{18,2},{3,19},{19,3},{4,20},{20... | collective-permute-start | bytes 294920 | tf_op jit(solution)/shard_map/ppermute | solution.py:163
  1.8 7.3 %collective-permute-start = (bf16[16,3072]{1,0:T(8,128)(2,1)S(1)}, bf16[16,3072]{1,0:T(8,128)(2,1)S(1)}, u32[]{:S(2)}, u32[]{:S(2)}) collective-permute-start(bf16[16,3072]{1,0:T(8,128)(2,1)S(1)} %constant_dynamic-slice_fusion), channel_id=1, source_target_pairs={{0,8},{4,12},{8,0},{12,4},{1,9},{5,13},{9,1},{13,5},{2,10},{6,14},... | collective-permute-start | bytes 294920 | tf_op jit(solution)/shard_map/ppermute | solution.py:178
  5.1 11.5 %collective-permute-start.3 = (bf16[32,3072]{1,0:T(8,128)(2,1)S(1)}, bf16[32,3072]{1,0:T(8,128)(2,1)S(1)}, u32[]{:S(2)}, u32[]{:S(2)}) collective-permute-start(bf16[32,3072]{1,0:T(8,128)(2,1)S(1)} %pad_maximum_fusion.3), channel_id=1, source_target_pairs={{0,12},{4,0},{8,4},{12,8},{1,13},{5,1},{9,5},{13,9},{2,14},{6,2},{... | collective-permute-start | bytes 589832 | tf_op jit(solution)/shard_map/ppermute | solution.py:178
  5.3 12.9 %collective-permute-start.2 = (bf16[32,3072]{1,0:T(8,128)(2,1)S(1)}, bf16[32,3072]{1,0:T(8,128)(2,1)S(1)}, u32[]{:S(2)}, u32[]{:S(2)}) collective-permute-start(bf16[32,3072]{1,0:T(8,128)(2,1)S(1)} %pad_maximum_fusion.3), channel_id=1, source_target_pairs={{0,4},{4,8},{8,12},{12,0},{1,5},{5,9},{9,13},{13,1},{2,6},{6,10},{... | collective-permute-start | bytes 589832 | tf_op jit(solution)/shard_map/ppermute | solution.py:178
  9.1 6.0 %collective-permute-start.9 = (bf16[16,3072]{1,0:T(8,128)(2,1)S(1)}, bf16[16,3072]{1,0:T(8,128)(2,1)S(1)}, u32[]{:S(2)}, u32[]{:S(2)}) collective-permute-start(bf16[16,3072]{1,0:T(8,128)(2,1)S(1)} %collective-permute-done), channel_id=1, source_target_pairs={{0,16},{16,0},{1,17},{17,1},{2,18},{18,2},{3,19},{19,3},{4,20},{20... | collective-permute-start | bytes 294920 | tf_op jit(solution)/shard_map/ppermute | solution.py:163
  12.8 6.6 %collective-permute-start.4 = (bf16[32,3072]{1,0:T(8,128)(2,1)S(1)}, bf16[32,3072]{1,0:T(8,128)(2,1)S(1)}, u32[]{:S(2)}, u32[]{:S(2)}) collective-permute-start(bf16[32,3072]{1,0:T(8,128)(2,1)S(1)} %constant_dynamic-update-slice_fusion.refs_1_), channel_id=1, source_target_pairs={{0,2},{2,0},{1,3},{3,1},{4,6},{6,4},{5,7},{7,5},{8,10},{10,8},{9,1... | collective-permute-start | bytes 589832 | tf_op jit(solution)/shard_map/ppermute | solution.py:167
  15.1 21.0 %collective-permute-start.12 = (bf16[64,3072]{1,0:T(8,128)(2,1)S(1)}, bf16[64,3072]{1,0:T(8,128)(2,1)S(1)}, u32[]{:S(2)}, u32[]{:S(2)}) collective-permute-start(bf16[64,3072]{1,0:T(8,128)(2,1)S(1)} %copy-done.2), channel_id=1, source_target_pairs={{0,16},{16,0},{1,17},{17,1},{2,18},{18,2},{3,19},{19,3},{4,20},{20... | collective-permute-start | bytes 1179656 | tf_op jit(solution)/shard_map/ppermute | solution.py:217
  16.6 16.6 %copy-start.1 = (bf16[16,12288]{1,0:T(8,128)(2,1)S(1)}, bf16[16,12288]{1,0:T(8,128)(2,1)}, u32[]{:S(2)}) copy-start(bf16[16,12288]{1,0:T(8,128)(2,1)} %refs_0_.3) | copy-start | bytes 1179652
  16.6 7.0 %collective-permute-start.6 = (bf16[16,3072]{1,0:T(8,128)(2,1)S(1)}, bf16[16,3072]{1,0:T(8,128)(2,1)S(1)}, u32[]{:S(2)}, u32[]{:S(2)}) collective-permute-start(bf16[16,3072]{1,0:T(8,128)(2,1)S(1)} %get-tuple-element.11.refs_3_), channel_id=1, source_target_pairs={{0,2},{2,0},{1,3},{3,1},{4,6},{6,4},{5,7},{7,5},{8,10},{10,8},{9,1... | collective-permute-start | bytes 294920 | tf_op jit(solution)/shard_map/ppermute | solution.py:167
  17.9 15.3 %copy-start = (bf16[1,96,128,128]{3,2,1,0:T(8,128)(2,1)S(1)}, bf16[1,96,128,128]{3,2,1,0:T(8,128)(2,1)}, u32[]{:S(2)}) copy-start(bf16[1,96,128,128]{3,2,1,0:T(8,128)(2,1)} %param.8) | copy-start | bytes 9437188
  17.9 13.6 %collective-permute-start.10 = (bf16[32,3072]{1,0:T(8,128)(2,1)S(1)}, bf16[32,3072]{1,0:T(8,128)(2,1)S(1)}, u32[]{:S(2)}, u32[]{:S(2)}) collective-permute-start(bf16[32,3072]{1,0:T(8,128)(2,1)S(1)} %pad_maximum_fusion.4.refs_9_), channel_id=1, source_target_pairs={{0,2},{2,0},{1,3},{3,1},{4,6},{6,4},{5,7},{7,5},{8,10},{10,8},{9,1... | collective-permute-start | bytes 589832 | tf_op jit(solution)/shard_map/ppermute | solution.py:167
  18.2 10.2 %collective-permute-start.5 = (bf16[32,3072]{1,0:T(8,128)(2,1)S(1)}, bf16[32,3072]{1,0:T(8,128)(2,1)S(1)}, u32[]{:S(2)}, u32[]{:S(2)}) collective-permute-start(bf16[32,3072]{1,0:T(8,128)(2,1)S(1)} %collective-permute-done.2.refs_2_), channel_id=1, source_target_pairs={{0,2},{2,0},{1,3},{3,1},{4,6},{6,4},{5,7},{7,5},{8,10},{10,8},{9,1... | collective-permute-start | bytes 589832 | tf_op jit(solution)/shard_map/ppermute | solution.py:167
  19.5 12.2 %collective-permute-start.7 = (bf16[64,3072]{1,0:T(8,128)(2,1)S(1)}, bf16[64,3072]{1,0:T(8,128)(2,1)S(1)}, u32[]{:S(2)}, u32[]{:S(2)}) collective-permute-start(bf16[64,3072]{1,0:T(8,128)(2,1)S(1)} %pad_maximum_fusion.1), channel_id=1, source_target_pairs={{0,1},{1,0},{2,3},{3,2},{4,5},{5,4},{6,7},{7,6},{8,9},{9,8},{10,11... | collective-permute-start | bytes 1179656 | tf_op jit(solution)/shard_map/ppermute | solution.py:172
  28.5 4.7 %collective-permute-start.8 = (bf16[96,3072]{1,0:T(8,128)(2,1)S(1)}, bf16[96,3072]{1,0:T(8,128)(2,1)S(1)}, u32[]{:S(2)}, u32[]{:S(2)}) collective-permute-start(bf16[96,3072]{1,0:T(8,128)(2,1)S(1)} %pad_maximum_fusion), channel_id=1, source_target_pairs={{0,1},{1,0},{2,3},{3,2},{4,5},{5,4},{6,7},{7,6},{8,9},{9,8},{10,11... | collective-permute-start | bytes 1769480 | tf_op jit(solution)/shard_map/ppermute | solution.py:172
  31.6 4.6 %collective-permute-start.11 = (bf16[64,3072]{1,0:T(8,128)(2,1)S(1)}, bf16[64,3072]{1,0:T(8,128)(2,1)S(1)}, u32[]{:S(2)}, u32[]{:S(2)}) collective-permute-start(bf16[64,3072]{1,0:T(8,128)(2,1)S(1)} %pad_maximum_fusion.2), channel_id=1, source_target_pairs={{0,1},{1,0},{2,3},{3,2},{4,5},{5,4},{6,7},{7,6},{8,9},{9,8},{10,11... | collective-permute-start | bytes 1179656 | tf_op jit(solution)/shard_map/ppermute | solution.py:172

commit v3 on v2

v3 whole, which is shorter than its diff:
```python
import functools

import jax
import jax.numpy as jnp
from jax import lax
from jax.experimental import pallas as pl
from jax.experimental.pallas import tpu as pltpu
from jax.sharding import PartitionSpec as P

UNROLL = 24
OUT_PARTS = 2
VMEM_LIMIT = 24 << 20


def block_kernel(plan, n_pieces, n_cots, shard, scale, table, place, *refs):
    pieces, cots = refs[:n_pieces], refs[n_pieces : n_pieces + n_cots]
    w, hid_hbm, grad_hbm, tok, cot, acc, hid, grad, sem = refs[n_pieces + n_cots :]
    capacity, side = w.shape[0], w.shape[1]
    col_blocks, group = acc.shape[0], acc.shape[1]
    slots = grad.shape[0]
    live, slot0 = place[place.shape[0] - 2], place[place.shape[0] - 1]
    acc[...] = jnp.zeros_like(acc)
    for operand, first, rows, row0, at in plan:
        src = pieces[operand]
        if at is None:
            tok[row0 : row0 + rows, :] = src[first : first + rows, :]
        else:
            lane = pl.multiple_of(place[at], 128)
            tok[row0 : row0 + rows, pl.ds(lane, src.shape[1])] = src[first : first + rows, :]
    for g, src in enumerate(cots):
        for i in range(group // shard):
            at = g * group + i * shard
            cot[at : at + shard, :] = src[pl.ds(pl.multiple_of(place[i], 16), shard), :]

    def grad_step(step, carry):
        base = step * UNROLL
        for u in range(UNROLL):
            k = slot0 + base + u
            lane = pl.multiple_of(table[0, k] * side, side)
            col = pl.multiple_of(table[1, k] * side, side)
            product = lax.dot_general(
                tok[:, pl.ds(lane, side)],
                cot[:, pl.ds(col, side)],
                (((0,), (0,)), ((), ())),
                preferred_element_type=jnp.float32,
            )
            grad[base + u] = jnp.where(k < live, product * scale, 0.0).astype(grad.dtype)
        return carry

    def hidden_step(step, carry):
        base = step * UNROLL
        products = []
        for u in range(UNROLL):
            k = base + u
            lane = pl.multiple_of(table[0, k] * side, side)
            product = jnp.dot(tok[0:group, pl.ds(lane, side)], w[k], preferred_element_type=jnp.float32)
            products.append(jnp.where(k < live, product, 0.0))
        for u in range(UNROLL):
            col = table[1, base + u]
            acc[col] = acc[col] + products[u]
        return carry

    per_part = slots // OUT_PARTS
    copies = []
    for i in range(OUT_PARTS):
        lax.fori_loop(i * per_part // UNROLL, (i + 1) * per_part // UNROLL, grad_step, 0)
        part = pl.ds(i * per_part, per_part)
        copies.append(pltpu.make_async_copy(grad.at[part], grad_hbm.at[part], sem.at[i]))
        copies[-1].start()
    lax.fori_loop(0, capacity // UNROLL, hidden_step, 0)
    for j in range(col_blocks):
        for i in range(group // shard):
            row0 = pl.multiple_of(place[i], 16)
            hid[pl.ds(row0, shard), j * side : (j + 1) * side] = acc[j, i * shard : (i + 1) * shard, :].astype(hid.dtype)
    copies.append(pltpu.make_async_copy(hid, hid_hbm, sem.at[OUT_PARTS]))
    copies[-1].start()
    for copy in copies:
        copy.wait()


def call_blocks(table, place, pieces, plan, weights, cots, slots, width, shard, scale):
    capacity, side, _ = weights.shape
    group, ff_dev = cots[0].shape
    total = group * len(cots)
    cost = pl.CostEstimate(
        flops=2 * side * side * (group * capacity + total * slots),
        bytes_accessed=2 * (weights.size + slots * side * side + total * (width + ff_dev) + group * ff_dev),
        transcendentals=0,
    )
    return pl.pallas_call(
        functools.partial(block_kernel, plan, len(pieces), len(cots), shard, scale),
        out_shape=(
            jax.ShapeDtypeStruct((group, ff_dev), jnp.bfloat16),
            jax.ShapeDtypeStruct((slots, side, side), jnp.bfloat16),
        ),
        in_specs=[pl.BlockSpec(memory_space=pltpu.SMEM)] * 2
        + [pl.BlockSpec(memory_space=pltpu.VMEM)] * (len(pieces) + len(cots) + 1),
        out_specs=(pl.BlockSpec(memory_space=pltpu.HBM),) * 2,
        scratch_shapes=[
            pltpu.VMEM((total, width), jnp.bfloat16),
            pltpu.VMEM((total, ff_dev), jnp.bfloat16),
            pltpu.VMEM((ff_dev // side, group, side), jnp.float32),
            pltpu.VMEM((group, ff_dev), jnp.bfloat16),
            pltpu.VMEM((slots, side, side), jnp.bfloat16),
            pltpu.SemaphoreType.DMA((OUT_PARTS + 1,)),
        ],
        compiler_params=pltpu.CompilerParams(vmem_limit_bytes=VMEM_LIMIT),
        cost_estimate=cost,
        name="blocks",
    )(table, place, *pieces, *cots, weights)


def two_group_plan(table, count, tokens, cotangent, weights, scale):
    tok_dev, width = tokens.shape
    quarter = width // 4
    group, ff_dev = cotangent.shape
    capacity, side, _ = weights.shape
    slots = capacity // 2
    row, col = lax.axis_index("row"), lax.axis_index("col")
    x, core = col // 2, col % 2
    swap_y = functools.partial(lax.ppermute, axis_name="dp", perm=[(0, 1), (1, 0)])

    def over_y(bundle):
        value, parts = bundle
        return swap_y(value), [(not own, shard, at) for own, shard, at in parts]

    def over_x(bundle):
        value, parts = bundle
        moved = lax.ppermute(value, "col", [(0, 2), (2, 0), (1, 3), (3, 1)])
        return moved, [(own, shard, at ^ 1) for own, shard, at in parts]

    def over_core(bundle):
        value, parts = bundle
        moved = lax.ppermute(value, "col", [(0, 1), (1, 0), (2, 3), (3, 2)])
        return moved, [(own, shard, at ^ 2) for own, shard, at in parts]

    def over_z(bundle, shard):
        value, parts = bundle
        by = (0, 1, 3, 2)[shard]
        moved = lax.ppermute(value, "row", [(i, (i + by) % 4) for i in range(4)])
        return moved, [(own, shard, at) for own, _, at in parts]

    def join(*bundles):
        return jnp.concatenate([v for v, _ in bundles], 0), [p for _, parts in bundles for p in parts]

    def cut(bundle, i, j):
        return bundle[0][i * tok_dev : j * tok_dev], bundle[1][i:j]

    def after(bundle, *earlier):
        return lax.optimization_barrier((bundle[0], [e[0] for e in earlier]))[0], bundle[1]

    place = [((row + 4 - by) % 4) * tok_dev for by in (0, 1, 3, 2)]
    place += [(xx * 2 + cc) * quarter for xx, cc in ((x, core), (1 - x, core), (x, 1 - core), (1 - x, 1 - core))]
    place = jnp.stack(place + [count, lax.axis_index("dp") * slots]).astype(jnp.int32)
    mine = lax.dynamic_slice_in_dim(tokens, col * quarter, quarter, 1)

    mine = (mine, [(True, 0, 0)])
    other0 = over_y(mine)
    own3 = over_z(mine, 3)
    both = join(mine, other0)
    both1 = over_z(both, 1)
    both2 = over_z(both, 2)
    other3 = over_y(own3)
    cot_other = swap_y(after((cotangent, None), other3)[0])
    own2, other2 = cut(both2, 0, 1), cut(both2, 1, 2)
    first = join(own3, other0)
    first_x = over_x(first)
    both1_x = over_x(both1)
    own2_x = over_x(own2)
    last = join(other3, other2)
    last_x = over_x(after(last, both1))
    near = join(first, both1)
    settled, (table, place) = lax.optimization_barrier((near[0], (table, place)))
    core_a = over_core((settled, near[1]))
    core_b = over_core(join(first_x, both1_x, own2, own2_x))
    core_c = over_core(join(last, last_x))
    got = [first, both1, own2, first_x, both1_x, own2_x, core_a, core_b, last, last_x, core_c]
    pieces, plan = [tokens], [(0, 0, tok_dev, 0, None)]
    for value, parts in got:
        for i, (own, shard, at) in enumerate(parts):
            plan.append((len(pieces), i * tok_dev, tok_dev, (0 if own else group) + shard * tok_dev, 4 + at))
        pieces.append(value)
    assert len(plan) == 29
    return call_blocks(
        table, place, pieces, plan, weights, [cotangent, cot_other], slots, width, tok_dev, scale
    )


def on_device(tokens, cotangent, weight_blocks, block_rows, block_cols, block_count):
    groups, steps = lax.axis_size("dp"), lax.axis_size("row")
    tok_dev, width = tokens.shape
    group, ff_dev = cotangent.shape
    weights = weight_blocks[0]
    capacity, side, _ = weights.shape
    scale = 1.0 / (group * groups) ** 0.5
    table, count = jnp.concatenate([block_rows, block_cols], 0), block_count[0]
    if (groups, steps, lax.axis_size("col")) == (2, 4, 4):
        hidden, grad = two_group_plan(table, count, tokens, cotangent, weights, scale)
        return hidden, grad[None]
    gathered = lax.all_gather(tokens, "row", axis=0, tiled=True)
    zero = jnp.zeros((), jnp.int32)
    place = jnp.stack([zero, count, zero])
    plan = [(0, 0, group, 0, None)]
    hidden, partial = call_blocks(table, place, [gathered], plan, weights, [cotangent], capacity, width, group, scale)
    return hidden, lax.psum_scatter(partial[None], "dp", scatter_dimension=1, tiled=True)


def solution(mesh):
    in_specs = (
        P(("dp", "row"), None),
        P("dp", ("row", "col")),
        P(("row", "col"), None, None, None),
        P(("row", "col"), None),
        P(("row", "col"), None),
        P(("row", "col")),
    )
    out_specs = (P("dp", ("row", "col")), P(("row", "col"), "dp", None, None))
    return jax.shard_map(
        on_device, mesh=mesh, in_specs=in_specs, out_specs=out_specs, check_vma=False
    )
```

time: 39.2 us -> 37.3 us (0.952)
  waiting for transfers between devices: 9.88 us -> 5.52 us
  starting transfers between devices: 20 us -> 24.1 us
  Pallas kernels: 5.79 us -> 4.25 us
    ppermute x4, waiting for transfers between devices: 4.89 us -> 0.68 us  [over_x(): moved = lax.ppermute(value, 'col', [(0, 2), (2, 0), (1, 3), (3, 1)])]
    ppermute x3, starting transfers between devices: 7.23 us -> 11.2 us  [over_core(): moved = lax.ppermute(value, 'col', [(0, 1), (1, 0), (2, 3), (3, 2)])]
    pallas_call x2 -> x1, Pallas kernels: 5.79 us -> 4.25 us  [call_blocks(): pl.pallas_call(functools.partial(block_kernel, plan, len(pieces), len(cot...]
  transfers between devices with their start and end apart: 13 -> 13, of which waited for: 5 -> 5; matrix products, arithmetic and copies ran while one was open for 2% -> 2% of each run, Pallas kernels for 8% -> 0%
where the time goes in v3:
time: 37.3 us; the launch traced here: 37.1 us
  starting transfers between devices  24.1 us (65%)
  waiting for transfers between devices  5.52 us (15%)
  Pallas kernels  4.25 us (11%)
  between operations  1.34 us (4%)
  local copies, waits for them, and re-layouts  1.08 us (3%)
  other arithmetic  0.81 us (2%)
    ppermute x3, starting transfers between devices, over_core(): moved = lax.ppermute(value, 'col', [(0, 1), (1, 0), (2, 3), (3, 2)])  11.2 us
    pallas_call x1, Pallas kernels, call_blocks(): pl.pallas_call(functools.partial(block_kernel, plan, len(pieces), len(cot...  4.25 us
    ppermute x4, starting transfers between devices, over_x(): moved = lax.ppermute(value, 'col', [(0, 2), (2, 0), (1, 3), (3, 1)])  4.15 us
    ppermute x2, starting transfers between devices, over_y(): return (swap_y(value), [(not own, shard, at) for own, shard, at in parts])  3.9 us
    ppermute x3, starting transfers between devices, over_z(): moved = lax.ppermute(value, 'row', [(i, (i + by) % 4) for i in range(4)])  3.37 us
    ppermute x2, waiting for transfers between devices, over_y(): return (swap_y(value), [(not own, shard, at) for own, shard, at in parts])  2.76 us
    ppermute x1, starting transfers between devices, two_group_plan(): cot_other = swap_y(after((cotangent, None), other3)[0])  1.46 us
    ppermute x3, waiting for transfers between devices, over_core(): moved = lax.ppermute(value, 'col', [(0, 1), (1, 0), (2, 3), (3, 2)])  1.35 us
  transfers between devices with their start and end apart: 13, of which 5 were waited for; matrix products, arithmetic and copies ran while one was open for 2% of the time, Pallas kernels for 0%

profile of v3, /device:TPU:29, one launch (start us, length us, event | category | flops | bytes accessed | tf_op | source)
XLA Modules:
  0.0 37.1 jit_solution(12264360762924173215)
XLA Ops:
  0.6 1.0 %constant_dynamic-slice_fusion = bf16[16,3072]{1,0:T(8,128)(2,1)S(1)} fusion(bf16[16,12288]{1,0:T(8,128)(2,1)} %refs_0_.1, s32[]{:T(128)S(6)} %select_n.30), kind=kLoop, calls=%fused_computation.8 | loop fusion | bytes 196612 | tf_op jit(solution)/shard_map/dynamic_slice | solution.py:155
  1.6 0.2 collective-permute-start.1
  1.8 0.1 collective-permute-start
  2.5 0.1 stack.39.place
  2.6 0.7 %pad_add_fusion.table = s32[2,96]{1,0:T(2,128)S(1)} fusion(s32[1,96]{1,0:T(1,128)} %param.10, s32[1,96]{1,0:T(1,128)} %param.9), kind=kLoop, calls=%fused_computation.7 | loop fusion | flops 192 | bytes 1536 | tf_op jit(solution)/shard_map/concatenate | solution.py:196
  3.3 1.8 %collective-permute-done.1 = bf16[16,3072]{1,0:T(8,128)(2,1)S(1)} collective-permute-done((bf16[16,3072]{1,0:T(8,128)(2,1)S(1)}, bf16[16,3072]{1,0:T(8,128)(2,1)S(1)}, u32[]{:S(2)}, u32[]{:S(2)}) %collective-permute-start.1) | collective-permute-done | bytes 98336 | tf_op jit(solution)/shard_map/ppermute | solution.py:125
  5.1 0.2 collective-permute-start.3
  5.3 3.1 %collective-permute-start.2 = (bf16[32,3072]{1,0:T(8,128)(2,1)S(1)}, bf16[32,3072]{1,0:T(8,128)(2,1)S(1)}, u32[]{:S(2)}, u32[]{:S(2)}) collective-permute-start(bf16[32,3072]{1,0:T(8,128)(2,1)S(1)} %pad_maximum_fusion.3), channel_id=1, source_target_pairs={{0,4},{4,8},{8,12},{12,0},{1,5},{5,9},{9,13},{13,1},{2,6},{6,10},{... | collective-permute-start | bytes 589832 | tf_op jit(solution)/shard_map/ppermute | solution.py:140
  8.4 0.7 %collective-permute-done = bf16[16,3072]{1,0:T(8,128)(2,1)S(1)} collective-permute-done((bf16[16,3072]{1,0:T(8,128)(2,1)S(1)}, bf16[16,3072]{1,0:T(8,128)(2,1)S(1)}, u32[]{:S(2)}, u32[]{:S(2)}) %collective-permute-start) | collective-permute-done | bytes 98336 | tf_op jit(solution)/shard_map/ppermute | solution.py:140
  9.1 3.7 %collective-permute-start.9 = (bf16[16,3072]{1,0:T(8,128)(2,1)S(1)}, bf16[16,3072]{1,0:T(8,128)(2,1)S(1)}, u32[]{:S(2)}, u32[]{:S(2)}) collective-permute-start(bf16[16,3072]{1,0:T(8,128)(2,1)S(1)} %collective-permute-done), channel_id=1, source_target_pairs={{0,16},{16,0},{1,17},{17,1},{2,18},{18,2},{3,19},{19,3},{4,20},{20... | collective-permute-start | bytes 294920 | tf_op jit(solution)/shard_map/ppermute | solution.py:125
  12.8 1.3 %collective-permute-start.4 = (bf16[32,3072]{1,0:T(8,128)(2,1)S(1)}, bf16[32,3072]{1,0:T(8,128)(2,1)S(1)}, u32[]{:S(2)}, u32[]{:S(2)}) collective-permute-start(bf16[32,3072]{1,0:T(8,128)(2,1)S(1)} %constant_dynamic-update-slice_fusion.refs_1_), channel_id=1, source_target_pairs={{0,2},{2,0},{1,3},{3,1},{4,6},{6,4},{5,7},{7,5},{8,10},{10,8},{9,1... | collective-permute-start | bytes 589832 | tf_op jit(solution)/shard_map/ppermute | solution.py:129
  14.1 1.0 %collective-permute-done.9 = bf16[16,3072]{1,0:T(8,128)(2,1)S(1)} collective-permute-done((bf16[16,3072]{1,0:T(8,128)(2,1)S(1)}, bf16[16,3072]{1,0:T(8,128)(2,1)S(1)}, u32[]{:S(2)}, u32[]{:S(2)}) %collective-permute-start.9) | collective-permute-done | bytes 98336 | tf_op jit(solution)/shard_map/ppermute | solution.py:125
  15.1 1.5 %collective-permute-start.12 = (bf16[64,3072]{1,0:T(8,128)(2,1)S(1)}, bf16[64,3072]{1,0:T(8,128)(2,1)S(1)}, u32[]{:S(2)}, u32[]{:S(2)}) collective-permute-start(bf16[64,3072]{1,0:T(8,128)(2,1)S(1)} %copy-done.2), channel_id=1, source_target_pairs={{0,16},{16,0},{1,17},{17,1},{2,18},{18,2},{3,19},{19,3},{4,20},{20... | collective-permute-start | bytes 1179656 | tf_op jit(solution)/shard_map/ppermute | solution.py:164
  16.6 1.3 %collective-permute-start.6 = (bf16[16,3072]{1,0:T(8,128)(2,1)S(1)}, bf16[16,3072]{1,0:T(8,128)(2,1)S(1)}, u32[]{:S(2)}, u32[]{:S(2)}) collective-permute-start(bf16[16,3072]{1,0:T(8,128)(2,1)S(1)} %get-tuple-element.17.refs_3_), channel_id=1, source_target_pairs={{0,2},{2,0},{1,3},{3,1},{4,6},{6,4},{5,7},{7,5},{8,10},{10,8},{9,1... | collective-permute-start | bytes 294920 | tf_op jit(solution)/shard_map/ppermute | solution.py:129
  17.9 0.9 %collective-permute-start.5 = (bf16[32,3072]{1,0:T(8,128)(2,1)S(1)}, bf16[32,3072]{1,0:T(8,128)(2,1)S(1)}, u32[]{:S(2)}, u32[]{:S(2)}) collective-permute-start(bf16[32,3072]{1,0:T(8,128)(2,1)S(1)} %collective-permute-done.2.refs_2_), channel_id=1, source_target_pairs={{0,2},{2,0},{1,3},{3,1},{4,6},{6,4},{5,7},{7,5},{8,10},{10,8},{9,1... | collective-permute-start | bytes 589832 | tf_op jit(solution)/shard_map/ppermute | solution.py:129
  18.9 0.7 %collective-permute-start.10 = (bf16[32,3072]{1,0:T(8,128)(2,1)S(1)}, bf16[32,3072]{1,0:T(8,128)(2,1)S(1)}, u32[]{:S(2)}, u32[]{:S(2)}) collective-permute-start(bf16[32,3072]{1,0:T(8,128)(2,1)S(1)} %pad_maximum_fusion.4.refs_9_), channel_id=1, source_target_pairs={{0,2},{2,0},{1,3},{3,1},{4,6},{6,4},{5,7},{7,5},{8,10},{10,8},{9,1... | collective-permute-start | bytes 589832 | tf_op jit(solution)/shard_map/ppermute | solution.py:129
  19.5 0.0 collective-permute-done.4.refs_4_
  19.5 4.0 %collective-permute-start.7 = (bf16[64,3072]{1,0:T(8,128)(2,1)S(1)}, bf16[64,3072]{1,0:T(8,128)(2,1)S(1)}, u32[]{:S(2)}, u32[]{:S(2)}) collective-permute-start(bf16[64,3072]{1,0:T(8,128)(2,1)S(1)} %pad_maximum_fusion.1), channel_id=1, source_target_pairs={{0,1},{1,0},{2,3},{3,2},{4,5},{5,4},{6,7},{7,6},{8,9},{9,8},{10,11... | collective-permute-start | bytes 1179656 | tf_op jit(solution)/shard_map/ppermute | solution.py:134
  23.5 0.0 collective-permute-done.6.refs_6_
  23.5 0.7 %collective-permute-done.5.refs_5_ = bf16[32,3072]{1,0:T(8,128)(2,1)S(1)} collective-permute-done((bf16[32,3072]{1,0:T(8,128)(2,1)S(1)}, bf16[32,3072]{1,0:T(8,128)(2,1)S(1)}, u32[]{:S(2)}, u32[]{:S(2)}) %collective-permute-start.5) | collective-permute-done | bytes 196640 | tf_op jit(solution)/shard_map/ppermute | solution.py:129
  24.3 5.2 %collective-permute-start.8 = (bf16[96,3072]{1,0:T(8,128)(2,1)S(1)}, bf16[96,3072]{1,0:T(8,128)(2,1)S(1)}, u32[]{:S(2)}, u32[]{:S(2)}) collective-permute-start(bf16[96,3072]{1,0:T(8,128)(2,1)S(1)} %pad_maximum_fusion), channel_id=1, source_target_pairs={{0,1},{1,0},{2,3},{3,2},{4,5},{5,4},{6,7},{7,6},{8,9},{9,8},{10,11... | collective-permute-start | bytes 1769480 | tf_op jit(solution)/shard_map/ppermute | solution.py:134
  29.4 2.1 %collective-permute-start.11 = (bf16[64,3072]{1,0:T(8,128)(2,1)S(1)}, bf16[64,3072]{1,0:T(8,128)(2,1)S(1)}, u32[]{:S(2)}, u32[]{:S(2)}) collective-permute-start(bf16[64,3072]{1,0:T(8,128)(2,1)S(1)} %pad_maximum_fusion.2), channel_id=1, source_target_pairs={{0,1},{1,0},{2,3},{3,2},{4,5},{5,4},{6,7},{7,6},{8,9},{9,8},{10,11... | collective-permute-start | bytes 1179656 | tf_op jit(solution)/shard_map/ppermute | solution.py:134
  31.5 1.3 %collective-permute-done.11.refs_11_ = bf16[64,3072]{1,0:T(8,128)(2,1)S(1)} collective-permute-done((bf16[64,3072]{1,0:T(8,128)(2,1)S(1)}, bf16[64,3072]{1,0:T(8,128)(2,1)S(1)}, u32[]{:S(2)}, u32[]{:S(2)}) %collective-permute-start.11) | collective-permute-done | bytes 393248 | tf_op jit(solution)/shard_map/ppermute | solution.py:134
  32.9 4.3 %blocks.1 = (bf16[64,3072]{1,0:T(8,128)(2,1)}, bf16[48,128,128]{2,1,0:T(8,128)(2,1)}) custom-call(s32[2,96]{1,0:T(2,128)S(1)} %pad_add_fusion.table, s32[10]{0:T(128)S(1)} %stack.39.place, bf16[16,12288]{1,0:T(8,128)(2,1)S(1)} %copy-done.1, bf16[32,3072]{1,0:T(8,128)(2,1)S(1)} %constant_dynamic-update-slice_fusion.refs_1_, ...), custom_call_target="tpu_custom_call" | custom-call | flops 402653184 | bytes 9043968 | tf_op jit(solution)/shard_map/blocks/pallas_call | solution.py:90
  (20 shorter events, 0.2 us)
Async XLA Ops:
  0.6 14.5 %copy-start.2 = (bf16[64,3072]{1,0:T(8,128)(2,1)S(1)}, bf16[64,3072]{1,0:T(8,128)(2,1)}, u32[]{:S(2)}) copy-start(bf16[64,3072]{1,0:T(8,128)(2,1)} %refs_12_.1) | copy-start | bytes 1179652
  1.6 3.5 %collective-permute-start.1 = (bf16[16,3072]{1,0:T(8,128)(2,1)S(1)}, bf16[16,3072]{1,0:T(8,128)(2,1)S(1)}, u32[]{:S(2)}, u32[]{:S(2)}) collective-permute-start(bf16[16,3072]{1,0:T(8,128)(2,1)S(1)} %constant_dynamic-slice_fusion), channel_id=1, source_target_pairs={{0,16},{16,0},{1,17},{17,1},{2,18},{18,2},{3,19},{19,3},{4,20},{20... | collective-permute-start | bytes 294920 | tf_op jit(solution)/shard_map/ppermute | solution.py:125
  1.8 7.3 %collective-permute-start = (bf16[16,3072]{1,0:T(8,128)(2,1)S(1)}, bf16[16,3072]{1,0:T(8,128)(2,1)S(1)}, u32[]{:S(2)}, u32[]{:S(2)}) collective-permute-start(bf16[16,3072]{1,0:T(8,128)(2,1)S(1)} %constant_dynamic-slice_fusion), channel_id=1, source_target_pairs={{0,8},{4,12},{8,0},{12,4},{1,9},{5,13},{9,1},{13,5},{2,10},{6,14},... | collective-permute-start | bytes 294920 | tf_op jit(solution)/shard_map/ppermute | solution.py:140
  5.1 11.5 %collective-permute-start.3 = (bf16[32,3072]{1,0:T(8,128)(2,1)S(1)}, bf16[32,3072]{1,0:T(8,128)(2,1)S(1)}, u32[]{:S(2)}, u32[]{:S(2)}) collective-permute-start(bf16[32,3072]{1,0:T(8,128)(2,1)S(1)} %pad_maximum_fusion.3), channel_id=1, source_target_pairs={{0,12},{4,0},{8,4},{12,8},{1,13},{5,1},{9,5},{13,9},{2,14},{6,2},{... | collective-permute-start | bytes 589832 | tf_op jit(solution)/shard_map/ppermute | solution.py:140
  5.3 12.6 %collective-permute-start.2 = (bf16[32,3072]{1,0:T(8,128)(2,1)S(1)}, bf16[32,3072]{1,0:T(8,128)(2,1)S(1)}, u32[]{:S(2)}, u32[]{:S(2)}) collective-permute-start(bf16[32,3072]{1,0:T(8,128)(2,1)S(1)} %pad_maximum_fusion.3), channel_id=1, source_target_pairs={{0,4},{4,8},{8,12},{12,0},{1,5},{5,9},{9,13},{13,1},{2,6},{6,10},{... | collective-permute-start | bytes 589832 | tf_op jit(solution)/shard_map/ppermute | solution.py:140
  9.1 6.0 %collective-permute-start.9 = (bf16[16,3072]{1,0:T(8,128)(2,1)S(1)}, bf16[16,3072]{1,0:T(8,128)(2,1)S(1)}, u32[]{:S(2)}, u32[]{:S(2)}) collective-permute-start(bf16[16,3072]{1,0:T(8,128)(2,1)S(1)} %collective-permute-done), channel_id=1, source_target_pairs={{0,16},{16,0},{1,17},{17,1},{2,18},{18,2},{3,19},{19,3},{4,20},{20... | collective-permute-start | bytes 294920 | tf_op jit(solution)/shard_map/ppermute | solution.py:125
  12.8 6.7 %collective-permute-start.4 = (bf16[32,3072]{1,0:T(8,128)(2,1)S(1)}, bf16[32,3072]{1,0:T(8,128)(2,1)S(1)}, u32[]{:S(2)}, u32[]{:S(2)}) collective-permute-start(bf16[32,3072]{1,0:T(8,128)(2,1)S(1)} %constant_dynamic-update-slice_fusion.refs_1_), channel_id=1, source_target_pairs={{0,2},{2,0},{1,3},{3,1},{4,6},{6,4},{5,7},{7,5},{8,10},{10,8},{9,1... | collective-permute-start | bytes 589832 | tf_op jit(solution)/shard_map/ppermute | solution.py:129
  15.1 16.4 %collective-permute-start.12 = (bf16[64,3072]{1,0:T(8,128)(2,1)S(1)}, bf16[64,3072]{1,0:T(8,128)(2,1)S(1)}, u32[]{:S(2)}, u32[]{:S(2)}) collective-permute-start(bf16[64,3072]{1,0:T(8,128)(2,1)S(1)} %copy-done.2), channel_id=1, source_target_pairs={{0,16},{16,0},{1,17},{17,1},{2,18},{18,2},{3,19},{19,3},{4,20},{20... | collective-permute-start | bytes 1179656 | tf_op jit(solution)/shard_map/ppermute | solution.py:164
  16.6 16.3 %copy-start.1 = (bf16[16,12288]{1,0:T(8,128)(2,1)S(1)}, bf16[16,12288]{1,0:T(8,128)(2,1)}, u32[]{:S(2)}) copy-start(bf16[16,12288]{1,0:T(8,128)(2,1)} %refs_0_.1) | copy-start | bytes 1179652
  16.6 7.0 %collective-permute-start.6 = (bf16[16,3072]{1,0:T(8,128)(2,1)S(1)}, bf16[16,3072]{1,0:T(8,128)(2,1)S(1)}, u32[]{:S(2)}, u32[]{:S(2)}) collective-permute-start(bf16[16,3072]{1,0:T(8,128)(2,1)S(1)} %get-tuple-element.17.refs_3_), channel_id=1, source_target_pairs={{0,2},{2,0},{1,3},{3,1},{4,6},{6,4},{5,7},{7,5},{8,10},{10,8},{9,1... | collective-permute-start | bytes 294920 | tf_op jit(solution)/shard_map/ppermute | solution.py:129
  17.9 15.0 %copy-start = (bf16[1,96,128,128]{3,2,1,0:T(8,128)(2,1)S(1)}, bf16[1,96,128,128]{3,2,1,0:T(8,128)(2,1)}, u32[]{:S(2)}) copy-start(bf16[1,96,128,128]{3,2,1,0:T(8,128)(2,1)} %param.8) | copy-start | bytes 9437188
  17.9 6.3 %collective-permute-start.5 = (bf16[32,3072]{1,0:T(8,128)(2,1)S(1)}, bf16[32,3072]{1,0:T(8,128)(2,1)S(1)}, u32[]{:S(2)}, u32[]{:S(2)}) collective-permute-start(bf16[32,3072]{1,0:T(8,128)(2,1)S(1)} %collective-permute-done.2.refs_2_), channel_id=1, source_target_pairs={{0,2},{2,0},{1,3},{3,1},{4,6},{6,4},{5,7},{7,5},{8,10},{10,8},{9,1... | collective-permute-start | bytes 589832 | tf_op jit(solution)/shard_map/ppermute | solution.py:129
  18.9 10.6 %collective-permute-start.10 = (bf16[32,3072]{1,0:T(8,128)(2,1)S(1)}, bf16[32,3072]{1,0:T(8,128)(2,1)S(1)}, u32[]{:S(2)}, u32[]{:S(2)}) collective-permute-start(bf16[32,3072]{1,0:T(8,128)(2,1)S(1)} %pad_maximum_fusion.4.refs_9_), channel_id=1, source_target_pairs={{0,2},{2,0},{1,3},{3,1},{4,6},{6,4},{5,7},{7,5},{8,10},{10,8},{9,1... | collective-permute-start | bytes 589832 | tf_op jit(solution)/shard_map/ppermute | solution.py:129
  19.5 12.0 %collective-permute-start.7 = (bf16[64,3072]{1,0:T(8,128)(2,1)S(1)}, bf16[64,3072]{1,0:T(8,128)(2,1)S(1)}, u32[]{:S(2)}, u32[]{:S(2)}) collective-permute-start(bf16[64,3072]{1,0:T(8,128)(2,1)S(1)} %pad_maximum_fusion.1), channel_id=1, source_target_pairs={{0,1},{1,0},{2,3},{3,2},{4,5},{5,4},{6,7},{7,6},{8,9},{9,8},{10,11... | collective-permute-start | bytes 1179656 | tf_op jit(solution)/shard_map/ppermute | solution.py:134
  24.3 8.6 %collective-permute-start.8 = (bf16[96,3072]{1,0:T(8,128)(2,1)S(1)}, bf16[96,3072]{1,0:T(8,128)(2,1)S(1)}, u32[]{:S(2)}, u32[]{:S(2)}) collective-permute-start(bf16[96,3072]{1,0:T(8,128)(2,1)S(1)} %pad_maximum_fusion), channel_id=1, source_target_pairs={{0,1},{1,0},{2,3},{3,2},{4,5},{5,4},{6,7},{7,6},{8,9},{9,8},{10,11... | collective-permute-start | bytes 1769480 | tf_op jit(solution)/shard_map/ppermute | solution.py:134
  29.4 3.4 %collective-permute-start.11 = (bf16[64,3072]{1,0:T(8,128)(2,1)S(1)}, bf16[64,3072]{1,0:T(8,128)(2,1)S(1)}, u32[]{:S(2)}, u32[]{:S(2)}) collective-permute-start(bf16[64,3072]{1,0:T(8,128)(2,1)S(1)} %pad_maximum_fusion.2), channel_id=1, source_target_pairs={{0,1},{1,0},{2,3},{3,2},{4,5},{5,4},{6,7},{7,6},{8,9},{9,8},{10,11... | collective-permute-start | bytes 1179656 | tf_op jit(solution)/shard_map/ppermute | solution.py:134

commit v4 on v3

--- a/solution.py
+++ b/solution.py
@@ -7,8 +7,8 @@
 from jax.experimental.pallas import tpu as pltpu
 from jax.sharding import PartitionSpec as P
 
-UNROLL = 24
-OUT_PARTS = 2
+UNROLL = 48
+OUT_PARTS = 1
 VMEM_LIMIT = 24 << 20
 
 
@@ -168,13 +168,14 @@
     both1_x = over_x(both1)
     own2_x = over_x(own2)
     last = join(other3, other2)
-    last_x = over_x(after(last, both1))
+    other2_x = over_x(after(other2, both1))
+    other3_x = over_y(after(cut(first_x, 0, 1), both1, own2_x))
     near = join(first, both1)
     settled, (table, place) = lax.optimization_barrier((near[0], (table, place)))
     core_a = over_core((settled, near[1]))
     core_b = over_core(join(first_x, both1_x, own2, own2_x))
-    core_c = over_core(join(last, last_x))
-    got = [first, both1, own2, first_x, both1_x, own2_x, core_a, core_b, last, last_x, core_c]
+    core_c = over_core(join(last, other2_x, other3_x))
+    got = [first, both1, own2, first_x, both1_x, own2_x, core_a, core_b, last, other2_x, other3_x, core_c]
     pieces, plan = [tokens], [(0, 0, tok_dev, 0, None)]
     for value, parts in got:
         for i, (own, shard, at) in enumerate(parts):

time: 37.3 us -> 35.8 us (0.960)
  starting transfers between devices: 24.1 us -> 20.8 us
  waiting for transfers between devices: 5.52 us -> 7.58 us
    ppermute x3, starting transfers between devices: 11.2 us -> 7.96 us  [over_core(): moved = lax.ppermute(value, 'col', [(0, 1), (1, 0), (2, 3), (3, 2)])]
    ppermute x4, waiting for transfers between devices: 0.68 us -> 2.78 us  [over_x(): moved = lax.ppermute(value, 'col', [(0, 2), (2, 0), (1, 3), (3, 1)])]
    ppermute x2 -> x3, starting transfers between devices: 3.9 us -> 3.97 us  [over_y(): return (swap_y(value), [(not own, shard, at) for own, shard, at in parts])]
    ppermute x2 -> x3, waiting for transfers between devices: 2.76 us -> 2.76 us  [over_y(): return (swap_y(value), [(not own, shard, at) for own, shard, at in parts])]
  transfers between devices with their start and end apart: 13 -> 14, of which waited for: 5 -> 5; matrix products, arithmetic and copies ran while one was open for 2% -> 3% of each run, Pallas kernels for 0% -> 0%
where the time goes in v4:
time: 35.8 us; the launch traced here: 35.6 us
  starting transfers between devices  20.8 us (58%)
  waiting for transfers between devices  7.58 us (21%)
  Pallas kernels  3.97 us (11%)
  between operations  1.37 us (4%)
  local copies, waits for them, and re-layouts  1.09 us (3%)
  other arithmetic  0.81 us (2%)
    ppermute x3, starting transfers between devices, over_core(): moved = lax.ppermute(value, 'col', [(0, 1), (1, 0), (2, 3), (3, 2)])  7.96 us
    ppermute x4, starting transfers between devices, over_x(): moved = lax.ppermute(value, 'col', [(0, 2), (2, 0), (1, 3), (3, 1)])  4.02 us
    ppermute x3, starting transfers between devices, over_y(): return (swap_y(value), [(not own, shard, at) for own, shard, at in parts])  3.97 us
    pallas_call x1, Pallas kernels, call_blocks(): pl.pallas_call(functools.partial(block_kernel, plan, len(pieces), len(cot...  3.97 us
    ppermute x3, starting transfers between devices, over_z(): moved = lax.ppermute(value, 'row', [(i, (i + by) % 4) for i in range(4)])  3.37 us
    ppermute x4, waiting for transfers between devices, over_x(): moved = lax.ppermute(value, 'col', [(0, 2), (2, 0), (1, 3), (3, 1)])  2.78 us
    ppermute x3, waiting for transfers between devices, over_y(): return (swap_y(value), [(not own, shard, at) for own, shard, at in parts])  2.76 us
    ppermute x1, starting transfers between devices, two_group_plan(): cot_other = swap_y(after((cotangent, None), other3)[0])  1.46 us
  transfers between devices with their start and end apart: 14, of which 5 were waited for; matrix products, arithmetic and copies ran while one was open for 3% of the time, Pallas kernels for 0%

profile of v4, /device:TPU:29, one launch (start us, length us, event | category | flops | bytes accessed | tf_op | source)
XLA Modules:
  0.0 35.6 jit_solution(12316470663923495344)
XLA Ops:
  0.6 1.0 %constant_dynamic-slice_fusion = bf16[16,3072]{1,0:T(8,128)(2,1)S(1)} fusion(bf16[16,12288]{1,0:T(8,128)(2,1)} %refs_0_.1, s32[]{:T(128)S(6)} %select_n.30), kind=kLoop, calls=%fused_computation.8 | loop fusion | bytes 196612 | tf_op jit(solution)/shard_map/dynamic_slice | solution.py:155
  1.6 0.2 collective-permute-start.1
  1.8 0.1 collective-permute-start
  2.5 0.1 stack.39.place
  2.6 0.7 %pad_add_fusion.table = s32[2,96]{1,0:T(2,128)S(1)} fusion(s32[1,96]{1,0:T(1,128)} %param.10, s32[1,96]{1,0:T(1,128)} %param.9), kind=kLoop, calls=%fused_computation.7 | loop fusion | flops 192 | bytes 1536 | tf_op jit(solution)/shard_map/concatenate | solution.py:197
  3.3 1.8 %collective-permute-done.1 = bf16[16,3072]{1,0:T(8,128)(2,1)S(1)} collective-permute-done((bf16[16,3072]{1,0:T(8,128)(2,1)S(1)}, bf16[16,3072]{1,0:T(8,128)(2,1)S(1)}, u32[]{:S(2)}, u32[]{:S(2)}) %collective-permute-start.1) | collective-permute-done | bytes 98336 | tf_op jit(solution)/shard_map/ppermute | solution.py:125
  5.1 0.2 collective-permute-start.3
  5.3 3.1 %collective-permute-start.2 = (bf16[32,3072]{1,0:T(8,128)(2,1)S(1)}, bf16[32,3072]{1,0:T(8,128)(2,1)S(1)}, u32[]{:S(2)}, u32[]{:S(2)}) collective-permute-start(bf16[32,3072]{1,0:T(8,128)(2,1)S(1)} %pad_maximum_fusion.3), channel_id=1, source_target_pairs={{0,4},{4,8},{8,12},{12,0},{1,5},{5,9},{9,13},{13,1},{2,6},{6,10},{... | collective-permute-start | bytes 589832 | tf_op jit(solution)/shard_map/ppermute | solution.py:140
  8.4 0.7 %collective-permute-done = bf16[16,3072]{1,0:T(8,128)(2,1)S(1)} collective-permute-done((bf16[16,3072]{1,0:T(8,128)(2,1)S(1)}, bf16[16,3072]{1,0:T(8,128)(2,1)S(1)}, u32[]{:S(2)}, u32[]{:S(2)}) %collective-permute-start) | collective-permute-done | bytes 98336 | tf_op jit(solution)/shard_map/ppermute | solution.py:140
  9.1 3.7 %collective-permute-start.9 = (bf16[16,3072]{1,0:T(8,128)(2,1)S(1)}, bf16[16,3072]{1,0:T(8,128)(2,1)S(1)}, u32[]{:S(2)}, u32[]{:S(2)}) collective-permute-start(bf16[16,3072]{1,0:T(8,128)(2,1)S(1)} %collective-permute-done), channel_id=1, source_target_pairs={{0,16},{16,0},{1,17},{17,1},{2,18},{18,2},{3,19},{19,3},{4,20},{20... | collective-permute-start | bytes 294920 | tf_op jit(solution)/shard_map/ppermute | solution.py:125
  12.8 1.3 %collective-permute-start.4 = (bf16[32,3072]{1,0:T(8,128)(2,1)S(1)}, bf16[32,3072]{1,0:T(8,128)(2,1)S(1)}, u32[]{:S(2)}, u32[]{:S(2)}) collective-permute-start(bf16[32,3072]{1,0:T(8,128)(2,1)S(1)} %constant_dynamic-update-slice_fusion.refs_1_), channel_id=1, source_target_pairs={{0,2},{2,0},{1,3},{3,1},{4,6},{6,4},{5,7},{7,5},{8,10},{10,8},{9,1... | collective-permute-start | bytes 589832 | tf_op jit(solution)/shard_map/ppermute | solution.py:129
  14.1 1.0 %collective-permute-done.9 = bf16[16,3072]{1,0:T(8,128)(2,1)S(1)} collective-permute-done((bf16[16,3072]{1,0:T(8,128)(2,1)S(1)}, bf16[16,3072]{1,0:T(8,128)(2,1)S(1)}, u32[]{:S(2)}, u32[]{:S(2)}) %collective-permute-start.9) | collective-permute-done | bytes 98336 | tf_op jit(solution)/shard_map/ppermute | solution.py:125
  15.1 1.5 %collective-permute-start.13 = (bf16[64,3072]{1,0:T(8,128)(2,1)S(1)}, bf16[64,3072]{1,0:T(8,128)(2,1)S(1)}, u32[]{:S(2)}, u32[]{:S(2)}) collective-permute-start(bf16[64,3072]{1,0:T(8,128)(2,1)S(1)} %copy-done.2), channel_id=1, source_target_pairs={{0,16},{16,0},{1,17},{17,1},{2,18},{18,2},{3,19},{19,3},{4,20},{20... | collective-permute-start | bytes 1179656 | tf_op jit(solution)/shard_map/ppermute | solution.py:164
  16.6 1.3 %collective-permute-start.6 = (bf16[16,3072]{1,0:T(8,128)(2,1)S(1)}, bf16[16,3072]{1,0:T(8,128)(2,1)S(1)}, u32[]{:S(2)}, u32[]{:S(2)}) collective-permute-start(bf16[16,3072]{1,0:T(8,128)(2,1)S(1)} %get-tuple-element.19.refs_3_), channel_id=1, source_target_pairs={{0,2},{2,0},{1,3},{3,1},{4,6},{6,4},{5,7},{7,5},{8,10},{10,8},{9,1... | collective-permute-start | bytes 294920 | tf_op jit(solution)/shard_map/ppermute | solution.py:129
  17.9 0.9 %collective-permute-start.10 = (bf16[16,3072]{1,0:T(8,128)(2,1)S(1)}, bf16[16,3072]{1,0:T(8,128)(2,1)S(1)}, u32[]{:S(2)}, u32[]{:S(2)}) collective-permute-start(bf16[16,3072]{1,0:T(8,128)(2,1)S(1)} %get-tuple-element.13), channel_id=1, source_target_pairs={{0,2},{2,0},{1,3},{3,1},{4,6},{6,4},{5,7},{7,5},{8,10},{10,8},{9,1... | collective-permute-start | bytes 294920 | tf_op jit(solution)/shard_map/ppermute | solution.py:129
  18.7 0.6 %collective-permute-start.5 = (bf16[32,3072]{1,0:T(8,128)(2,1)S(1)}, bf16[32,3072]{1,0:T(8,128)(2,1)S(1)}, u32[]{:S(2)}, u32[]{:S(2)}) collective-permute-start(bf16[32,3072]{1,0:T(8,128)(2,1)S(1)} %collective-permute-done.2.refs_2_), channel_id=1, source_target_pairs={{0,2},{2,0},{1,3},{3,1},{4,6},{6,4},{5,7},{7,5},{8,10},{10,8},{9,1... | collective-permute-start | bytes 589832 | tf_op jit(solution)/shard_map/ppermute | solution.py:129
  19.4 0.0 collective-permute-done.4.refs_4_
  19.4 4.1 %collective-permute-start.7 = (bf16[64,3072]{1,0:T(8,128)(2,1)S(1)}, bf16[64,3072]{1,0:T(8,128)(2,1)S(1)}, u32[]{:S(2)}, u32[]{:S(2)}) collective-permute-start(bf16[64,3072]{1,0:T(8,128)(2,1)S(1)} %pad_maximum_fusion.1), channel_id=1, source_target_pairs={{0,1},{1,0},{2,3},{3,2},{4,5},{5,4},{6,7},{7,6},{8,9},{9,8},{10,11... | collective-permute-start | bytes 1179656 | tf_op jit(solution)/shard_map/ppermute | solution.py:134
  23.5 0.1 collective-permute-start.11
  23.6 2.8 %collective-permute-done.5.refs_5_ = bf16[32,3072]{1,0:T(8,128)(2,1)S(1)} collective-permute-done((bf16[32,3072]{1,0:T(8,128)(2,1)S(1)}, bf16[32,3072]{1,0:T(8,128)(2,1)S(1)}, u32[]{:S(2)}, u32[]{:S(2)}) %collective-permute-start.5) | collective-permute-done | bytes 196640 | tf_op jit(solution)/shard_map/ppermute | solution.py:129
  26.4 3.0 %collective-permute-start.8 = (bf16[96,3072]{1,0:T(8,128)(2,1)S(1)}, bf16[96,3072]{1,0:T(8,128)(2,1)S(1)}, u32[]{:S(2)}, u32[]{:S(2)}) collective-permute-start(bf16[96,3072]{1,0:T(8,128)(2,1)S(1)} %pad_maximum_fusion), channel_id=1, source_target_pairs={{0,1},{1,0},{2,3},{3,2},{4,5},{5,4},{6,7},{7,6},{8,9},{9,8},{10,11... | collective-permute-start | bytes 1769480 | tf_op jit(solution)/shard_map/ppermute | solution.py:134
  29.5 0.8 %collective-permute-start.12 = (bf16[64,3072]{1,0:T(8,128)(2,1)S(1)}, bf16[64,3072]{1,0:T(8,128)(2,1)S(1)}, u32[]{:S(2)}, u32[]{:S(2)}) collective-permute-start(bf16[64,3072]{1,0:T(8,128)(2,1)S(1)} %pad_maximum_fusion.2), channel_id=1, source_target_pairs={{0,1},{1,0},{2,3},{3,2},{4,5},{5,4},{6,7},{7,6},{8,9},{9,8},{10,11... | collective-permute-start | bytes 1179656 | tf_op jit(solution)/shard_map/ppermute | solution.py:134
  30.3 1.3 %collective-permute-done.12.refs_12_ = bf16[64,3072]{1,0:T(8,128)(2,1)S(1)} collective-permute-done((bf16[64,3072]{1,0:T(8,128)(2,1)S(1)}, bf16[64,3072]{1,0:T(8,128)(2,1)S(1)}, u32[]{:S(2)}, u32[]{:S(2)}) %collective-permute-start.12) | collective-permute-done | bytes 393248 | tf_op jit(solution)/shard_map/ppermute | solution.py:134
  31.6 4.0 %blocks.1 = (bf16[64,3072]{1,0:T(8,128)(2,1)}, bf16[48,128,128]{2,1,0:T(8,128)(2,1)}) custom-call(s32[2,96]{1,0:T(2,128)S(1)} %pad_add_fusion.table, s32[10]{0:T(128)S(1)} %stack.39.place, bf16[16,12288]{1,0:T(8,128)(2,1)S(1)} %copy-done.1, bf16[32,3072]{1,0:T(8,128)(2,1)S(1)} %constant_dynamic-update-slice_fusion.refs_1_, ...), custom_call_target="tpu_custom_call" | custom-call | flops 402653184 | bytes 9043968 | tf_op jit(solution)/shard_map/blocks/pallas_call | solution.py:90
  (23 shorter events, 0.2 us)
Async XLA Ops:
  0.6 14.5 %copy-start.2 = (bf16[64,3072]{1,0:T(8,128)(2,1)S(1)}, bf16[64,3072]{1,0:T(8,128)(2,1)}, u32[]{:S(2)}) copy-start(bf16[64,3072]{1,0:T(8,128)(2,1)} %refs_13_.1) | copy-start | bytes 1179652
  1.6 3.5 %collective-permute-start.1 = (bf16[16,3072]{1,0:T(8,128)(2,1)S(1)}, bf16[16,3072]{1,0:T(8,128)(2,1)S(1)}, u32[]{:S(2)}, u32[]{:S(2)}) collective-permute-start(bf16[16,3072]{1,0:T(8,128)(2,1)S(1)} %constant_dynamic-slice_fusion), channel_id=1, source_target_pairs={{0,16},{16,0},{1,17},{17,1},{2,18},{18,2},{3,19},{19,3},{4,20},{20... | collective-permute-start | bytes 294920 | tf_op jit(solution)/shard_map/ppermute | solution.py:125
  1.8 7.3 %collective-permute-start = (bf16[16,3072]{1,0:T(8,128)(2,1)S(1)}, bf16[16,3072]{1,0:T(8,128)(2,1)S(1)}, u32[]{:S(2)}, u32[]{:S(2)}) collective-permute-start(bf16[16,3072]{1,0:T(8,128)(2,1)S(1)} %constant_dynamic-slice_fusion), channel_id=1, source_target_pairs={{0,8},{4,12},{8,0},{12,4},{1,9},{5,13},{9,1},{13,5},{2,10},{6,14},... | collective-permute-start | bytes 294920 | tf_op jit(solution)/shard_map/ppermute | solution.py:140
  5.1 11.5 %collective-permute-start.3 = (bf16[32,3072]{1,0:T(8,128)(2,1)S(1)}, bf16[32,3072]{1,0:T(8,128)(2,1)S(1)}, u32[]{:S(2)}, u32[]{:S(2)}) collective-permute-start(bf16[32,3072]{1,0:T(8,128)(2,1)S(1)} %pad_maximum_fusion.3), channel_id=1, source_target_pairs={{0,12},{4,0},{8,4},{12,8},{1,13},{5,1},{9,5},{13,9},{2,14},{6,2},{... | collective-permute-start | bytes 589832 | tf_op jit(solution)/shard_map/ppermute | solution.py:140
  5.3 12.6 %collective-permute-start.2 = (bf16[32,3072]{1,0:T(8,128)(2,1)S(1)}, bf16[32,3072]{1,0:T(8,128)(2,1)S(1)}, u32[]{:S(2)}, u32[]{:S(2)}) collective-permute-start(bf16[32,3072]{1,0:T(8,128)(2,1)S(1)} %pad_maximum_fusion.3), channel_id=1, source_target_pairs={{0,4},{4,8},{8,12},{12,0},{1,5},{5,9},{9,13},{13,1},{2,6},{6,10},{... | collective-permute-start | bytes 589832 | tf_op jit(solution)/shard_map/ppermute | solution.py:140
  9.1 6.0 %collective-permute-start.9 = (bf16[16,3072]{1,0:T(8,128)(2,1)S(1)}, bf16[16,3072]{1,0:T(8,128)(2,1)S(1)}, u32[]{:S(2)}, u32[]{:S(2)}) collective-permute-start(bf16[16,3072]{1,0:T(8,128)(2,1)S(1)} %collective-permute-done), channel_id=1, source_target_pairs={{0,16},{16,0},{1,17},{17,1},{2,18},{18,2},{3,19},{19,3},{4,20},{20... | collective-permute-start | bytes 294920 | tf_op jit(solution)/shard_map/ppermute | solution.py:125
  12.8 6.6 %collective-permute-start.4 = (bf16[32,3072]{1,0:T(8,128)(2,1)S(1)}, bf16[32,3072]{1,0:T(8,128)(2,1)S(1)}, u32[]{:S(2)}, u32[]{:S(2)}) collective-permute-start(bf16[32,3072]{1,0:T(8,128)(2,1)S(1)} %constant_dynamic-update-slice_fusion.refs_1_), channel_id=1, source_target_pairs={{0,2},{2,0},{1,3},{3,1},{4,6},{6,4},{5,7},{7,5},{8,10},{10,8},{9,1... | collective-permute-start | bytes 589832 | tf_op jit(solution)/shard_map/ppermute | solution.py:129
  15.1 15.2 %collective-permute-start.13 = (bf16[64,3072]{1,0:T(8,128)(2,1)S(1)}, bf16[64,3072]{1,0:T(8,128)(2,1)S(1)}, u32[]{:S(2)}, u32[]{:S(2)}) collective-permute-start(bf16[64,3072]{1,0:T(8,128)(2,1)S(1)} %copy-done.2), channel_id=1, source_target_pairs={{0,16},{16,0},{1,17},{17,1},{2,18},{18,2},{3,19},{19,3},{4,20},{20... | collective-permute-start | bytes 1179656 | tf_op jit(solution)/shard_map/ppermute | solution.py:164
  16.6 15.1 %copy-start.1 = (bf16[16,12288]{1,0:T(8,128)(2,1)S(1)}, bf16[16,12288]{1,0:T(8,128)(2,1)}, u32[]{:S(2)}) copy-start(bf16[16,12288]{1,0:T(8,128)(2,1)} %refs_0_.1) | copy-start | bytes 1179652
  16.6 6.9 %collective-permute-start.6 = (bf16[16,3072]{1,0:T(8,128)(2,1)S(1)}, bf16[16,3072]{1,0:T(8,128)(2,1)S(1)}, u32[]{:S(2)}, u32[]{:S(2)}) collective-permute-start(bf16[16,3072]{1,0:T(8,128)(2,1)S(1)} %get-tuple-element.19.refs_3_), channel_id=1, source_target_pairs={{0,2},{2,0},{1,3},{3,1},{4,6},{6,4},{5,7},{7,5},{8,10},{10,8},{9,1... | collective-permute-start | bytes 294920 | tf_op jit(solution)/shard_map/ppermute | solution.py:129
  17.9 11.6 %collective-permute-start.10 = (bf16[16,3072]{1,0:T(8,128)(2,1)S(1)}, bf16[16,3072]{1,0:T(8,128)(2,1)S(1)}, u32[]{:S(2)}, u32[]{:S(2)}) collective-permute-start(bf16[16,3072]{1,0:T(8,128)(2,1)S(1)} %get-tuple-element.13), channel_id=1, source_target_pairs={{0,2},{2,0},{1,3},{3,1},{4,6},{6,4},{5,7},{7,5},{8,10},{10,8},{9,1... | collective-permute-start | bytes 294920 | tf_op jit(solution)/shard_map/ppermute | solution.py:129
  18.7 7.6 %collective-permute-start.5 = (bf16[32,3072]{1,0:T(8,128)(2,1)S(1)}, bf16[32,3072]{1,0:T(8,128)(2,1)S(1)}, u32[]{:S(2)}, u32[]{:S(2)}) collective-permute-start(bf16[32,3072]{1,0:T(8,128)(2,1)S(1)} %collective-permute-done.2.refs_2_), channel_id=1, source_target_pairs={{0,2},{2,0},{1,3},{3,1},{4,6},{6,4},{5,7},{7,5},{8,10},{10,8},{9,1... | collective-permute-start | bytes 589832 | tf_op jit(solution)/shard_map/ppermute | solution.py:129
  19.3 12.3 %copy-start = (bf16[1,96,128,128]{3,2,1,0:T(8,128)(2,1)S(1)}, bf16[1,96,128,128]{3,2,1,0:T(8,128)(2,1)}, u32[]{:S(2)}) copy-start(bf16[1,96,128,128]{3,2,1,0:T(8,128)(2,1)} %param.8) | copy-start | bytes 9437188
  19.4 10.9 %collective-permute-start.7 = (bf16[64,3072]{1,0:T(8,128)(2,1)S(1)}, bf16[64,3072]{1,0:T(8,128)(2,1)S(1)}, u32[]{:S(2)}, u32[]{:S(2)}) collective-permute-start(bf16[64,3072]{1,0:T(8,128)(2,1)S(1)} %pad_maximum_fusion.1), channel_id=1, source_target_pairs={{0,1},{1,0},{2,3},{3,2},{4,5},{5,4},{6,7},{7,6},{8,9},{9,8},{10,11... | collective-permute-start | bytes 1179656 | tf_op jit(solution)/shard_map/ppermute | solution.py:134
  23.5 5.9 %collective-permute-start.11 = (bf16[16,3072]{1,0:T(8,128)(2,1)S(1)}, bf16[16,3072]{1,0:T(8,128)(2,1)S(1)}, u32[]{:S(2)}, u32[]{:S(2)}) collective-permute-start(bf16[16,3072]{1,0:T(8,128)(2,1)S(1)} %slice.14), channel_id=1, source_target_pairs={{0,16},{16,0},{1,17},{17,1},{2,18},{18,2},{3,19},{19,3},{4,20},{20... | collective-permute-start | bytes 294920 | tf_op jit(solution)/shard_map/ppermute | solution.py:125
  26.4 5.3 %collective-permute-start.8 = (bf16[96,3072]{1,0:T(8,128)(2,1)S(1)}, bf16[96,3072]{1,0:T(8,128)(2,1)S(1)}, u32[]{:S(2)}, u32[]{:S(2)}) collective-permute-start(bf16[96,3072]{1,0:T(8,128)(2,1)S(1)} %pad_maximum_fusion), channel_id=1, source_target_pairs={{0,1},{1,0},{2,3},{3,2},{4,5},{5,4},{6,7},{7,6},{8,9},{9,8},{10,11... | collective-permute-start | bytes 1769480 | tf_op jit(solution)/shard_map/ppermute | solution.py:134
  29.5 2.2 %collective-permute-start.12 = (bf16[64,3072]{1,0:T(8,128)(2,1)S(1)}, bf16[64,3072]{1,0:T(8,128)(2,1)S(1)}, u32[]{:S(2)}, u32[]{:S(2)}) collective-permute-start(bf16[64,3072]{1,0:T(8,128)(2,1)S(1)} %pad_maximum_fusion.2), channel_id=1, source_target_pairs={{0,1},{1,0},{2,3},{3,2},{4,5},{5,4},{6,7},{7,6},{8,9},{9,8},{10,11... | collective-permute-start | bytes 1179656 | tf_op jit(solution)/shard_map/ppermute | solution.py:134

commit v5 on v4

--- a/solution.py
+++ b/solution.py
@@ -174,8 +174,9 @@
     settled, (table, place) = lax.optimization_barrier((near[0], (table, place)))
     core_a = over_core((settled, near[1]))
     core_b = over_core(join(first_x, both1_x, own2, own2_x))
-    core_c = over_core(join(last, other2_x, other3_x))
-    got = [first, both1, own2, first_x, both1_x, own2_x, core_a, core_b, last, other2_x, other3_x, core_c]
+    core_c = over_core(last)
+    core_d = over_core(join(other2_x, other3_x))
+    got = [first, both1, own2, first_x, both1_x, own2_x, core_a, core_b, last, other2_x, other3_x, core_c, core_d]
     pieces, plan = [tokens], [(0, 0, tok_dev, 0, None)]
     for value, parts in got:
         for i, (own, shard, at) in enumerate(parts):

time: 35.8 us -> 35.3 us (0.986)
  waiting for transfers between devices: 7.58 us -> 5.6 us
  starting transfers between devices: 20.8 us -> 22.1 us
    ppermute x4, waiting for transfers between devices: 2.78 us -> 0.98 us  [over_x(): moved = lax.ppermute(value, 'col', [(0, 2), (2, 0), (1, 3), (3, 1)])]
    ppermute x3 -> x4, starting transfers between devices: 7.96 us -> 8.64 us  [over_core(): moved = lax.ppermute(value, 'col', [(0, 1), (1, 0), (2, 3), (3, 2)])]
    ppermute x4, starting transfers between devices: 4.02 us -> 4.65 us  [over_x(): moved = lax.ppermute(value, 'col', [(0, 2), (2, 0), (1, 3), (3, 1)])]
    ppermute x3 -> x4, waiting for transfers between devices: 1.32 us -> 1.15 us  [over_core(): moved = lax.ppermute(value, 'col', [(0, 1), (1, 0), (2, 3), (3, 2)])]
  transfers between devices with their start and end apart: 14 -> 15, of which waited for: 5 -> 5; matrix products, arithmetic and copies ran while one was open for 3% -> 3% of each run, Pallas kernels for 0% -> 0%
where the time goes in v5:
time: 35.3 us; the launch traced here: 35 us
  starting transfers between devices  22.1 us (63%)
  waiting for transfers between devices  5.6 us (16%)
  Pallas kernels  3.99 us (11%)
  between operations  1.38 us (4%)
  local copies, waits for them, and re-layouts  1.09 us (3%)
  other arithmetic  0.8 us (2%)
    ppermute x4, starting transfers between devices, over_core(): moved = lax.ppermute(value, 'col', [(0, 1), (1, 0), (2, 3), (3, 2)])  8.64 us
    ppermute x4, starting transfers between devices, over_x(): moved = lax.ppermute(value, 'col', [(0, 2), (2, 0), (1, 3), (3, 1)])  4.65 us
    pallas_call x1, Pallas kernels, call_blocks(): pl.pallas_call(functools.partial(block_kernel, plan, len(pieces), len(cot...  3.99 us
    ppermute x3, starting transfers between devices, over_y(): return (swap_y(value), [(not own, shard, at) for own, shard, at in parts])  3.97 us
    ppermute x3, starting transfers between devices, over_z(): moved = lax.ppermute(value, 'row', [(i, (i + by) % 4) for i in range(4)])  3.37 us
    ppermute x3, waiting for transfers between devices, over_y(): return (swap_y(value), [(not own, shard, at) for own, shard, at in parts])  2.75 us
    ppermute x1, starting transfers between devices, two_group_plan(): cot_other = swap_y(after((cotangent, None), other3)[0])  1.46 us
    ppermute x4, waiting for transfers between devices, over_core(): moved = lax.ppermute(value, 'col', [(0, 1), (1, 0), (2, 3), (3, 2)])  1.15 us
  transfers between devices with their start and end apart: 15, of which 5 were waited for; matrix products, arithmetic and copies ran while one was open for 3% of the time, Pallas kernels for 0%

profile of v5, /device:TPU:29, one launch (start us, length us, event | category | flops | bytes accessed | tf_op | source)
XLA Modules:
  0.0 35.0 jit_solution(605484252107846719)
XLA Ops:
  0.6 1.0 %constant_dynamic-slice_fusion = bf16[16,3072]{1,0:T(8,128)(2,1)S(1)} fusion(bf16[16,12288]{1,0:T(8,128)(2,1)} %refs_0_.1, s32[]{:T(128)S(6)} %select_n.30), kind=kLoop, calls=%fused_computation.8 | loop fusion | bytes 196612 | tf_op jit(solution)/shard_map/dynamic_slice | solution.py:155
  1.6 0.2 collective-permute-start.1
  1.8 0.1 collective-permute-start
  2.5 0.1 stack.39.place
  2.6 0.7 %pad_add_fusion.table = s32[2,96]{1,0:T(2,128)S(1)} fusion(s32[1,96]{1,0:T(1,128)} %param.10, s32[1,96]{1,0:T(1,128)} %param.9), kind=kLoop, calls=%fused_computation.7 | loop fusion | flops 192 | bytes 1536 | tf_op jit(solution)/shard_map/concatenate | solution.py:198
  3.3 1.8 %collective-permute-done.1 = bf16[16,3072]{1,0:T(8,128)(2,1)S(1)} collective-permute-done((bf16[16,3072]{1,0:T(8,128)(2,1)S(1)}, bf16[16,3072]{1,0:T(8,128)(2,1)S(1)}, u32[]{:S(2)}, u32[]{:S(2)}) %collective-permute-start.1) | collective-permute-done | bytes 98336 | tf_op jit(solution)/shard_map/ppermute | solution.py:125
  5.1 0.2 collective-permute-start.3
  5.3 3.1 %collective-permute-start.2 = (bf16[32,3072]{1,0:T(8,128)(2,1)S(1)}, bf16[32,3072]{1,0:T(8,128)(2,1)S(1)}, u32[]{:S(2)}, u32[]{:S(2)}) collective-permute-start(bf16[32,3072]{1,0:T(8,128)(2,1)S(1)} %pad_maximum_fusion.2), channel_id=1, source_target_pairs={{0,4},{4,8},{8,12},{12,0},{1,5},{5,9},{9,13},{13,1},{2,6},{6,10},{... | collective-permute-start | bytes 589832 | tf_op jit(solution)/shard_map/ppermute | solution.py:140
  8.4 0.7 %collective-permute-done = bf16[16,3072]{1,0:T(8,128)(2,1)S(1)} collective-permute-done((bf16[16,3072]{1,0:T(8,128)(2,1)S(1)}, bf16[16,3072]{1,0:T(8,128)(2,1)S(1)}, u32[]{:S(2)}, u32[]{:S(2)}) %collective-permute-start) | collective-permute-done | bytes 98336 | tf_op jit(solution)/shard_map/ppermute | solution.py:140
  9.1 3.7 %collective-permute-start.9 = (bf16[16,3072]{1,0:T(8,128)(2,1)S(1)}, bf16[16,3072]{1,0:T(8,128)(2,1)S(1)}, u32[]{:S(2)}, u32[]{:S(2)}) collective-permute-start(bf16[16,3072]{1,0:T(8,128)(2,1)S(1)} %collective-permute-done), channel_id=1, source_target_pairs={{0,16},{16,0},{1,17},{17,1},{2,18},{18,2},{3,19},{19,3},{4,20},{20... | collective-permute-start | bytes 294920 | tf_op jit(solution)/shard_map/ppermute | solution.py:125
  12.8 1.3 %collective-permute-start.4 = (bf16[32,3072]{1,0:T(8,128)(2,1)S(1)}, bf16[32,3072]{1,0:T(8,128)(2,1)S(1)}, u32[]{:S(2)}, u32[]{:S(2)}) collective-permute-start(bf16[32,3072]{1,0:T(8,128)(2,1)S(1)} %constant_dynamic-update-slice_fusion.refs_1_), channel_id=1, source_target_pairs={{0,2},{2,0},{1,3},{3,1},{4,6},{6,4},{5,7},{7,5},{8,10},{10,8},{9,1... | collective-permute-start | bytes 589832 | tf_op jit(solution)/shard_map/ppermute | solution.py:129
  14.1 1.0 %collective-permute-done.9 = bf16[16,3072]{1,0:T(8,128)(2,1)S(1)} collective-permute-done((bf16[16,3072]{1,0:T(8,128)(2,1)S(1)}, bf16[16,3072]{1,0:T(8,128)(2,1)S(1)}, u32[]{:S(2)}, u32[]{:S(2)}) %collective-permute-start.9) | collective-permute-done | bytes 98336 | tf_op jit(solution)/shard_map/ppermute | solution.py:125
  15.1 1.5 %collective-permute-start.14 = (bf16[64,3072]{1,0:T(8,128)(2,1)S(1)}, bf16[64,3072]{1,0:T(8,128)(2,1)S(1)}, u32[]{:S(2)}, u32[]{:S(2)}) collective-permute-start(bf16[64,3072]{1,0:T(8,128)(2,1)S(1)} %copy-done.2), channel_id=1, source_target_pairs={{0,16},{16,0},{1,17},{17,1},{2,18},{18,2},{3,19},{19,3},{4,20},{20... | collective-permute-start | bytes 1179656 | tf_op jit(solution)/shard_map/ppermute | solution.py:164
  16.6 1.3 %collective-permute-start.6 = (bf16[16,3072]{1,0:T(8,128)(2,1)S(1)}, bf16[16,3072]{1,0:T(8,128)(2,1)S(1)}, u32[]{:S(2)}, u32[]{:S(2)}) collective-permute-start(bf16[16,3072]{1,0:T(8,128)(2,1)S(1)} %get-tuple-element.19.refs_3_), channel_id=1, source_target_pairs={{0,2},{2,0},{1,3},{3,1},{4,6},{6,4},{5,7},{7,5},{8,10},{10,8},{9,1... | collective-permute-start | bytes 294920 | tf_op jit(solution)/shard_map/ppermute | solution.py:129
  17.9 0.9 %collective-permute-start.5 = (bf16[32,3072]{1,0:T(8,128)(2,1)S(1)}, bf16[32,3072]{1,0:T(8,128)(2,1)S(1)}, u32[]{:S(2)}, u32[]{:S(2)}) collective-permute-start(bf16[32,3072]{1,0:T(8,128)(2,1)S(1)} %collective-permute-done.2.refs_2_), channel_id=1, source_target_pairs={{0,2},{2,0},{1,3},{3,1},{4,6},{6,4},{5,7},{7,5},{8,10},{10,8},{9,1... | collective-permute-start | bytes 589832 | tf_op jit(solution)/shard_map/ppermute | solution.py:129
  18.8 3.2 %collective-permute-start.12 = (bf16[32,3072]{1,0:T(8,128)(2,1)S(1)}, bf16[32,3072]{1,0:T(8,128)(2,1)S(1)}, u32[]{:S(2)}, u32[]{:S(2)}) collective-permute-start(bf16[32,3072]{1,0:T(8,128)(2,1)S(1)} %pad_maximum_fusion.3.refs_9_), channel_id=1, source_target_pairs={{0,1},{1,0},{2,3},{3,2},{4,5},{5,4},{6,7},{7,6},{8,9},{9,8},{10,11... | collective-permute-start | bytes 589832 | tf_op jit(solution)/shard_map/ppermute | solution.py:134
  21.9 1.2 %collective-permute-start.10 = (bf16[16,3072]{1,0:T(8,128)(2,1)S(1)}, bf16[16,3072]{1,0:T(8,128)(2,1)S(1)}, u32[]{:S(2)}, u32[]{:S(2)}) collective-permute-start(bf16[16,3072]{1,0:T(8,128)(2,1)S(1)} %get-tuple-element.13), channel_id=1, source_target_pairs={{0,2},{2,0},{1,3},{3,1},{4,6},{6,4},{5,7},{7,5},{8,10},{10,8},{9,1... | collective-permute-start | bytes 294920 | tf_op jit(solution)/shard_map/ppermute | solution.py:129
  23.2 0.1 collective-permute-start.11
  23.3 1.0 %collective-permute-done.5.refs_5_ = bf16[32,3072]{1,0:T(8,128)(2,1)S(1)} collective-permute-done((bf16[32,3072]{1,0:T(8,128)(2,1)S(1)}, bf16[32,3072]{1,0:T(8,128)(2,1)S(1)}, u32[]{:S(2)}, u32[]{:S(2)}) %collective-permute-start.5) | collective-permute-done | bytes 196640 | tf_op jit(solution)/shard_map/ppermute | solution.py:129
  24.3 4.1 %collective-permute-start.8 = (bf16[96,3072]{1,0:T(8,128)(2,1)S(1)}, bf16[96,3072]{1,0:T(8,128)(2,1)S(1)}, u32[]{:S(2)}, u32[]{:S(2)}) collective-permute-start(bf16[96,3072]{1,0:T(8,128)(2,1)S(1)} %pad_maximum_fusion), channel_id=1, source_target_pairs={{0,1},{1,0},{2,3},{3,2},{4,5},{5,4},{6,7},{7,6},{8,9},{9,8},{10,11... | collective-permute-start | bytes 1769480 | tf_op jit(solution)/shard_map/ppermute | solution.py:134
  28.4 0.9 %collective-permute-start.7 = (bf16[64,3072]{1,0:T(8,128)(2,1)S(1)}, bf16[64,3072]{1,0:T(8,128)(2,1)S(1)}, u32[]{:S(2)}, u32[]{:S(2)}) collective-permute-start(bf16[64,3072]{1,0:T(8,128)(2,1)S(1)} %pad_maximum_fusion.1), channel_id=1, source_target_pairs={{0,1},{1,0},{2,3},{3,2},{4,5},{5,4},{6,7},{7,6},{8,9},{9,8},{10,11... | collective-permute-start | bytes 1179656 | tf_op jit(solution)/shard_map/ppermute | solution.py:134
  29.3 0.5 %collective-permute-start.13 = (bf16[32,3072]{1,0:T(8,128)(2,1)S(1)}, bf16[32,3072]{1,0:T(8,128)(2,1)S(1)}, u32[]{:S(2)}, u32[]{:S(2)}) collective-permute-start(bf16[32,3072]{1,0:T(8,128)(2,1)S(1)} %pad_maximum_fusion.4), channel_id=1, source_target_pairs={{0,1},{1,0},{2,3},{3,2},{4,5},{5,4},{6,7},{7,6},{8,9},{9,8},{10,11... | collective-permute-start | bytes 589832 | tf_op jit(solution)/shard_map/ppermute | solution.py:134
  29.8 1.1 %collective-permute-done.13.refs_13_ = bf16[32,3072]{1,0:T(8,128)(2,1)S(1)} collective-permute-done((bf16[32,3072]{1,0:T(8,128)(2,1)S(1)}, bf16[32,3072]{1,0:T(8,128)(2,1)S(1)}, u32[]{:S(2)}, u32[]{:S(2)}) %collective-permute-start.13) | collective-permute-done | bytes 196640 | tf_op jit(solution)/shard_map/ppermute | solution.py:134
  31.0 4.0 %blocks.1 = (bf16[64,3072]{1,0:T(8,128)(2,1)}, bf16[48,128,128]{2,1,0:T(8,128)(2,1)}) custom-call(s32[2,96]{1,0:T(2,128)S(1)} %pad_add_fusion.table, s32[10]{0:T(128)S(1)} %stack.39.place, bf16[16,12288]{1,0:T(8,128)(2,1)S(1)} %copy-done.1, bf16[32,3072]{1,0:T(8,128)(2,1)S(1)} %constant_dynamic-update-slice_fusion.refs_1_, ...), custom_call_target="tpu_custom_call" | custom-call | flops 402653184 | bytes 9043968 | tf_op jit(solution)/shard_map/blocks/pallas_call | solution.py:90
  (25 shorter events, 0.2 us)
Async XLA Ops:
  0.6 14.5 %copy-start.2 = (bf16[64,3072]{1,0:T(8,128)(2,1)S(1)}, bf16[64,3072]{1,0:T(8,128)(2,1)}, u32[]{:S(2)}) copy-start(bf16[64,3072]{1,0:T(8,128)(2,1)} %refs_14_.1) | copy-start | bytes 1179652
  1.6 3.5 %collective-permute-start.1 = (bf16[16,3072]{1,0:T(8,128)(2,1)S(1)}, bf16[16,3072]{1,0:T(8,128)(2,1)S(1)}, u32[]{:S(2)}, u32[]{:S(2)}) collective-permute-start(bf16[16,3072]{1,0:T(8,128)(2,1)S(1)} %constant_dynamic-slice_fusion), channel_id=1, source_target_pairs={{0,16},{16,0},{1,17},{17,1},{2,18},{18,2},{3,19},{19,3},{4,20},{20... | collective-permute-start | bytes 294920 | tf_op jit(solution)/shard_map/ppermute | solution.py:125
  1.8 7.3 %collective-permute-start = (bf16[16,3072]{1,0:T(8,128)(2,1)S(1)}, bf16[16,3072]{1,0:T(8,128)(2,1)S(1)}, u32[]{:S(2)}, u32[]{:S(2)}) collective-permute-start(bf16[16,3072]{1,0:T(8,128)(2,1)S(1)} %constant_dynamic-slice_fusion), channel_id=1, source_target_pairs={{0,8},{4,12},{8,0},{12,4},{1,9},{5,13},{9,1},{13,5},{2,10},{6,14},... | collective-permute-start | bytes 294920 | tf_op jit(solution)/shard_map/ppermute | solution.py:140
  5.1 11.5 %collective-permute-start.3 = (bf16[32,3072]{1,0:T(8,128)(2,1)S(1)}, bf16[32,3072]{1,0:T(8,128)(2,1)S(1)}, u32[]{:S(2)}, u32[]{:S(2)}) collective-permute-start(bf16[32,3072]{1,0:T(8,128)(2,1)S(1)} %pad_maximum_fusion.2), channel_id=1, source_target_pairs={{0,12},{4,0},{8,4},{12,8},{1,13},{5,1},{9,5},{13,9},{2,14},{6,2},{... | collective-permute-start | bytes 589832 | tf_op jit(solution)/shard_map/ppermute | solution.py:140
  5.3 12.6 %collective-permute-start.2 = (bf16[32,3072]{1,0:T(8,128)(2,1)S(1)}, bf16[32,3072]{1,0:T(8,128)(2,1)S(1)}, u32[]{:S(2)}, u32[]{:S(2)}) collective-permute-start(bf16[32,3072]{1,0:T(8,128)(2,1)S(1)} %pad_maximum_fusion.2), channel_id=1, source_target_pairs={{0,4},{4,8},{8,12},{12,0},{1,5},{5,9},{9,13},{13,1},{2,6},{6,10},{... | collective-permute-start | bytes 589832 | tf_op jit(solution)/shard_map/ppermute | solution.py:140
  9.1 6.0 %collective-permute-start.9 = (bf16[16,3072]{1,0:T(8,128)(2,1)S(1)}, bf16[16,3072]{1,0:T(8,128)(2,1)S(1)}, u32[]{:S(2)}, u32[]{:S(2)}) collective-permute-start(bf16[16,3072]{1,0:T(8,128)(2,1)S(1)} %collective-permute-done), channel_id=1, source_target_pairs={{0,16},{16,0},{1,17},{17,1},{2,18},{18,2},{3,19},{19,3},{4,20},{20... | collective-permute-start | bytes 294920 | tf_op jit(solution)/shard_map/ppermute | solution.py:125
  12.8 18.2 %copy-start.1 = (bf16[16,12288]{1,0:T(8,128)(2,1)S(1)}, bf16[16,12288]{1,0:T(8,128)(2,1)}, u32[]{:S(2)}) copy-start(bf16[16,12288]{1,0:T(8,128)(2,1)} %refs_0_.1) | copy-start | bytes 1179652
  12.8 9.1 %collective-permute-start.4 = (bf16[32,3072]{1,0:T(8,128)(2,1)S(1)}, bf16[32,3072]{1,0:T(8,128)(2,1)S(1)}, u32[]{:S(2)}, u32[]{:S(2)}) collective-permute-start(bf16[32,3072]{1,0:T(8,128)(2,1)S(1)} %constant_dynamic-update-slice_fusion.refs_1_), channel_id=1, source_target_pairs={{0,2},{2,0},{1,3},{3,1},{4,6},{6,4},{5,7},{7,5},{8,10},{10,8},{9,1... | collective-permute-start | bytes 589832 | tf_op jit(solution)/shard_map/ppermute | solution.py:129
  15.1 14.7 %collective-permute-start.14 = (bf16[64,3072]{1,0:T(8,128)(2,1)S(1)}, bf16[64,3072]{1,0:T(8,128)(2,1)S(1)}, u32[]{:S(2)}, u32[]{:S(2)}) collective-permute-start(bf16[64,3072]{1,0:T(8,128)(2,1)S(1)} %copy-done.2), channel_id=1, source_target_pairs={{0,16},{16,0},{1,17},{17,1},{2,18},{18,2},{3,19},{19,3},{4,20},{20... | collective-permute-start | bytes 1179656 | tf_op jit(solution)/shard_map/ppermute | solution.py:164
  16.6 14.4 %copy-start = (bf16[1,96,128,128]{3,2,1,0:T(8,128)(2,1)S(1)}, bf16[1,96,128,128]{3,2,1,0:T(8,128)(2,1)}, u32[]{:S(2)}) copy-start(bf16[1,96,128,128]{3,2,1,0:T(8,128)(2,1)} %param.8) | copy-start | bytes 9437188
  16.6 6.6 %collective-permute-start.6 = (bf16[16,3072]{1,0:T(8,128)(2,1)S(1)}, bf16[16,3072]{1,0:T(8,128)(2,1)S(1)}, u32[]{:S(2)}, u32[]{:S(2)}) collective-permute-start(bf16[16,3072]{1,0:T(8,128)(2,1)S(1)} %get-tuple-element.19.refs_3_), channel_id=1, source_target_pairs={{0,2},{2,0},{1,3},{3,1},{4,6},{6,4},{5,7},{7,5},{8,10},{10,8},{9,1... | collective-permute-start | bytes 294920 | tf_op jit(solution)/shard_map/ppermute | solution.py:129
  17.9 6.4 %collective-permute-start.5 = (bf16[32,3072]{1,0:T(8,128)(2,1)S(1)}, bf16[32,3072]{1,0:T(8,128)(2,1)S(1)}, u32[]{:S(2)}, u32[]{:S(2)}) collective-permute-start(bf16[32,3072]{1,0:T(8,128)(2,1)S(1)} %collective-permute-done.2.refs_2_), channel_id=1, source_target_pairs={{0,2},{2,0},{1,3},{3,1},{4,6},{6,4},{5,7},{7,5},{8,10},{10,8},{9,1... | collective-permute-start | bytes 589832 | tf_op jit(solution)/shard_map/ppermute | solution.py:129
  18.8 11.1 %collective-permute-start.12 = (bf16[32,3072]{1,0:T(8,128)(2,1)S(1)}, bf16[32,3072]{1,0:T(8,128)(2,1)S(1)}, u32[]{:S(2)}, u32[]{:S(2)}) collective-permute-start(bf16[32,3072]{1,0:T(8,128)(2,1)S(1)} %pad_maximum_fusion.3.refs_9_), channel_id=1, source_target_pairs={{0,1},{1,0},{2,3},{3,2},{4,5},{5,4},{6,7},{7,6},{8,9},{9,8},{10,11... | collective-permute-start | bytes 589832 | tf_op jit(solution)/shard_map/ppermute | solution.py:134
  21.9 6.5 %collective-permute-start.10 = (bf16[16,3072]{1,0:T(8,128)(2,1)S(1)}, bf16[16,3072]{1,0:T(8,128)(2,1)S(1)}, u32[]{:S(2)}, u32[]{:S(2)}) collective-permute-start(bf16[16,3072]{1,0:T(8,128)(2,1)S(1)} %get-tuple-element.13), channel_id=1, source_target_pairs={{0,2},{2,0},{1,3},{3,1},{4,6},{6,4},{5,7},{7,5},{8,10},{10,8},{9,1... | collective-permute-start | bytes 294920 | tf_op jit(solution)/shard_map/ppermute | solution.py:129
  23.2 6.1 %collective-permute-start.11 = (bf16[16,3072]{1,0:T(8,128)(2,1)S(1)}, bf16[16,3072]{1,0:T(8,128)(2,1)S(1)}, u32[]{:S(2)}, u32[]{:S(2)}) collective-permute-start(bf16[16,3072]{1,0:T(8,128)(2,1)S(1)} %slice.14), channel_id=1, source_target_pairs={{0,16},{16,0},{1,17},{17,1},{2,18},{18,2},{3,19},{19,3},{4,20},{20... | collective-permute-start | bytes 294920 | tf_op jit(solution)/shard_map/ppermute | solution.py:125
  24.3 6.7 %collective-permute-start.8 = (bf16[96,3072]{1,0:T(8,128)(2,1)S(1)}, bf16[96,3072]{1,0:T(8,128)(2,1)S(1)}, u32[]{:S(2)}, u32[]{:S(2)}) collective-permute-start(bf16[96,3072]{1,0:T(8,128)(2,1)S(1)} %pad_maximum_fusion), channel_id=1, source_target_pairs={{0,1},{1,0},{2,3},{3,2},{4,5},{5,4},{6,7},{7,6},{8,9},{9,8},{10,11... | collective-permute-start | bytes 1769480 | tf_op jit(solution)/shard_map/ppermute | solution.py:134
  28.4 2.5 %collective-permute-start.7 = (bf16[64,3072]{1,0:T(8,128)(2,1)S(1)}, bf16[64,3072]{1,0:T(8,128)(2,1)S(1)}, u32[]{:S(2)}, u32[]{:S(2)}) collective-permute-start(bf16[64,3072]{1,0:T(8,128)(2,1)S(1)} %pad_maximum_fusion.1), channel_id=1, source_target_pairs={{0,1},{1,0},{2,3},{3,2},{4,5},{5,4},{6,7},{7,6},{8,9},{9,8},{10,11... | collective-permute-start | bytes 1179656 | tf_op jit(solution)/shard_map/ppermute | solution.py:134
  29.3 1.6 %collective-permute-start.13 = (bf16[32,3072]{1,0:T(8,128)(2,1)S(1)}, bf16[32,3072]{1,0:T(8,128)(2,1)S(1)}, u32[]{:S(2)}, u32[]{:S(2)}) collective-permute-start(bf16[32,3072]{1,0:T(8,128)(2,1)S(1)} %pad_maximum_fusion.4), channel_id=1, source_target_pairs={{0,1},{1,0},{2,3},{3,2},{4,5},{5,4},{6,7},{7,6},{8,9},{9,8},{10,11... | collective-permute-start | bytes 589832 | tf_op jit(solution)/shard_map/ppermute | solution.py:134

commit v6 on v5

--- a/solution.py
+++ b/solution.py
@@ -168,8 +168,8 @@
     both1_x = over_x(both1)
     own2_x = over_x(own2)
     last = join(other3, other2)
-    other2_x = over_x(after(other2, both1))
-    other3_x = over_y(after(cut(first_x, 0, 1), both1, own2_x))
+    other2_x = over_x(after(other2, both1, first_x))
+    other3_x = over_y(after(cut(first_x, 0, 1), own2_x))
     near = join(first, both1)
     settled, (table, place) = lax.optimization_barrier((near[0], (table, place)))
     core_a = over_core((settled, near[1]))

time: 35.3 us -> 35.3 us (level)
  no operation moved by 1% of the time
where the time goes in v6:
time: 35.3 us; the launch traced here: 34.9 us
  starting transfers between devices  22.1 us (63%)
  waiting for transfers between devices  5.6 us (16%)
  Pallas kernels  3.97 us (11%)
  between operations  1.38 us (4%)
  local copies, waits for them, and re-layouts  1.09 us (3%)
  other arithmetic  0.8 us (2%)
    ppermute x4, starting transfers between devices, over_core(): moved = lax.ppermute(value, 'col', [(0, 1), (1, 0), (2, 3), (3, 2)])  8.64 us
    ppermute x4, starting transfers between devices, over_x(): moved = lax.ppermute(value, 'col', [(0, 2), (2, 0), (1, 3), (3, 1)])  4.65 us
    ppermute x3, starting transfers between devices, over_y(): return (swap_y(value), [(not own, shard, at) for own, shard, at in parts])  3.97 us
    pallas_call x1, Pallas kernels, call_blocks(): pl.pallas_call(functools.partial(block_kernel, plan, len(pieces), len(cot...  3.97 us
    ppermute x3, starting transfers between devices, over_z(): moved = lax.ppermute(value, 'row', [(i, (i + by) % 4) for i in range(4)])  3.37 us
    ppermute x3, waiting for transfers between devices, over_y(): return (swap_y(value), [(not own, shard, at) for own, shard, at in parts])  2.75 us
    ppermute x1, starting transfers between devices, two_group_plan(): cot_other = swap_y(after((cotangent, None), other3)[0])  1.46 us
    ppermute x4, waiting for transfers between devices, over_core(): moved = lax.ppermute(value, 'col', [(0, 1), (1, 0), (2, 3), (3, 2)])  1.15 us
  transfers between devices with their start and end apart: 15, of which 5 were waited for; matrix products, arithmetic and copies ran while one was open for 3% of the time, Pallas kernels for 0%

profile of v6, /device:TPU:29, one launch (start us, length us, event | category | flops | bytes accessed | tf_op | source)
XLA Modules:
  0.0 34.9 jit_solution(605484252107846719)
XLA Ops:
  0.6 1.0 %constant_dynamic-slice_fusion = bf16[16,3072]{1,0:T(8,128)(2,1)S(1)} fusion(bf16[16,12288]{1,0:T(8,128)(2,1)} %refs_0_.1, s32[]{:T(128)S(6)} %select_n.30), kind=kLoop, calls=%fused_computation.8 | loop fusion | bytes 196612 | tf_op jit(solution)/shard_map/dynamic_slice | solution.py:155
  1.6 0.2 collective-permute-start.1
  1.8 0.1 collective-permute-start
  2.5 0.1 stack.39.place
  2.6 0.7 %pad_add_fusion.table = s32[2,96]{1,0:T(2,128)S(1)} fusion(s32[1,96]{1,0:T(1,128)} %param.10, s32[1,96]{1,0:T(1,128)} %param.9), kind=kLoop, calls=%fused_computation.7 | loop fusion | flops 192 | bytes 1536 | tf_op jit(solution)/shard_map/concatenate | solution.py:198
  3.3 1.8 %collective-permute-done.1 = bf16[16,3072]{1,0:T(8,128)(2,1)S(1)} collective-permute-done((bf16[16,3072]{1,0:T(8,128)(2,1)S(1)}, bf16[16,3072]{1,0:T(8,128)(2,1)S(1)}, u32[]{:S(2)}, u32[]{:S(2)}) %collective-permute-start.1) | collective-permute-done | bytes 98336 | tf_op jit(solution)/shard_map/ppermute | solution.py:125
  5.1 0.2 collective-permute-start.3
  5.3 3.1 %collective-permute-start.2 = (bf16[32,3072]{1,0:T(8,128)(2,1)S(1)}, bf16[32,3072]{1,0:T(8,128)(2,1)S(1)}, u32[]{:S(2)}, u32[]{:S(2)}) collective-permute-start(bf16[32,3072]{1,0:T(8,128)(2,1)S(1)} %pad_maximum_fusion.2), channel_id=1, source_target_pairs={{0,4},{4,8},{8,12},{12,0},{1,5},{5,9},{9,13},{13,1},{2,6},{6,10},{... | collective-permute-start | bytes 589832 | tf_op jit(solution)/shard_map/ppermute | solution.py:140
  8.4 0.7 %collective-permute-done = bf16[16,3072]{1,0:T(8,128)(2,1)S(1)} collective-permute-done((bf16[16,3072]{1,0:T(8,128)(2,1)S(1)}, bf16[16,3072]{1,0:T(8,128)(2,1)S(1)}, u32[]{:S(2)}, u32[]{:S(2)}) %collective-permute-start) | collective-permute-done | bytes 98336 | tf_op jit(solution)/shard_map/ppermute | solution.py:140
  9.1 3.7 %collective-permute-start.9 = (bf16[16,3072]{1,0:T(8,128)(2,1)S(1)}, bf16[16,3072]{1,0:T(8,128)(2,1)S(1)}, u32[]{:S(2)}, u32[]{:S(2)}) collective-permute-start(bf16[16,3072]{1,0:T(8,128)(2,1)S(1)} %collective-permute-done), channel_id=1, source_target_pairs={{0,16},{16,0},{1,17},{17,1},{2,18},{18,2},{3,19},{19,3},{4,20},{20... | collective-permute-start | bytes 294920 | tf_op jit(solution)/shard_map/ppermute | solution.py:125
  12.8 1.3 %collective-permute-start.4 = (bf16[32,3072]{1,0:T(8,128)(2,1)S(1)}, bf16[32,3072]{1,0:T(8,128)(2,1)S(1)}, u32[]{:S(2)}, u32[]{:S(2)}) collective-permute-start(bf16[32,3072]{1,0:T(8,128)(2,1)S(1)} %constant_dynamic-update-slice_fusion.refs_1_), channel_id=1, source_target_pairs={{0,2},{2,0},{1,3},{3,1},{4,6},{6,4},{5,7},{7,5},{8,10},{10,8},{9,1... | collective-permute-start | bytes 589832 | tf_op jit(solution)/shard_map/ppermute | solution.py:129
  14.1 1.0 %collective-permute-done.9 = bf16[16,3072]{1,0:T(8,128)(2,1)S(1)} collective-permute-done((bf16[16,3072]{1,0:T(8,128)(2,1)S(1)}, bf16[16,3072]{1,0:T(8,128)(2,1)S(1)}, u32[]{:S(2)}, u32[]{:S(2)}) %collective-permute-start.9) | collective-permute-done | bytes 98336 | tf_op jit(solution)/shard_map/ppermute | solution.py:125
  15.1 1.5 %collective-permute-start.14 = (bf16[64,3072]{1,0:T(8,128)(2,1)S(1)}, bf16[64,3072]{1,0:T(8,128)(2,1)S(1)}, u32[]{:S(2)}, u32[]{:S(2)}) collective-permute-start(bf16[64,3072]{1,0:T(8,128)(2,1)S(1)} %copy-done.2), channel_id=1, source_target_pairs={{0,16},{16,0},{1,17},{17,1},{2,18},{18,2},{3,19},{19,3},{4,20},{20... | collective-permute-start | bytes 1179656 | tf_op jit(solution)/shard_map/ppermute | solution.py:164
  16.6 1.3 %collective-permute-start.6 = (bf16[16,3072]{1,0:T(8,128)(2,1)S(1)}, bf16[16,3072]{1,0:T(8,128)(2,1)S(1)}, u32[]{:S(2)}, u32[]{:S(2)}) collective-permute-start(bf16[16,3072]{1,0:T(8,128)(2,1)S(1)} %get-tuple-element.19.refs_3_), channel_id=1, source_target_pairs={{0,2},{2,0},{1,3},{3,1},{4,6},{6,4},{5,7},{7,5},{8,10},{10,8},{9,1... | collective-permute-start | bytes 294920 | tf_op jit(solution)/shard_map/ppermute | solution.py:129
  17.9 0.9 %collective-permute-start.5 = (bf16[32,3072]{1,0:T(8,128)(2,1)S(1)}, bf16[32,3072]{1,0:T(8,128)(2,1)S(1)}, u32[]{:S(2)}, u32[]{:S(2)}) collective-permute-start(bf16[32,3072]{1,0:T(8,128)(2,1)S(1)} %collective-permute-done.2.refs_2_), channel_id=1, source_target_pairs={{0,2},{2,0},{1,3},{3,1},{4,6},{6,4},{5,7},{7,5},{8,10},{10,8},{9,1... | collective-permute-start | bytes 589832 | tf_op jit(solution)/shard_map/ppermute | solution.py:129
  18.8 3.2 %collective-permute-start.12 = (bf16[32,3072]{1,0:T(8,128)(2,1)S(1)}, bf16[32,3072]{1,0:T(8,128)(2,1)S(1)}, u32[]{:S(2)}, u32[]{:S(2)}) collective-permute-start(bf16[32,3072]{1,0:T(8,128)(2,1)S(1)} %pad_maximum_fusion.3.refs_9_), channel_id=1, source_target_pairs={{0,1},{1,0},{2,3},{3,2},{4,5},{5,4},{6,7},{7,6},{8,9},{9,8},{10,11... | collective-permute-start | bytes 589832 | tf_op jit(solution)/shard_map/ppermute | solution.py:134
  21.9 1.2 %collective-permute-start.10 = (bf16[16,3072]{1,0:T(8,128)(2,1)S(1)}, bf16[16,3072]{1,0:T(8,128)(2,1)S(1)}, u32[]{:S(2)}, u32[]{:S(2)}) collective-permute-start(bf16[16,3072]{1,0:T(8,128)(2,1)S(1)} %get-tuple-element.13), channel_id=1, source_target_pairs={{0,2},{2,0},{1,3},{3,1},{4,6},{6,4},{5,7},{7,5},{8,10},{10,8},{9,1... | collective-permute-start | bytes 294920 | tf_op jit(solution)/shard_map/ppermute | solution.py:129
  23.2 0.1 collective-permute-start.11
  23.3 1.0 %collective-permute-done.5.refs_5_ = bf16[32,3072]{1,0:T(8,128)(2,1)S(1)} collective-permute-done((bf16[32,3072]{1,0:T(8,128)(2,1)S(1)}, bf16[32,3072]{1,0:T(8,128)(2,1)S(1)}, u32[]{:S(2)}, u32[]{:S(2)}) %collective-permute-start.5) | collective-permute-done | bytes 196640 | tf_op jit(solution)/shard_map/ppermute | solution.py:129
  24.3 4.1 %collective-permute-start.8 = (bf16[96,3072]{1,0:T(8,128)(2,1)S(1)}, bf16[96,3072]{1,0:T(8,128)(2,1)S(1)}, u32[]{:S(2)}, u32[]{:S(2)}) collective-permute-start(bf16[96,3072]{1,0:T(8,128)(2,1)S(1)} %pad_maximum_fusion), channel_id=1, source_target_pairs={{0,1},{1,0},{2,3},{3,2},{4,5},{5,4},{6,7},{7,6},{8,9},{9,8},{10,11... | collective-permute-start | bytes 1769480 | tf_op jit(solution)/shard_map/ppermute | solution.py:134
  28.4 0.9 %collective-permute-start.7 = (bf16[64,3072]{1,0:T(8,128)(2,1)S(1)}, bf16[64,3072]{1,0:T(8,128)(2,1)S(1)}, u32[]{:S(2)}, u32[]{:S(2)}) collective-permute-start(bf16[64,3072]{1,0:T(8,128)(2,1)S(1)} %pad_maximum_fusion.1), channel_id=1, source_target_pairs={{0,1},{1,0},{2,3},{3,2},{4,5},{5,4},{6,7},{7,6},{8,9},{9,8},{10,11... | collective-permute-start | bytes 1179656 | tf_op jit(solution)/shard_map/ppermute | solution.py:134
  29.3 0.5 %collective-permute-start.13 = (bf16[32,3072]{1,0:T(8,128)(2,1)S(1)}, bf16[32,3072]{1,0:T(8,128)(2,1)S(1)}, u32[]{:S(2)}, u32[]{:S(2)}) collective-permute-start(bf16[32,3072]{1,0:T(8,128)(2,1)S(1)} %pad_maximum_fusion.4), channel_id=1, source_target_pairs={{0,1},{1,0},{2,3},{3,2},{4,5},{5,4},{6,7},{7,6},{8,9},{9,8},{10,11... | collective-permute-start | bytes 589832 | tf_op jit(solution)/shard_map/ppermute | solution.py:134
  29.8 1.1 %collective-permute-done.13.refs_13_ = bf16[32,3072]{1,0:T(8,128)(2,1)S(1)} collective-permute-done((bf16[32,3072]{1,0:T(8,128)(2,1)S(1)}, bf16[32,3072]{1,0:T(8,128)(2,1)S(1)}, u32[]{:S(2)}, u32[]{:S(2)}) %collective-permute-start.13) | collective-permute-done | bytes 196640 | tf_op jit(solution)/shard_map/ppermute | solution.py:134
  31.0 4.0 %blocks.1 = (bf16[64,3072]{1,0:T(8,128)(2,1)}, bf16[48,128,128]{2,1,0:T(8,128)(2,1)}) custom-call(s32[2,96]{1,0:T(2,128)S(1)} %pad_add_fusion.table, s32[10]{0:T(128)S(1)} %stack.39.place, bf16[16,12288]{1,0:T(8,128)(2,1)S(1)} %copy-done.1, bf16[32,3072]{1,0:T(8,128)(2,1)S(1)} %constant_dynamic-update-slice_fusion.refs_1_, ...), custom_call_target="tpu_custom_call" | custom-call | flops 402653184 | bytes 9043968 | tf_op jit(solution)/shard_map/blocks/pallas_call | solution.py:90
  (25 shorter events, 0.2 us)
Async XLA Ops:
  0.6 14.5 %copy-start.2 = (bf16[64,3072]{1,0:T(8,128)(2,1)S(1)}, bf16[64,3072]{1,0:T(8,128)(2,1)}, u32[]{:S(2)}) copy-start(bf16[64,3072]{1,0:T(8,128)(2,1)} %refs_14_.1) | copy-start | bytes 1179652
  1.6 3.5 %collective-permute-start.1 = (bf16[16,3072]{1,0:T(8,128)(2,1)S(1)}, bf16[16,3072]{1,0:T(8,128)(2,1)S(1)}, u32[]{:S(2)}, u32[]{:S(2)}) collective-permute-start(bf16[16,3072]{1,0:T(8,128)(2,1)S(1)} %constant_dynamic-slice_fusion), channel_id=1, source_target_pairs={{0,16},{16,0},{1,17},{17,1},{2,18},{18,2},{3,19},{19,3},{4,20},{20... | collective-permute-start | bytes 294920 | tf_op jit(solution)/shard_map/ppermute | solution.py:125
  1.8 7.3 %collective-permute-start = (bf16[16,3072]{1,0:T(8,128)(2,1)S(1)}, bf16[16,3072]{1,0:T(8,128)(2,1)S(1)}, u32[]{:S(2)}, u32[]{:S(2)}) collective-permute-start(bf16[16,3072]{1,0:T(8,128)(2,1)S(1)} %constant_dynamic-slice_fusion), channel_id=1, source_target_pairs={{0,8},{4,12},{8,0},{12,4},{1,9},{5,13},{9,1},{13,5},{2,10},{6,14},... | collective-permute-start | bytes 294920 | tf_op jit(solution)/shard_map/ppermute | solution.py:140
  5.1 11.5 %collective-permute-start.3 = (bf16[32,3072]{1,0:T(8,128)(2,1)S(1)}, bf16[32,3072]{1,0:T(8,128)(2,1)S(1)}, u32[]{:S(2)}, u32[]{:S(2)}) collective-permute-start(bf16[32,3072]{1,0:T(8,128)(2,1)S(1)} %pad_maximum_fusion.2), channel_id=1, source_target_pairs={{0,12},{4,0},{8,4},{12,8},{1,13},{5,1},{9,5},{13,9},{2,14},{6,2},{... | collective-permute-start | bytes 589832 | tf_op jit(solution)/shard_map/ppermute | solution.py:140
  5.3 12.6 %collective-permute-start.2 = (bf16[32,3072]{1,0:T(8,128)(2,1)S(1)}, bf16[32,3072]{1,0:T(8,128)(2,1)S(1)}, u32[]{:S(2)}, u32[]{:S(2)}) collective-permute-start(bf16[32,3072]{1,0:T(8,128)(2,1)S(1)} %pad_maximum_fusion.2), channel_id=1, source_target_pairs={{0,4},{4,8},{8,12},{12,0},{1,5},{5,9},{9,13},{13,1},{2,6},{6,10},{... | collective-permute-start | bytes 589832 | tf_op jit(solution)/shard_map/ppermute | solution.py:140
  9.1 6.0 %collective-permute-start.9 = (bf16[16,3072]{1,0:T(8,128)(2,1)S(1)}, bf16[16,3072]{1,0:T(8,128)(2,1)S(1)}, u32[]{:S(2)}, u32[]{:S(2)}) collective-permute-start(bf16[16,3072]{1,0:T(8,128)(2,1)S(1)} %collective-permute-done), channel_id=1, source_target_pairs={{0,16},{16,0},{1,17},{17,1},{2,18},{18,2},{3,19},{19,3},{4,20},{20... | collective-permute-start | bytes 294920 | tf_op jit(solution)/shard_map/ppermute | solution.py:125
  12.8 18.2 %copy-start.1 = (bf16[16,12288]{1,0:T(8,128)(2,1)S(1)}, bf16[16,12288]{1,0:T(8,128)(2,1)}, u32[]{:S(2)}) copy-start(bf16[16,12288]{1,0:T(8,128)(2,1)} %refs_0_.1) | copy-start | bytes 1179652
  12.8 9.1 %collective-permute-start.4 = (bf16[32,3072]{1,0:T(8,128)(2,1)S(1)}, bf16[32,3072]{1,0:T(8,128)(2,1)S(1)}, u32[]{:S(2)}, u32[]{:S(2)}) collective-permute-start(bf16[32,3072]{1,0:T(8,128)(2,1)S(1)} %constant_dynamic-update-slice_fusion.refs_1_), channel_id=1, source_target_pairs={{0,2},{2,0},{1,3},{3,1},{4,6},{6,4},{5,7},{7,5},{8,10},{10,8},{9,1... | collective-permute-start | bytes 589832 | tf_op jit(solution)/shard_map/ppermute | solution.py:129
  15.1 14.7 %collective-permute-start.14 = (bf16[64,3072]{1,0:T(8,128)(2,1)S(1)}, bf16[64,3072]{1,0:T(8,128)(2,1)S(1)}, u32[]{:S(2)}, u32[]{:S(2)}) collective-permute-start(bf16[64,3072]{1,0:T(8,128)(2,1)S(1)} %copy-done.2), channel_id=1, source_target_pairs={{0,16},{16,0},{1,17},{17,1},{2,18},{18,2},{3,19},{19,3},{4,20},{20... | collective-permute-start | bytes 1179656 | tf_op jit(solution)/shard_map/ppermute | solution.py:164
  16.6 14.4 %copy-start = (bf16[1,96,128,128]{3,2,1,0:T(8,128)(2,1)S(1)}, bf16[1,96,128,128]{3,2,1,0:T(8,128)(2,1)}, u32[]{:S(2)}) copy-start(bf16[1,96,128,128]{3,2,1,0:T(8,128)(2,1)} %param.8) | copy-start | bytes 9437188
  16.6 6.6 %collective-permute-start.6 = (bf16[16,3072]{1,0:T(8,128)(2,1)S(1)}, bf16[16,3072]{1,0:T(8,128)(2,1)S(1)}, u32[]{:S(2)}, u32[]{:S(2)}) collective-permute-start(bf16[16,3072]{1,0:T(8,128)(2,1)S(1)} %get-tuple-element.19.refs_3_), channel_id=1, source_target_pairs={{0,2},{2,0},{1,3},{3,1},{4,6},{6,4},{5,7},{7,5},{8,10},{10,8},{9,1... | collective-permute-start | bytes 294920 | tf_op jit(solution)/shard_map/ppermute | solution.py:129
  17.9 6.4 %collective-permute-start.5 = (bf16[32,3072]{1,0:T(8,128)(2,1)S(1)}, bf16[32,3072]{1,0:T(8,128)(2,1)S(1)}, u32[]{:S(2)}, u32[]{:S(2)}) collective-permute-start(bf16[32,3072]{1,0:T(8,128)(2,1)S(1)} %collective-permute-done.2.refs_2_), channel_id=1, source_target_pairs={{0,2},{2,0},{1,3},{3,1},{4,6},{6,4},{5,7},{7,5},{8,10},{10,8},{9,1... | collective-permute-start | bytes 589832 | tf_op jit(solution)/shard_map/ppermute | solution.py:129
  18.8 11.1 %collective-permute-start.12 = (bf16[32,3072]{1,0:T(8,128)(2,1)S(1)}, bf16[32,3072]{1,0:T(8,128)(2,1)S(1)}, u32[]{:S(2)}, u32[]{:S(2)}) collective-permute-start(bf16[32,3072]{1,0:T(8,128)(2,1)S(1)} %pad_maximum_fusion.3.refs_9_), channel_id=1, source_target_pairs={{0,1},{1,0},{2,3},{3,2},{4,5},{5,4},{6,7},{7,6},{8,9},{9,8},{10,11... | collective-permute-start | bytes 589832 | tf_op jit(solution)/shard_map/ppermute | solution.py:134
  21.9 6.5 %collective-permute-start.10 = (bf16[16,3072]{1,0:T(8,128)(2,1)S(1)}, bf16[16,3072]{1,0:T(8,128)(2,1)S(1)}, u32[]{:S(2)}, u32[]{:S(2)}) collective-permute-start(bf16[16,3072]{1,0:T(8,128)(2,1)S(1)} %get-tuple-element.13), channel_id=1, source_target_pairs={{0,2},{2,0},{1,3},{3,1},{4,6},{6,4},{5,7},{7,5},{8,10},{10,8},{9,1... | collective-permute-start | bytes 294920 | tf_op jit(solution)/shard_map/ppermute | solution.py:129
  23.2 6.1 %collective-permute-start.11 = (bf16[16,3072]{1,0:T(8,128)(2,1)S(1)}, bf16[16,3072]{1,0:T(8,128)(2,1)S(1)}, u32[]{:S(2)}, u32[]{:S(2)}) collective-permute-start(bf16[16,3072]{1,0:T(8,128)(2,1)S(1)} %slice.14), channel_id=1, source_target_pairs={{0,16},{16,0},{1,17},{17,1},{2,18},{18,2},{3,19},{19,3},{4,20},{20... | collective-permute-start | bytes 294920 | tf_op jit(solution)/shard_map/ppermute | solution.py:125
  24.3 6.7 %collective-permute-start.8 = (bf16[96,3072]{1,0:T(8,128)(2,1)S(1)}, bf16[96,3072]{1,0:T(8,128)(2,1)S(1)}, u32[]{:S(2)}, u32[]{:S(2)}) collective-permute-start(bf16[96,3072]{1,0:T(8,128)(2,1)S(1)} %pad_maximum_fusion), channel_id=1, source_target_pairs={{0,1},{1,0},{2,3},{3,2},{4,5},{5,4},{6,7},{7,6},{8,9},{9,8},{10,11... | collective-permute-start | bytes 1769480 | tf_op jit(solution)/shard_map/ppermute | solution.py:134
  28.4 2.5 %collective-permute-start.7 = (bf16[64,3072]{1,0:T(8,128)(2,1)S(1)}, bf16[64,3072]{1,0:T(8,128)(2,1)S(1)}, u32[]{:S(2)}, u32[]{:S(2)}) collective-permute-start(bf16[64,3072]{1,0:T(8,128)(2,1)S(1)} %pad_maximum_fusion.1), channel_id=1, source_target_pairs={{0,1},{1,0},{2,3},{3,2},{4,5},{5,4},{6,7},{7,6},{8,9},{9,8},{10,11... | collective-permute-start | bytes 1179656 | tf_op jit(solution)/shard_map/ppermute | solution.py:134
  29.3 1.6 %collective-permute-start.13 = (bf16[32,3072]{1,0:T(8,128)(2,1)S(1)}, bf16[32,3072]{1,0:T(8,128)(2,1)S(1)}, u32[]{:S(2)}, u32[]{:S(2)}) collective-permute-start(bf16[32,3072]{1,0:T(8,128)(2,1)S(1)} %pad_maximum_fusion.4), channel_id=1, source_target_pairs={{0,1},{1,0},{2,3},{3,2},{4,5},{5,4},{6,7},{7,6},{8,9},{9,8},{10,11... | collective-permute-start | bytes 589832 | tf_op jit(solution)/shard_map/ppermute | solution.py:134
